TPU v7x, 32 devices: a whole 2x2x4 slice. The times are simulated.
32 devices in a mesh: ctx: 8 (over y, x, core), fsdp: 4 (over z).
Axes of the slice: x: 2, y: 2, z: 4, core: 2. Of those that a mesh axis runs over, the one named last changes fastest.
Arguments:
- tokens: bfloat16 [4, 1152, 768], P('fsdp', 'ctx'), may hold values from -6 to 6
- segment_ids: int32 [4, 1152], P('fsdp', 'ctx'), may hold values from 0 to 1151, as said below
- valid_rows: int32 [4, 1152], P('fsdp', 'ctx'), may hold values from 0 to 1, as said below
- teacher: bfloat16 [4, 1152, 768], P('fsdp', 'ctx'), may hold values from -16 to 16
- cotangent: bfloat16 [4, 1152, 768], P('fsdp', 'ctx'), may hold values from -6 to 6
- first_gain: bfloat16 [768], P('fsdp'), may hold values from 0.5 to 1.5
- first_shift: bfloat16 [768], P('fsdp'), may hold values from -3 to 3
- query_weight: bfloat16 [768, 768], P('fsdp'), may hold values from -0.3125 to 0.3125
- query_bias: bfloat16 [768], P('fsdp'), may hold values from -3 to 3
- key_weight: bfloat16 [768, 768], P('fsdp'), may hold values from -0.3125 to 0.3125
- value_weight: bfloat16 [768, 768], P('fsdp'), may hold values from -0.21875 to 0.21875
- value_bias: bfloat16 [768], P('fsdp'), may hold values from -3 to 3
- output_weight: bfloat16 [768, 768], P('fsdp'), may hold values from -0.875 to 0.875
- output_bias: bfloat16 [768], P('fsdp'), may hold values from -3 to 3
- second_gain: bfloat16 [768], P('fsdp'), may hold values from 0.5 to 1.5
- second_shift: bfloat16 [768], P('fsdp'), may hold values from -3 to 3
- up_weight: bfloat16 [768, 3072], P('fsdp'), may hold values from -0.21875 to 0.21875
- up_bias: bfloat16 [3072], P('fsdp'), may hold values from -3 to 3
- down_weight: bfloat16 [3072, 768], P('fsdp'), may hold values from -0.109375 to 0.109375
- down_bias: bfloat16 [768], P('fsdp'), may hold values from -3 to 3
Outputs:
- layer_output: bfloat16 [4, 1152, 768], P('fsdp', 'ctx')
- loss_value: float32 [], replicated
- grad_tokens: bfloat16 [4, 1152, 768], P('fsdp', 'ctx')
- grad_first_gain: float32 [768], P('fsdp')
- grad_first_shift: float32 [768], P('fsdp')
- grad_query_weight: float32 [768, 768], P('fsdp')
- grad_query_bias: float32 [768], P('fsdp')
- grad_key_weight: float32 [768, 768], P('fsdp')
- grad_value_weight: float32 [768, 768], P('fsdp')
- grad_value_bias: float32 [768], P('fsdp')
- grad_output_weight: float32 [768, 768], P('fsdp')
- grad_output_bias: float32 [768], P('fsdp')
- grad_second_gain: float32 [768], P('fsdp')
- grad_second_shift: float32 [768], P('fsdp')
- grad_up_weight: float32 [768, 3072], P('fsdp')
- grad_up_bias: float32 [3072], P('fsdp')
- grad_down_weight: float32 [3072, 768], P('fsdp')
- grad_down_bias: float32 [768], P('fsdp')
Inputs may be any that keep to these rules, and one draw needn't show every extreme that they name: `segment_ids`: within a sequence the ids never fall, and each is the position within the sequence of its document's first row; in every sequence one document has rows on every index of ctx. `valid_rows`: 1 where a row holds a token, 0 where it is padding.
All inputs are finite; a program needn't handle non-finite values.
Results may differ from a plain program's by a relative error of at most 0.023.
Values may be sent and summed in bfloat16 or wider, within the bound.
No kernel may reach another device: no remote copies, remote signals or barrier semaphores. Data moves between devices by JAX's collectives and lax.ppermute only.
A program may use at most 256 MiB of HBM per device.

v0:
```python
import jax
import jax.numpy as jnp
from jax import lax
from jax.sharding import PartitionSpec as P

HEADS = 12
HEAD_DIM = 64


EPSILON = 1e-06
MASKED = -1e30


def norm_rows(values, gain, shift):
    centre = jnp.mean(values, axis=-1, keepdims=True)
    centred = values - centre
    spread = jnp.mean(centred * centred, axis=-1, keepdims=True)
    return centred * lax.rsqrt(spread + EPSILON) * gain + shift


def tanh_gelu(values):
    return jax.nn.gelu(values, approximate=True)


def key_allowed(query_segment, query_place, key_codes, key_place):
    same_doc = query_segment[:, None] == (key_codes // 2)[None, :]
    usable = (key_codes % 2 == 1)[None, :] | (query_place[:, None] == key_place[None, :])
    return (same_doc & usable)[None, :, :]


def split_heads(values):
    return values.reshape(values.shape[0], HEADS, HEAD_DIM)


def head_scores(query_heads, key_heads, scale):
    return (
        jnp.einsum("qhd,khd->hqk", query_heads, key_heads, preferred_element_type=jnp.float32)
        * scale
    )


def row_sum(values):
    return jnp.sum(values, axis=0, dtype=jnp.float32)


def left_product(left, right):
    return jnp.einsum("rd,rf->df", left, right, preferred_element_type=jnp.float32)


def right_product(left, right):
    return jnp.einsum("rf,df->rd", left, right, preferred_element_type=jnp.float32)


def shards(
    tokens,
    segment_ids,
    valid_rows,
    teacher,
    cotangent,
    first_gain,
    first_shift,
    query_weight,
    query_bias,
    key_weight,
    value_weight,
    value_bias,
    output_weight,
    output_bias,
    second_gain,
    second_shift,
    up_weight,
    up_bias,
    down_weight,
    down_bias,
):
    tok_rows = tokens.shape[1]
    feature_width = tokens.shape[2]
    shard_count = lax.axis_size("ctx")
    key_block = 4 * tok_rows
    block_count = shard_count // 4
    scale = HEAD_DIM ** (-0.5)
    gain_one, shift_one, w_query, b_query, w_key, w_value, b_value, w_output, b_output = (
        lax.all_gather(first_gain, "fsdp", axis=0, tiled=True),
        lax.all_gather(first_shift, "fsdp", axis=0, tiled=True),
        lax.all_gather(query_weight, "fsdp", axis=0, tiled=True),
        lax.all_gather(query_bias, "fsdp", axis=0, tiled=True),
        lax.all_gather(key_weight, "fsdp", axis=0, tiled=True),
        lax.all_gather(value_weight, "fsdp", axis=0, tiled=True),
        lax.all_gather(value_bias, "fsdp", axis=0, tiled=True),
        lax.all_gather(output_weight, "fsdp", axis=0, tiled=True),
        lax.all_gather(output_bias, "fsdp", axis=0, tiled=True),
    )
    gain_two, shift_two, w_up, b_up, w_down, b_down = (
        lax.all_gather(second_gain, "fsdp", axis=0, tiled=True),
        lax.all_gather(second_shift, "fsdp", axis=0, tiled=True),
        lax.all_gather(up_weight, "fsdp", axis=0, tiled=True),
        lax.all_gather(up_bias, "fsdp", axis=0, tiled=True),
        lax.all_gather(down_weight, "fsdp", axis=0, tiled=True),
        lax.all_gather(down_bias, "fsdp", axis=0, tiled=True),
    )
    local_segment = segment_ids[0]
    local_valid = valid_rows[0]
    local_codes = local_segment * 2 + local_valid
    all_codes = lax.all_gather(local_codes, "ctx", axis=0, tiled=True)
    query_place = lax.axis_index("ctx") * tok_rows + jnp.arange(tok_rows, dtype=jnp.int32)
    inputs = tokens[0].astype(jnp.float32)
    gain_first = gain_one.astype(jnp.float32)
    shift_first = shift_one.astype(jnp.float32)
    gain_second = gain_two.astype(jnp.float32)
    shift_second = shift_two.astype(jnp.float32)
    h_one = norm_rows(inputs, gain_first, shift_first)
    h_one_low = h_one.astype(jnp.bfloat16)
    query_low = (
        jnp.dot(h_one_low, w_query, preferred_element_type=jnp.float32)
        + b_query.astype(jnp.float32)
    ).astype(jnp.bfloat16)
    key_low = jnp.dot(h_one_low, w_key, preferred_element_type=jnp.float32).astype(jnp.bfloat16)
    value_low = (
        jnp.dot(h_one_low, w_value, preferred_element_type=jnp.float32)
        + b_value.astype(jnp.float32)
    ).astype(jnp.bfloat16)
    key_all, value_all = (
        lax.all_gather(key_low, "ctx", axis=0, tiled=True),
        lax.all_gather(value_low, "ctx", axis=0, tiled=True),
    )
    query_heads = split_heads(query_low)

    def block_rows(source, block_index):
        return split_heads(lax.dynamic_slice_in_dim(source, block_index * key_block, key_block, 0))

    def block_allowed(block_index):
        start = block_index * key_block
        codes = lax.dynamic_slice_in_dim(all_codes, start, key_block, 0)
        return key_allowed(
            local_segment, query_place, codes, start + jnp.arange(key_block, dtype=jnp.int32)
        )

    def stats_step(block_index, state_pair):
        running_max, running_sum = state_pair
        allowed = block_allowed(block_index)
        scores = jnp.where(
            allowed, head_scores(query_heads, block_rows(key_all, block_index), scale), MASKED
        )
        new_max = jnp.maximum(running_max, jnp.max(scores, axis=2))
        weights = jnp.where(allowed, jnp.exp(scores - new_max[:, :, None]), 0.0)
        return (new_max, running_sum * jnp.exp(running_max - new_max) + jnp.sum(weights, axis=2))

    start_max = jnp.full((HEADS, tok_rows), MASKED, jnp.float32)
    start_sum = jnp.zeros((HEADS, tok_rows), jnp.float32)
    running_max, running_sum = lax.fori_loop(0, block_count, stats_step, (start_max, start_sum))
    log_total = running_max + jnp.log(running_sum)

    def mix_step(block_index, mixed_sum):
        allowed = block_allowed(block_index)
        scores = head_scores(query_heads, block_rows(key_all, block_index), scale)
        probs = jnp.where(allowed, jnp.exp(scores - log_total[:, :, None]), 0.0).astype(
            jnp.bfloat16
        )
        return mixed_sum + jnp.einsum(
            "hqk,khd->qhd",
            probs,
            block_rows(value_all, block_index),
            preferred_element_type=jnp.float32,
        )

    mixed_heads = lax.fori_loop(
        0, block_count, mix_step, jnp.zeros((tok_rows, HEADS, HEAD_DIM), jnp.float32)
    )
    mixed = mixed_heads.reshape(tok_rows, feature_width)
    mixed_low = mixed.astype(jnp.bfloat16)
    second = (
        inputs
        + jnp.dot(mixed_low, w_output, preferred_element_type=jnp.float32)
        + b_output.astype(jnp.float32)
    )
    h_two = norm_rows(second, gain_second, shift_second)
    h_two_low = h_two.astype(jnp.bfloat16)
    up_value = jnp.dot(h_two_low, w_up, preferred_element_type=jnp.float32) + b_up.astype(
        jnp.float32
    )
    act_low = tanh_gelu(up_value).astype(jnp.bfloat16)
    result = (
        second
        + jnp.dot(act_low, w_down, preferred_element_type=jnp.float32)
        + b_down.astype(jnp.float32)
    )
    layer_output = result.astype(jnp.bfloat16)[None]
    valid_float = local_valid.astype(jnp.float32)
    mismatch = result - teacher[0].astype(jnp.float32)
    error_sum, valid_count = lax.psum(
        (jnp.sum(valid_float[:, None] * mismatch * mismatch), jnp.sum(valid_float)), ("ctx", "fsdp")
    )
    loss_value = error_sum / (feature_width * valid_count)
    d_result = (
        cotangent[0].astype(jnp.float32)
        + 2.0 / (feature_width * valid_count) * valid_float[:, None] * mismatch
    )
    d_down = d_result.astype(jnp.bfloat16)
    grad_down_bias = row_sum(d_down)
    grad_down_weight = left_product(act_low, d_down)
    d_act = right_product(d_down, w_down)
    gelu_value, gelu_pull = jax.vjp(tanh_gelu, up_value)
    d_up = gelu_pull(d_act)[0].astype(jnp.bfloat16)
    grad_up_bias = row_sum(d_up)
    grad_up_weight = left_product(h_two_low, d_up)
    d_h_two = right_product(d_up, w_up)
    norm_two_value, norm_two_pull = jax.vjp(norm_rows, second, gain_second, shift_second)
    d_second_norm, grad_second_gain, grad_second_shift = norm_two_pull(d_h_two)
    d_second = d_result + d_second_norm
    d_attn = d_second.astype(jnp.bfloat16)
    grad_output_bias = row_sum(d_attn)
    grad_output_weight = left_product(mixed_low, d_attn)
    d_mixed = right_product(d_attn, w_output).astype(jnp.bfloat16)
    d_heads = split_heads(d_mixed)
    delta = jnp.einsum("qhd,qhd->hq", d_heads.astype(jnp.float32), mixed_heads)
    key_back, value_back = (key_all, value_all)

    def score_grads(block_index):
        allowed = block_allowed(block_index)
        key_piece = block_rows(key_back, block_index)
        value_piece = block_rows(value_back, block_index)
        scores = head_scores(query_heads, key_piece, scale)
        probs = jnp.where(allowed, jnp.exp(scores - log_total[:, :, None]), 0.0)
        d_probs = jnp.einsum(
            "qhd,khd->hqk", d_heads, value_piece, preferred_element_type=jnp.float32
        )
        d_scores = (probs * (d_probs - delta[:, :, None])).astype(jnp.bfloat16)
        return (key_piece, probs, d_scores)

    zero_query = jnp.zeros((tok_rows, HEADS, HEAD_DIM), jnp.float32)

    def reduce_step(block_index, state_triple):
        d_query_sum, d_key_rows, d_value_rows = state_triple
        key_piece, probs, d_scores = score_grads(block_index)
        d_query_sum = d_query_sum + jnp.einsum(
            "hqk,khd->qhd", d_scores, key_piece, preferred_element_type=jnp.float32
        )
        d_key_piece = jnp.einsum(
            "hqk,qhd->khd", d_scores, query_heads, preferred_element_type=jnp.float32
        ).reshape(key_block, feature_width)
        d_value_piece = jnp.einsum(
            "hqk,qhd->khd", probs.astype(jnp.bfloat16), d_heads, preferred_element_type=jnp.float32
        ).reshape(key_block, feature_width)
        d_key_rows = lax.dynamic_update_slice_in_dim(
            d_key_rows, d_key_piece, block_index * key_block, 0
        )
        d_value_rows = lax.dynamic_update_slice_in_dim(
            d_value_rows, d_value_piece, block_index * key_block, 0
        )
        return (d_query_sum, d_key_rows, d_value_rows)

    zero_rows = jnp.zeros((key_block * block_count, feature_width), jnp.float32)
    d_query_sum, d_key_rows, d_value_rows = lax.fori_loop(
        0, block_count, reduce_step, (zero_query, zero_rows, zero_rows)
    )
    d_key_local, d_value_local = (
        lax.psum_scatter(d_key_rows, "ctx", scatter_dimension=0, tiled=True),
        lax.psum_scatter(d_value_rows, "ctx", scatter_dimension=0, tiled=True),
    )
    d_query = (d_query_sum.reshape(tok_rows, feature_width) * scale).astype(jnp.bfloat16)
    d_key = (d_key_local * scale).astype(jnp.bfloat16)
    d_value = d_value_local.astype(jnp.bfloat16)
    grad_query_bias = row_sum(d_query)
    grad_query_weight = left_product(h_one_low, d_query)
    grad_key_weight = left_product(h_one_low, d_key)
    grad_value_bias = row_sum(d_value)
    grad_value_weight = left_product(h_one_low, d_value)
    d_h_one = (
        right_product(d_query, w_query)
        + right_product(d_key, w_key)
        + right_product(d_value, w_value)
    )
    norm_one_value, norm_one_pull = jax.vjp(norm_rows, inputs, gain_first, shift_first)
    d_inputs_norm, grad_first_gain, grad_first_shift = norm_one_pull(d_h_one)
    grad_tokens = (d_second + d_inputs_norm).astype(jnp.bfloat16)[None]
    shares = (
        lax.psum_scatter(
            grad_first_gain.astype(jnp.bfloat16), "fsdp", scatter_dimension=0, tiled=True
        ).astype(jnp.float32),
        lax.psum_scatter(
            grad_first_shift.astype(jnp.bfloat16), "fsdp", scatter_dimension=0, tiled=True
        ).astype(jnp.float32),
        lax.psum_scatter(
            grad_query_weight.astype(jnp.bfloat16), "fsdp", scatter_dimension=0, tiled=True
        ).astype(jnp.float32),
        lax.psum_scatter(
            grad_query_bias.astype(jnp.bfloat16), "fsdp", scatter_dimension=0, tiled=True
        ).astype(jnp.float32),
        lax.psum_scatter(
            grad_key_weight.astype(jnp.bfloat16), "fsdp", scatter_dimension=0, tiled=True
        ).astype(jnp.float32),
        lax.psum_scatter(
            grad_value_weight.astype(jnp.bfloat16), "fsdp", scatter_dimension=0, tiled=True
        ).astype(jnp.float32),
        lax.psum_scatter(
            grad_value_bias.astype(jnp.bfloat16), "fsdp", scatter_dimension=0, tiled=True
        ).astype(jnp.float32),
        lax.psum_scatter(
            grad_output_weight.astype(jnp.bfloat16), "fsdp", scatter_dimension=0, tiled=True
        ).astype(jnp.float32),
        lax.psum_scatter(
            grad_output_bias.astype(jnp.bfloat16), "fsdp", scatter_dimension=0, tiled=True
        ).astype(jnp.float32),
        lax.psum_scatter(
            grad_second_gain.astype(jnp.bfloat16), "fsdp", scatter_dimension=0, tiled=True
        ).astype(jnp.float32),
        lax.psum_scatter(
            grad_second_shift.astype(jnp.bfloat16), "fsdp", scatter_dimension=0, tiled=True
        ).astype(jnp.float32),
        lax.psum_scatter(
            grad_up_weight.astype(jnp.bfloat16), "fsdp", scatter_dimension=0, tiled=True
        ).astype(jnp.float32),
        lax.psum_scatter(
            grad_up_bias.astype(jnp.bfloat16), "fsdp", scatter_dimension=0, tiled=True
        ).astype(jnp.float32),
        lax.psum_scatter(
            grad_down_weight.astype(jnp.bfloat16), "fsdp", scatter_dimension=0, tiled=True
        ).astype(jnp.float32),
        lax.psum_scatter(
            grad_down_bias.astype(jnp.bfloat16), "fsdp", scatter_dimension=0, tiled=True
        ).astype(jnp.float32),
    )
    totals = lax.psum(
        (
            shares[0],
            shares[1],
            shares[2],
            shares[3],
            shares[4],
            shares[5],
            shares[6],
            shares[7],
            shares[8],
            shares[9],
            shares[10],
            shares[11],
            shares[12],
            shares[13],
            shares[14],
        ),
        "ctx",
    )
    return (
        layer_output,
        loss_value,
        grad_tokens,
        totals[0],
        totals[1],
        totals[2],
        totals[3],
        totals[4],
        totals[5],
        totals[6],
        totals[7],
        totals[8],
        totals[9],
        totals[10],
        totals[11],
        totals[12],
        totals[13],
        totals[14],
    )


def solution(mesh):
    placed = (
        P("fsdp", "ctx", None),
        P("fsdp", "ctx"),
        P("fsdp", "ctx"),
        P("fsdp", "ctx", None),
        P("fsdp", "ctx", None),
        P("fsdp"),
        P("fsdp"),
        P("fsdp", None),
        P("fsdp"),
        P("fsdp", None),
        P("fsdp", None),
        P("fsdp"),
        P("fsdp", None),
        P("fsdp"),
        P("fsdp"),
        P("fsdp"),
        P("fsdp", None),
        P("fsdp"),
        P("fsdp", None),
        P("fsdp"),
    )
    return jax.shard_map(
        shards,
        mesh=mesh,
        in_specs=placed,
        out_specs=(
            P("fsdp", "ctx", None),
            P(),
            P("fsdp", "ctx", None),
            P("fsdp"),
            P("fsdp"),
            P("fsdp", None),
            P("fsdp"),
            P("fsdp", None),
            P("fsdp", None),
            P("fsdp"),
            P("fsdp", None),
            P("fsdp"),
            P("fsdp"),
            P("fsdp"),
            P("fsdp", None),
            P("fsdp"),
            P("fsdp", None),
            P("fsdp"),
        ),
        check_vma=False,
    )
```

profile of v0, /device:TPU:0, one launch (start us, length us, event | category | flops | bytes accessed | tf_op | source)
XLA Modules:
  0.0 1037.2 jit_solution(15729542971114790504)
XLA Ops:
  18.2 21.0 %all-reduce.21 = (bf16[768]{0:T(1024)(128)(2,1)S(1)}, bf16[768]{0:T(1024)(128)(2,1)S(1)}, bf16[768]{0:T(1024)(128)(2,1)S(1)}, bf16[768]{0:T(1024)(128)(2,1)S(1)}...) all-reduce(bf16[768]{0:T(1024)(128)(2,1)S(1)} %dynamic-update-slice, ...), channel_id=1, replica_groups=mesh['ctx'=8,'fsdp'=4] {'fsdp'}, use_global_device_ids=true, to_apply=%add.2 | all-reduce | flops 6144 | bytes 24576
  45.8 28.7 %all-gather.15.cloned.1.call-done = bf16[768,768]{1,0:T(8,128)(2,1)} async-done(((bf16[192,768]{1,0:T(8,128)(2,1)}), bf16[768,768]{1,0:T(8,128)(2,1)}) %all-gather.15.cloned.1.call-update) | async-done | bytes 1179664 | tf_op jit(solution)/shard_map/all_gather | solution.py:87
  81.2 8.1 all-reduce.3
  89.3 13.4 %all-gather.1 = bf16[4,1,768]{2,1,0:T(2,128)(2,1)S(1)} all-gather(bf16[1,1,768]{2,1,0:T(2,128)(2,1)S(1)} %reshape.521), channel_id=1, replica_groups=mesh['ctx'=8,'fsdp'=4] {'fsdp'}, dimensions={0}, use_global_device_ids=true | all-gather | bytes 7680 | tf_op jit(solution)/shard_map/all_gather | solution.py:97
  108.4 25.4 %all-gather.13.cloned.1.call-done = bf16[1152,768]{1,0:T(8,128)(2,1)} async-done(((bf16[144,768]{1,0:T(8,128)(2,1)}), bf16[1152,768]{1,0:T(8,128)(2,1)}) %all-gather.13.cloned.1.call-update) | async-done | bytes 1769488 | tf_op jit(solution)/shard_map/all_gather | solution.py:124
  133.8 3.9 copy.55
  137.7 25.0 %all-gather.17.cloned.1.call-done = bf16[1152,768]{1,0:T(8,128)(2,1)} async-done(((bf16[144,768]{1,0:T(8,128)(2,1)}), bf16[1152,768]{1,0:T(8,128)(2,1)}) %all-gather.17.cloned.1.call-update) | async-done | bytes 1769488 | tf_op jit(solution)/shard_map/all_gather | solution.py:123
  162.7 3.9 copy.56
  166.6 19.6 %while.54 = (s32[]{:T(128)}, f32[12,144]{1,0:T(8,128)S(1)}, f32[12,144]{1,0:T(8,128)S(1)}, s32[1,144]{1,0:T(1,128)S(1)}, s32[1152]{0:T(1024)S(1)}, /*index=5*/bf...) while((s32[]{:T(128)}, f32[12,144]{1,0:T(8,128)S(1)}, ...), condition=%wide.region_5.6_spmd.clone, body=%wide.region_2.5_spmd.clone.sunk | while | flops 135719008 | bytes 11194762 | solution.py:150
  168.6 4.1 fusion.180
  178.4 4.1 fusion.180
  182.5 3.6 select_reduce_fusion.2
  186.8 12.0 %while.55 = (s32[]{:T(128)}, f32[144,12,64]{0,2,1:T(8,128)S(1)}, bf16[1152,768]{0,1:T(8,128)(2,1)}, s32[1,144]{1,0:T(1,128)S(1)}, s32[1152]{0:T(1024)S(1)}, /*in...) while((s32[]{:T(128)}, f32[144,12,64]{0,2,1:T(8,128)S(1)}, ...), condition=%wide.region_7.8_spmd.clone, body=%wide.region_6.7_spmd.clone.sunk | while | flops 259352208 | bytes 6605201 | solution.py:166
  201.0 83.7 %all-gather.23.cloned.1.call-done = bf16[768,3072]{1,0:T(8,128)(2,1)} async-done(((bf16[192,3072]{1,0:T(8,128)(2,1)}), bf16[768,3072]{1,0:T(8,128)(2,1)}) %all-gather.23.cloned.1.call-update) | async-done | bytes 4718608 | tf_op jit(solution)/shard_map/all_gather | solution.py:96
  284.7 4.6 convolution_add_fusion
  289.3 84.9 %all-gather.25.cloned.1.call-done = bf16[3072,768]{1,0:T(8,128)(2,1)} async-done(((bf16[768,768]{1,0:T(8,128)(2,1)}), bf16[3072,768]{1,0:T(8,128)(2,1)}) %all-gather.25.cloned.1.call-update) | async-done | bytes 4718608 | tf_op jit(solution)/shard_map/all_gather | solution.py:98
  374.2 4.0 fusion.53
  379.6 39.1 %all-reduce.18 = (f32[]{:T(128)}, f32[]{:T(128)}) all-reduce(f32[]{:T(128)} %get-tuple-element.1085, f32[]{:T(128)} %convert_reduce_fusion.3), channel_id=1, replica_groups=mesh['ctx'=8,'fsdp'=4] {'ctx','fsdp'}, use_global_device_ids=true, to_apply=%region_11.12 | all-reduce | flops 2 | bytes 16 | tf_op jit(solution)/shard_map/psum | solution.py:190
  420.2 6.1 fusion.110
  437.3 50.2 %while.56 = (s32[]{:T(128)}, f32[144,12,64]{0,2,1:T(8,128)}, f32[1152,768]{1,0:T(8,128)}, f32[1152,768]{1,0:T(8,128)}, bf16[1152,768]{0,1:T(8,128)(2,1)}, /*inde...) while((s32[]{:T(128)}, f32[144,12,64]{0,2,1:T(8,128)}, ...), condition=%wide.region_17.18_spmd.clone, body=%wide.region_16.17_spmd.clone.sunk | while | flops 647530112 | bytes 82789392 | solution.py:253
  492.5 43.2 %reduce-scatter.25.cloned.1.call-done = f32[144,768]{1,0:T(8,128)} async-done(((f32[1152,768]{1,0:T(8,128)}), f32[144,768]{1,0:T(8,128)}) %reduce-scatter.25.cloned.1.call-update) | async-done | bytes 442384
  538.8 48.4 %reduce-scatter.27.cloned.1.call-done = f32[144,768]{1,0:T(8,128)} async-done(((f32[1152,768]{1,0:T(8,128)}), f32[144,768]{1,0:T(8,128)}) %reduce-scatter.27.cloned.1.call-update) | async-done | bytes 442384
  590.1 3.7 convolution_convert_fusion.1
  594.8 5.4 convolution_convert_fusion
  604.1 15.1 %reduce-scatter.13.cloned.1.call-done = bf16[192,768]{1,0:T(8,128)(2,1)} async-done(((bf16[768,768]{1,0:T(8,128)(2,1)}), bf16[192,768]{1,0:T(8,128)(2,1)}) %reduce-scatter.13.cloned.1.call-update) | async-done | bytes 294928 | tf_op jit(solution)/shard_map/reduce_scatter | solution.py:283
  619.2 30.1 %reduce-scatter.19.cloned.1.call-done = bf16[192,768]{1,0:T(8,128)(2,1)} async-done(((bf16[768,768]{1,0:T(8,128)(2,1)}), bf16[192,768]{1,0:T(8,128)(2,1)}) %reduce-scatter.19.cloned.1.call-update) | async-done | bytes 294928 | tf_op jit(solution)/shard_map/reduce_scatter | solution.py:298
  652.6 17.4 %all-reduce.20 = (bf16[768]{0:T(1024)(128)(2,1)S(1)}, bf16[768]{0:T(1024)(128)(2,1)S(1)}, bf16[768]{0:T(1024)(128)(2,1)S(1)}, bf16[768]{0:T(1024)(128)(2,1)S(1)}...) all-reduce(bf16[768]{0:T(1024)(128)(2,1)S(1)} %get-tuple-element.96, ...), channel_id=5, replica_groups=mesh['ctx'=8,'fsdp'=4] {'fsdp'}, use_global_device_ids=true, to_apply=%region_23.24.clone | all-reduce | flops 9216 | bytes 36864
  671.3 9.5 reduce-scatter.15.cloned.1.call-done
  680.8 30.1 %reduce-scatter.17.cloned.1.call-done = bf16[192,768]{1,0:T(8,128)(2,1)} async-done(((bf16[768,768]{1,0:T(8,128)(2,1)}), bf16[192,768]{1,0:T(8,128)(2,1)}) %reduce-scatter.17.cloned.1.call-update) | async-done | bytes 294928 | tf_op jit(solution)/shard_map/reduce_scatter | solution.py:292
  710.9 86.1 %reduce-scatter.21.cloned.1.call-done = bf16[192,3072]{1,0:T(8,128)(2,1)} async-done(((bf16[768,3072]{1,0:T(8,128)(2,1)}), bf16[192,3072]{1,0:T(8,128)(2,1)}) %reduce-scatter.21.cloned.1.call-update) | async-done | bytes 1179664 | tf_op jit(solution)/shard_map/reduce_scatter | solution.py:310
  797.0 88.0 %reduce-scatter.23.cloned.1.call-done = bf16[768,768]{1,0:T(8,128)(2,1)} async-done(((bf16[3072,768]{1,0:T(8,128)(2,1)}), bf16[768,768]{1,0:T(8,128)(2,1)}) %reduce-scatter.23.cloned.1.call-update) | async-done | bytes 1179664 | tf_op jit(solution)/shard_map/reduce_scatter | solution.py:316
  885.0 144.6 %all-reduce.23 = (f32[192]{0:T(256)}, f32[192]{0:T(256)}, f32[192,768]{1,0:T(8,128)}, f32[192]{0:T(256)}, f32[192,768]{1,0:T(8,128)}, /*index=5*/f32[192,768]{1,...) all-reduce(f32[192]{0:T(256)S(1)} %get-tuple-element.1104, ...), channel_id=1, replica_groups=mesh['ctx'=8,'fsdp'=4] {'ctx'}, use_global_device_ids=true, to_apply=%region_24.25 | all-reduce | flops 1771776 | bytes 10635264 | tf_op jit(solution)/shard_map/psum | solution.py:323
  (294 shorter events, 132.0 us)
Async XLA Ops:
  7.2 67.3 %copy-start.6 = (bf16[1,144,768]{2,1,0:T(8,128)(2,1)S(1)}, bf16[1,144,768]{2,1,0:T(8,128)(2,1)}, u32[]{:S(2)}) copy-start(bf16[1,144,768]{2,1,0:T(8,128)(2,1)} %param.26) | copy-start | bytes 663556
  7.2 36.0 %all-gather.11.cloned.1.call-start = ((), (), s32[]{:S(2)}) async-start(), calls=%async_computation.8 | async-start | bytes 1474560 | tf_op jit(solution)/shard_map/all_gather | solution.py:88
  7.9 66.5 %all-gather.15.cloned.1.call-start = ((), (), s32[]{:S(2)}) async-start(), calls=%async_computation.10 | async-start | bytes 1474560 | tf_op jit(solution)/shard_map/all_gather | solution.py:87
  8.7 97.1 %all-gather.19.cloned.1.call-start = ((), (), s32[]{:S(2)}) async-start(), calls=%async_computation.12 | async-start | bytes 1474560 | tf_op jit(solution)/shard_map/all_gather | solution.py:85
  9.4 124.4 %all-gather.13.cloned.1.call-start = ((), (), s32[]{:S(2)}) async-start(), calls=%async_computation.9 | async-start | bytes 1990656 | tf_op jit(solution)/shard_map/all_gather | solution.py:124
  39.2 66.7 %copy-start.32 = (f32[768]{0:T(1024)}, f32[768]{0:T(1024)S(1)}, u32[]{:S(2)}) copy-start(f32[768]{0:T(1024)S(1)} %convert_element_type.239) | copy-start | bytes 9220
  39.2 66.6 %copy-start.26 = (f32[768]{0:T(1024)}, f32[768]{0:T(1024)S(1)}, u32[]{:S(2)}) copy-start(f32[768]{0:T(1024)S(1)} %convert_element_type.238) | copy-start | bytes 9220
  40.3 65.6 %copy-start.30 = (f32[144]{0:T(256)}, f32[144]{0:T(256)S(1)}, u32[]{:S(2)}) copy-start(f32[144]{0:T(256)S(1)} %broadcast_multiply_fusion.2) | copy-start | bytes 1732
  41.5 64.4 %copy-start.36 = (f32[144]{0:T(256)}, f32[144]{0:T(256)S(1)}, u32[]{:S(2)}) copy-start(f32[144]{0:T(256)S(1)} %fusion.82) | copy-start | bytes 1732
  45.7 116.9 %all-gather.17.cloned.1.call-start = ((), (), s32[]{:S(2)}) async-start(), calls=%async_computation.11 | async-start | bytes 1990656 | tf_op jit(solution)/shard_map/all_gather | solution.py:123
  76.9 122.0 %all-gather.21.cloned.1.call-start = ((), (), s32[]{:S(2)}) async-start(), calls=%async_computation.13 | async-start | bytes 1474560 | tf_op jit(solution)/shard_map/all_gather | solution.py:90
  77.5 207.3 %all-gather.23.cloned.1.call-start = ((), (), s32[]{:S(2)}) async-start(), calls=%async_computation.14 | async-start | bytes 5898240 | tf_op jit(solution)/shard_map/all_gather | solution.py:96
  78.2 296.0 %all-gather.25.cloned.1.call-start = ((), (), s32[]{:S(2)}) async-start(), calls=%async_computation.15 | async-start | bytes 5898240 | tf_op jit(solution)/shard_map/all_gather | solution.py:98
  79.0 456.8 %reduce-scatter.25.cloned.1.call-start = ((), (), s32[]{:S(2)}) async-start(), calls=%async_computation.22 | async-start | bytes 3981312
  102.7 182.0 %copy-start.28 = (f32[768]{0:T(1024)}, f32[768]{0:T(1024)S(1)}, u32[]{:S(2)}) copy-start(f32[768]{0:T(1024)S(1)} %convert_element_type.250) | copy-start | bytes 9220
  198.8 90.5 %copy-start.15 = (bf16[144,12,64]{0,2,1:T(8,128)(2,1)}, bf16[144,12,64]{0,2,1:T(8,128)(2,1)S(1)}, u32[]{:S(2)}) copy-start(bf16[144,12,64]{0,2,1:T(8,128)(2,1)S(1)} %convert_element_type.246) | copy-start | bytes 663556
  200.7 228.0 %copy-start.4 = (f32[144,768]{1,0:T(8,128)}, f32[144,768]{1,0:T(8,128)S(1)}, u32[]{:S(2)}) copy-start(f32[144,768]{1,0:T(8,128)S(1)} %get-tuple-element.1092) | copy-start | bytes 1327108
  200.8 228.0 %copy-start.34 = (f32[144]{0:T(256)}, f32[144]{0:T(256)S(1)}, u32[]{:S(2)}) copy-start(f32[144]{0:T(256)S(1)} %broadcast_multiply_fusion.1) | copy-start | bytes 1732
  201.0 227.8 %copy-start.38 = (f32[144]{0:T(256)}, f32[144]{0:T(256)S(1)}, u32[]{:S(2)}) copy-start(f32[144]{0:T(256)S(1)} %fusion.83) | copy-start | bytes 1732
  289.3 88.9 %copy-start.21 = (bf16[1,144,768]{2,1,0:T(8,128)(2,1)S(1)}, bf16[1,144,768]{2,1,0:T(8,128)(2,1)}, u32[]{:S(2)}) copy-start(bf16[1,144,768]{2,1,0:T(8,128)(2,1)} %param.29) | copy-start | bytes 663556
  289.3 130.2 %copy-start.25 = (bf16[1,144,768]{2,1,0:T(8,128)(2,1)S(1)}, bf16[1,144,768]{2,1,0:T(8,128)(2,1)}, u32[]{:S(2)}) copy-start(bf16[1,144,768]{2,1,0:T(8,128)(2,1)} %param.30) | copy-start | bytes 663556
  487.5 99.6 %reduce-scatter.27.cloned.1.call-start = ((), (), s32[]{:S(2)}) async-start(), calls=%async_computation.23 | async-start | bytes 3981312
  488.1 131.1 %reduce-scatter.13.cloned.1.call-start = ((), (), s32[]{:S(2)}) async-start(), calls=%async_computation.16 | async-start | bytes 1474560 | tf_op jit(solution)/shard_map/reduce_scatter | solution.py:283
  490.6 158.7 %reduce-scatter.19.cloned.1.call-start = ((), (), s32[]{:S(2)}) async-start(), calls=%async_computation.19 | async-start | bytes 1474560 | tf_op jit(solution)/shard_map/reduce_scatter | solution.py:298
  492.5 188.3 %reduce-scatter.15.cloned.1.call-start = ((), (), s32[]{:S(2)}) async-start(), calls=%async_computation.17 | async-start | bytes 1474560 | tf_op jit(solution)/shard_map/reduce_scatter | solution.py:289
  538.7 51.4 %copy-start.5 = (f32[144,768]{1,0:T(8,128)S(1)}, f32[144,768]{1,0:T(8,128)}, u32[]{:S(2)}) copy-start(f32[144,768]{1,0:T(8,128)} %copy-done.4) | copy-start | bytes 1327108
  538.7 51.4 %copy-start.14 = (bf16[144,3072]{1,0:T(8,128)(2,1)S(1)}, bf16[144,3072]{1,0:T(8,128)(2,1)}, u32[]{:S(2)}) copy-start(bf16[144,3072]{1,0:T(8,128)(2,1)} %copy-done.13) | copy-start | bytes 2654212
  538.7 172.1 %reduce-scatter.17.cloned.1.call-start = ((), (), s32[]{:S(2)}) async-start(), calls=%async_computation.18 | async-start | bytes 1474560 | tf_op jit(solution)/shard_map/reduce_scatter | solution.py:292
  590.0 207.0 %reduce-scatter.21.cloned.1.call-start = ((), (), s32[]{:S(2)}) async-start(), calls=%async_computation.20 | async-start | bytes 5898240 | tf_op jit(solution)/shard_map/reduce_scatter | solution.py:310
  593.8 291.1 %reduce-scatter.23.cloned.1.call-start = ((), (), s32[]{:S(2)}) async-start(), calls=%async_computation.21 | async-start | bytes 5898240 | tf_op jit(solution)/shard_map/reduce_scatter | solution.py:316
  652.1 232.9 %copy-start.22 = (bf16[192,768]{1,0:T(8,128)(2,1)S(1)}, bf16[192,768]{1,0:T(8,128)(2,1)}, u32[]{:S(2)}) copy-start(bf16[192,768]{1,0:T(8,128)(2,1)} %reduce-scatter.13.cloned.1.call-done) | copy-start | bytes 884740
  652.1 232.8 %copy-start.23 = (bf16[192,768]{1,0:T(8,128)(2,1)S(1)}, bf16[192,768]{1,0:T(8,128)(2,1)}, u32[]{:S(2)}) copy-start(bf16[192,768]{1,0:T(8,128)(2,1)} %reduce-scatter.19.cloned.1.call-done) | copy-start | bytes 884740
  (41 other events, 371.4 us)
Sparse Core Ops, SparseCore 0:
  9.6 33.5 all-gather.10
  44.8 29.6 all-gather.14
  76.0 29.7 all-gather.18
  108.1 25.6 all-gather.12
  136.1 26.5 all-gather.16
  164.1 30.4 all-gather.20
  196.1 88.5 all-gather.22
  286.3 87.8 all-gather.24
  487.6 48.0 reduce-scatter.24
  539.1 48.0 reduce-scatter.26
  590.1 29.1 reduce-scatter.12
  621.4 27.8 reduce-scatter.18
  652.2 28.4 reduce-scatter.14
  682.9 27.8 reduce-scatter.16
  713.0 83.9 reduce-scatter.20
  799.2 85.7 reduce-scatter.22
where the time goes:
time: 1040 us
  waiting for transfers between devices  608 us (58%)
  blocking collectives  244 us (23%)
  matrix products  87 us (8%)
  local copies, waits for them, and re-layouts  58.1 us (6%)
  other arithmetic  19.9 us (2%)
  between operations  19.8 us (2%)
    psum x1, blocking collectives, shards(): lax.psum((shares[0], shares[1], shares[2], shares[3], shares[4], shares[5...  145 us
    unnamed x18, waiting for transfers between devices  96.1 us
    reduce_scatter x1, waiting for transfers between devices, shards(): lax.psum_scatter(grad_down_weight.astype(jnp.bfloat16), 'fsdp', scatter_d...  88 us
    reduce_scatter x1, waiting for transfers between devices, shards(): lax.psum_scatter(grad_up_weight.astype(jnp.bfloat16), 'fsdp', scatter_dim...  86.1 us
    all_gather x1, waiting for transfers between devices, shards(): lax.all_gather(down_weight, 'fsdp', axis=0, tiled=True)  84.9 us
    all_gather x1, waiting for transfers between devices, shards(): lax.all_gather(up_weight, 'fsdp', axis=0, tiled=True)  83.7 us
    psum x1, blocking collectives, shards(): lax.psum((jnp.sum(valid_float[:, None] * mismatch * mismatch), jnp.sum(va...  39.1 us
    unnamed x2, blocking collectives  38.4 us
  transfers between devices with their start and end apart: 16, of which 15 were waited for; matrix products, arithmetic and copies ran while one was open for 9% of the time, Pallas kernels for 0%

commit v1 on v0

--- a/solution.py
+++ b/solution.py
@@ -1,6 +1,8 @@
 import jax
 import jax.numpy as jnp
 from jax import lax
+from jax.experimental import pallas as pl
+from jax.experimental.pallas import tpu as pltpu
 from jax.sharding import PartitionSpec as P
 
 HEADS = 12
@@ -362,7 +364,993 @@
     )
 
 
+F32 = jnp.float32
+BF16 = jnp.bfloat16
+ANY = pl.BlockSpec(memory_space=pl.ANY)
+VMEM = pl.BlockSpec(memory_space=pltpu.VMEM)
+SMEM = pl.BlockSpec(memory_space=pltpu.SMEM)
+NT = (((1,), (1,)), ((), ()))
+TN = (((0,), (0,)), ((), ()))
+NN = (((1,), (0,)), ((), ()))
+
+
+def swap_cores(value):
+    size = lax.axis_size("ctx")
+    return lax.ppermute(value, "ctx", [(i, i ^ 1) for i in range(size)])
+
+
+def both_cores(value):
+    pairs = [[i, i + 1] for i in range(0, lax.axis_size("ctx"), 2)]
+    return lax.all_gather(value, "ctx", axis=0, tiled=True, axis_index_groups=pairs)
+
+
+def swap_chips(value, step):
+    size = lax.axis_size("ctx")
+    return lax.ppermute(value, "ctx", [(i, i ^ (2 * step)) for i in range(size)])
+
+
+def swap_planes(value, step):
+    size = lax.axis_size("fsdp")
+    return lax.ppermute(value, "fsdp", [(i, i ^ step) for i in range(size)])
+
+
+def trade_chips(value):
+    size = lax.axis_size("ctx")
+    groups = [[i for i in range(size) if i % 2 == c] for c in (0, 1)]
+    return lax.all_to_all(value, "ctx", 0, 0, axis_index_groups=groups, tiled=True)
+
+
+def trade_planes(value):
+    return lax.all_to_all(value, "fsdp", 0, 0, tiled=True)
+
+
+def shaped(*shape, dtype=BF16):
+    return jax.ShapeDtypeStruct(shape, dtype)
+
+
+def wide(*shape):
+    return jax.ShapeDtypeStruct(shape, F32)
+
+
+def local_call(body, outs, where, args, far=(), scratch=(), after=(), scalar=None, vmem=12, cost=0):
+    args, after, many = list(args), list(after), isinstance(outs, tuple)
+    count = len(args)
+
+    def kernel(where_ref, *refs):
+        body(where_ref, *refs[:count], *refs[count + len(after) :])
+
+    return pl.pallas_call(
+        kernel,
+        out_shape=outs,
+        in_specs=[pl.BlockSpec(memory_space=pltpu.SMEM)]
+        + [ANY if i in far else VMEM for i in range(count)]
+        + [ANY] * len(after),
+        out_specs=tuple(SMEM if i == scalar else VMEM for i in range(len(outs))) if many else VMEM,
+        scratch_shapes=scratch,
+        compiler_params=pltpu.CompilerParams(vmem_limit_bytes=vmem << 20),
+        cost_estimate=pl.CostEstimate(
+            flops=cost * 10**9, transcendentals=0, bytes_accessed=cost * 10**6
+        ),
+    )(where, *args, *after)
+
+
+def core_rows(core, count):
+    return pl.ds(pl.multiple_of(count * core, 16), count)
+
+
+def rows_at(start, count, align):
+    return pl.ds(pl.multiple_of(start, align), count)
+
+
+def dot(left, right, dims):
+    return lax.dot_general(left, right, dims, preferred_element_type=F32)
+
+
+def run_copies(copies, sems):
+    started = [
+        pltpu.make_async_copy(source, target, sems.at[i])
+        for i, (source, target) in enumerate(copies)
+    ]
+    for copy in started:
+        copy.start()
+    for copy in started:
+        copy.wait()
+
+
+def unit_rows(values):
+    centred = values - jnp.mean(values, axis=-1, keepdims=True)
+    spread = jnp.mean(centred * centred, axis=-1, keepdims=True)
+    inverse = lax.rsqrt(spread + EPSILON)
+    return centred * inverse, inverse
+
+
+def unit_back(grad, gain, unit, inverse):
+    scaled = grad * gain
+    return inverse * (
+        scaled
+        - jnp.mean(scaled, axis=-1, keepdims=True)
+        - unit * jnp.mean(scaled * unit, axis=-1, keepdims=True)
+    )
+
+
+def pack_tokens(where, tokens, segment, valid, out):
+    rows, width = tokens.shape
+    ids = segment[...]
+    line = lax.broadcasted_iota(jnp.int32, (16, rows), 0)
+    codes = jnp.where(
+        line == 0,
+        ids >> 7,
+        jnp.where(line == 1, ids & 127, jnp.where(line == 2, valid[...], 0)),
+    )
+    codes = codes.astype(F32).astype(out.dtype)
+    for i in range(4):
+        start = (rows + 16) * i
+        out[start : start + rows, :] = tokens[...]
+        out[start + rows : start + rows + 16, :] = jnp.zeros((16, width), out.dtype)
+        out[start + rows : start + rows + 16, :rows] = codes
+
+
+def pack_projections(where, *refs):
+    weights, vectors, long, valid, out = refs[:3], refs[3:11], refs[11], refs[12], refs[13]
+    held, small, held_long, sems = refs[14], refs[15:23], refs[23], refs[24]
+    half, feat = held.shape[1], small[0].shape[0]
+    own_rows = rows_at(half * where[1], half, 32)
+    run_copies(
+        [(w.at[own_rows], held.at[i]) for i, w in enumerate(weights)]
+        + list(zip(vectors, small))
+        + [(long, held_long)],
+        sems,
+    )
+    for chip in range(4):
+
+        @pl.when(where[0] == chip)
+        def _():
+            for i in range(3):
+                out[:, feat * i : feat * (i + 1)] = held[i, :, feat * chip : feat * (chip + 1)]
+
+    spread = held_long[...].astype(F32).reshape(1, 4 * feat)
+    count = jnp.sum(valid[...].astype(F32), axis=1, keepdims=True)
+    lines = [v[...].astype(F32).reshape(1, feat) for v in small]
+    lines += [spread[:, feat * i : feat * (i + 1)] for i in range(4)]
+    lines += [jnp.broadcast_to(count, (1, feat)), jnp.zeros((half - 13, feat), F32)]
+    out[:, 3 * feat :] = jnp.concatenate(lines, axis=0).astype(out.dtype)
+
+
+def pack_blocks(where, up, output, down, out_up, out_down, sems):
+    chip, core = where[0], where[1]
+    part, units = out_up.shape[0], out_up.shape[1] // 5
+    rows = rows_at(part * chip, part, 16)
+    down_part = out_down.shape[0]
+    copies = [
+        (
+            up.at[rows, rows_at(2 * units * i + units * core, units, 128)],
+            out_up.at[:, units * i : units * (i + 1)],
+        )
+        for i in range(4)
+    ]
+    copies += [
+        (output.at[rows, rows_at(units * core, units, 128)], out_up.at[:, 4 * units :]),
+        (down.at[rows_at(4 * down_part * core + down_part * chip, down_part, 32)], out_down),
+    ]
+    run_copies(copies, sems)
+
+
+def stack_rows(where, *refs):
+    pieces, out = refs[:-1], refs[-1]
+    rows = pieces[0].shape[0]
+    for i, piece in enumerate(pieces):
+        out[rows * i : rows * (i + 1), :] = piece[...]
+
+
+def three_blocks(pieces, part):
+    p0, p1, p2, low, high = pieces
+    parts = [(k, [(p, 0)]) for k, p in enumerate((p0, p1, p2))] + [(3, [(low, 0), (high, low.shape[0])])]
+    found = []
+    for k, refs in parts:
+        for s in (1, 2, 3):
+            for ref, base in refs:
+                start, end = max(part * (s - 1), base), min(part * s, base + ref.shape[0])
+                if start < end:
+                    found.append((k, s, start - part * (s - 1), end - start, ref, start - base))
+    return found
+
+
+def cross_halves(where, from_x, from_y, to_x, to_y):
+    cut = to_x.shape[0]
+    to_x[...] = from_y[:cut, :]
+    to_y[...] = from_x[cut:, :]
+
+
+def build_up(where, up, p0, p1, p2, p3, p4, out, sems):
+    chip, core, plane = where[0], where[1], where[2]
+    units, shard = up.shape[1] // 8, up.shape[0]
+    part = shard // 4
+    own = rows_at(shard * plane, shard, 64)
+    copies = [
+        pltpu.make_async_copy(
+            up.at[:, rows_at(2 * units * i + units * core, units, 128)],
+            out.at[own, units * i : units * (i + 1)],
+            sems.at[i],
+        )
+        for i in range(4)
+    ]
+    for copy in copies:
+        copy.start()
+    for k, s, offset, count, piece, start in three_blocks((p0, p1, p2, p3, p4), part):
+        at = rows_at(shard * (plane ^ s) + part * (chip ^ k) + offset, count, 16)
+        out[at, :] = piece[start : start + count, : 4 * units]
+    for copy in copies:
+        copy.wait()
+
+
+def build_half(where, output, p0, p1, p2, p3, p4, out):
+    chip, core, plane = where[0], where[1], where[2]
+    shard, units = output.shape[0], out.shape[1]
+    part = shard // 4
+    out[rows_at(shard * plane, shard, 64), :] = output[:, rows_at(units * core, units, 128)]
+    for k, s, offset, count, piece, start in three_blocks((p0, p1, p2, p3, p4), part):
+        at = rows_at(shard * (plane ^ s) + part * (chip ^ k) + offset, count, 16)
+        out[at, :] = piece[start : start + count, 4 * units :]
+
+
+def build_down(where, down, p0, p1, p2, p3, p4, out, sem):
+    chip, core, plane = where[0], where[1], where[2]
+    mine = down.shape[0] // 2
+    part = mine // 4
+    own = pltpu.make_async_copy(
+        down.at[rows_at(mine * core, mine, 128)], out.at[rows_at(mine * plane, mine, 128)], sem
+    )
+    own.start()
+    for k, s, offset, count, piece, start in three_blocks((p0, p1, p2, p3, p4), part):
+        at = rows_at(mine * (plane ^ s) + part * (chip ^ k) + offset, count, 16)
+        out[at, :] = piece[start : start + count, :]
+    own.wait()
+
+
+def build_output(where, near, far, out):
+    units = near.shape[1]
+    out[:, rows_at(units * where[1], units, 128)] = near[...]
+    out[:, rows_at(units * (1 - where[1]), units, 128)] = far[...]
+
+
+def normalize_tokens(where, near, far, unit_low, key_row, query_column):
+    rows = query_column.shape[0] // 4
+    for i in range(8):
+        block = (near if i < 4 else far).at[(rows + 16) * (i % 4) : (rows + 16) * (i % 4 + 1), :]
+        unit, _ = unit_rows(block[:rows, :].astype(F32))
+        unit_low[rows * i : rows * (i + 1), :] = unit
+        codes = block[rows:, :].astype(F32)
+        ids = codes[0:1, :rows] * 128.0 + codes[1:2, :rows]
+        key_row[0:1, rows * i : rows * (i + 1)] = jnp.where(codes[2:3, :rows] == 1.0, ids, -1.0)
+        if i < 4:
+            query_column[rows * i : rows * (i + 1), :] = jnp.broadcast_to(
+                ids.reshape(rows, 1), (rows, 128)
+            )
+
+
+def attend(where, *refs):
+    units, key_row, query_column, weights, far_weights = refs[:3] + (refs[3:7], refs[7])
+    h_one, w_three, projected, probs, mixed, sent, vectors, long = refs[8:16]
+    small, bias = refs[16:]
+    core, plane = where[1], where[2]
+    half, width = weights[0].shape
+    feat = width // 4
+    group = query_column.shape[0]
+    rows = group // 4
+
+    count = jnp.zeros((1, 1), F32)
+    for s, piece in enumerate(weights):
+        base = 2 * half * (plane ^ s)
+        w_three[rows_at(base + half * core, half, 32), :] = piece[:, : 3 * feat]
+        other = far_weights[half * s : half * (s + 1), :]
+        w_three[rows_at(base + half * (1 - core), half, 32), :] = other[:, : 3 * feat]
+        near = piece[:16, 3 * feat :].astype(F32)
+        small[plane ^ s] = near
+        count += near[12:13, :1] + other[12:13, 3 * feat : 3 * feat + 1].astype(F32)
+    vectors[...] = jnp.zeros(vectors.shape, F32)
+    for p in range(4):
+        lines = small[p]
+        for i, r in enumerate((0, 1, 4, 5, 6, 7)):
+            vectors[i : i + 1, feat * p : feat * (p + 1)] = lines[r : r + 1, :]
+        pair = jnp.where(core == 0, lines[8:10, :], lines[10:12, :])
+        long[:, 2 * feat * p : 2 * feat * p + feat] = pair[:1, :]
+        long[:, 2 * feat * p + feat : 2 * feat * (p + 1)] = pair[1:, :]
+    gain, shift = vectors[0:1, :], vectors[1:2, :]
+    short = small[where[0]]
+    h_one[...] = (units[...] * gain + shift).astype(BF16)
+    values = dot(h_one[...], w_three[...], NN)
+    query = (values[:group, :feat] + short[2:3, :]).astype(BF16) * jnp.asarray(
+        HEAD_DIM**-0.5, BF16
+    )
+    projected[:group, :feat] = query
+    projected[group:, :feat] = jnp.zeros((group, feat), BF16)
+    projected[:, feat : 2 * feat] = values[:, feat : 2 * feat].astype(BF16)
+    projected[:, 2 * feat :] = (values[:, 2 * feat :] + short[3:4, :]).astype(BF16)
+    column = lax.broadcasted_iota(jnp.int32, (rows, 2 * group), 1)
+    line = lax.broadcasted_iota(jnp.int32, (rows, 2 * group), 0)
+    for k in range(4):
+        ids = query_column[rows * k : rows * (k + 1), :1]
+        allowed = (ids == key_row[0:1, :]) | (column == line + rows * k)
+        bias[rows * k : rows * (k + 1), :] = jnp.where(allowed, 0.0, MASKED)
+    for h in range(feat // HEAD_DIM):
+        at = slice(HEAD_DIM * h, HEAD_DIM * (h + 1))
+        keys = projected[:, feat + HEAD_DIM * h : feat + HEAD_DIM * (h + 1)]
+        held = projected[:, 2 * feat + HEAD_DIM * h : 2 * feat + HEAD_DIM * (h + 1)]
+        for k in range(4):
+            block = slice(rows * k, rows * (k + 1))
+            scores = dot(projected[block, at], keys, NT) + bias[block, :]
+            weight = jnp.exp(scores - jnp.max(scores, axis=1, keepdims=True))
+            weight = weight * (1.0 / jnp.sum(weight, axis=1, keepdims=True))
+            low = weight.astype(BF16)
+            probs[h, block, :] = low
+            result = dot(low, held, NN)
+            mixed[block, at] = result
+            sent[(rows + 16) * k : (rows + 16) * k + rows, at] = result.astype(BF16)
+    high = jnp.floor(count / 128.0)
+    side = lax.broadcasted_iota(jnp.int32, (16, feat), 1)
+    digits = jnp.where(side == 0, high, jnp.where(side == 1, count - 128.0 * high, 0.0))
+    for k in range(4):
+        sent[(rows + 16) * k + rows : (rows + 16) * (k + 1), :] = digits.astype(BF16)
+
+
+def attend_back(where, d_all, probs, projected, mixed, h_one, w_three, vectors, *outs):
+    d_three, kept, given, lines, d_scores, grads = outs
+    core = where[1]
+    group, feat = d_all.shape
+    rows, width = group // 4, h_one.shape[1]
+    scale = HEAD_DIM**-0.5
+    d_three[group:, :feat] = jnp.zeros((group, feat), BF16)
+    for h in range(feat // HEAD_DIM):
+        at = slice(HEAD_DIM * h, HEAD_DIM * (h + 1))
+        key_at = slice(feat + HEAD_DIM * h, feat + HEAD_DIM * (h + 1))
+        value_at = slice(2 * feat + HEAD_DIM * h, 2 * feat + HEAD_DIM * (h + 1))
+        keys, held = projected[:, key_at], projected[:, value_at]
+        for k in range(4):
+            block = slice(rows * k, rows * (k + 1))
+            d_mixed = d_all[block, at]
+            delta = jnp.sum(d_mixed.astype(F32) * mixed[block, at], axis=1, keepdims=True)
+            d_probs = dot(d_mixed, held, NT)
+            low = (probs[h, block, :].astype(F32) * (d_probs - delta)).astype(BF16)
+            d_scores[block, :] = low
+            d_three[block, at] = (dot(low, keys, NN) * scale).astype(BF16)
+        d_three[:, key_at] = dot(d_scores[...], projected[:group, at], TN).astype(BF16)
+        d_three[:, value_at] = dot(probs[h], d_all[:, at], TN).astype(BF16)
+    grads[...] = dot(h_one[...], d_three[...], TN)
+    half = kept.shape[0] // 4
+    for p in range(4):
+        block = slice(half * p, half * (p + 1))
+        kept[block, :] = grads[rows_at(2 * half * p + half * core, half, 32), :]
+        given[block, :] = grads[rows_at(2 * half * p + half * (1 - core), half, 32), :].astype(BF16)
+    sums = jnp.sum(d_three[...].astype(F32), axis=0, keepdims=True)
+    weight = w_three[...].astype(F32)
+    with_gain = jnp.sum(grads[...] * weight, axis=1, keepdims=True)
+    with_shift = jnp.sum(weight * sums, axis=1, keepdims=True)
+    side = lax.broadcasted_iota(jnp.int32, (width, 128), 1)
+    both = jnp.where(side == 0, with_gain, jnp.where(side == 1, with_shift, 0.0)).T
+    d_shift = both[1:2, :]
+    lines[0:1, :] = (both[0:1, :] - vectors[1:2, :] * d_shift) / vectors[0:1, :]
+    lines[1:2, :] = d_shift
+    lines[2:3, :] = jnp.zeros((1, width), F32)
+    lines[2:3, :feat] = sums[:, :feat]
+    lines[3:4, :] = jnp.zeros((1, width), F32)
+    lines[3:4, :feat] = sums[:, 2 * feat :]
+    lines[4:, :] = jnp.zeros((4, width), F32)
+
+
+def inputs_back(where, d_three, w_three, near, far):
+    group = near.shape[0]
+    near[...] = dot(d_three[:group, :], w_three[...], NT)
+    far[...] = dot(d_three[group:, :], w_three[...], NT).astype(BF16)
+
+
+def share_inputs(where, near, far, *outs):
+    rows = outs[0].shape[0]
+    for k, out in enumerate(outs):
+        at = rows_at(rows * (where[0] ^ k), rows, 16)
+        out[...] = (near[at, :] + far[at, :].astype(F32)).astype(out.dtype)
+
+
+def finish_inputs(where, d0, d1, d2, d3, tokens, d_second, vectors, out):
+    total = d0[...]
+    for piece in (d1, d2, d3):
+        total = total + piece[...].astype(F32)
+    unit, inverse = unit_rows(tokens[...].astype(F32))
+    d_inputs = unit_back(total, vectors[0:1, :], unit, inverse)
+    out[...] = (d_second[...] + d_inputs).astype(BF16)
+
+
+def project_output(where, mixed, w_output, tokens, vectors, second, h_two, count):
+    rows, width = tokens.shape
+    feat = mixed.shape[1]
+    total = tokens[...].astype(F32) + vectors[2:3, :]
+    valid = jnp.zeros((1, 1), F32)
+    for k in range(4):
+        start = (rows + 16) * k
+        total += dot(mixed[start : start + rows, :], w_output[feat * k : feat * (k + 1), :], NN)
+        digits = mixed[start + rows : start + rows + 16, :].astype(F32)
+        valid += digits[0:1, 0:1] * 128.0 + digits[0:1, 1:2]
+    second[...] = total
+    unit, _ = unit_rows(total)
+    h_two[...] = (unit * vectors[3:4, :] + vectors[4:5, :]).astype(BF16)
+    count[...] = jnp.broadcast_to(valid, count.shape)
+
+
+def activate(where, h_pair, w_up, b_up, act, slope):
+    rows = h_pair.shape[0] // 2
+    root = 0.7978845608028654
+    for i in range(2):
+        block = slice(rows * i, rows * (i + 1))
+        value = dot(h_pair[block, :], w_up[...], NN) + b_up[...]
+        square = value * value
+        bent = jnp.tanh(root * value * (1.0 + 0.044715 * square))
+        act[block, :] = (0.5 * value * (1.0 + bent)).astype(BF16)
+        slope[block, :] = 0.5 * (1.0 + bent) + 0.5 * value * (1.0 - bent * bent) * root * (
+            1.0 + 3.0 * 0.044715 * square
+        )
+
+
+def project_down(where, act, w_down, near, far):
+    rows, core = near.shape[0], where[1]
+    near[...] = dot(act[core_rows(core, rows), :], w_down[...], NN)
+    far[...] = dot(act[core_rows(1 - core, rows), :], w_down[...], NN).astype(BF16)
+
+
+def compare(where, second, near, far, vectors, teacher, cotangent, valid, count, *outs):
+    layer_output, d_result, d_down, lines = outs
+    rows, width = second.shape
+    other = far[core_rows(1 - where[1], rows), :].astype(F32)
+    result = second[...] + near[...] + other + vectors[5:6, :]
+    layer_output[...] = result.astype(BF16)
+    kept = valid[...].astype(F32).reshape(rows, 1)
+    mismatch = result - teacher[...].astype(F32)
+    weighted = kept * mismatch
+    error = jnp.sum(jnp.sum(weighted * mismatch, axis=1, keepdims=True), axis=0, keepdims=True)
+    total = cotangent[...].astype(F32) + 2.0 / (width * count[0:1, 0:1]) * weighted
+    d_result[...] = total
+    low = total.astype(BF16)
+    d_down[...] = low
+    high = error.astype(BF16).astype(F32)
+    middle = (error - high).astype(BF16).astype(F32)
+    side = lax.broadcasted_iota(jnp.int32, (1, width), 1)
+    parts = jnp.where(
+        side == 0, high, jnp.where(side == 1, middle, jnp.where(side == 2, error - high - middle, 0.0))
+    )
+    lines[0:1, :] = jnp.sum(low.astype(F32), axis=0, keepdims=True)
+    lines[1:2, :] = parts
+    lines[2:, :] = jnp.zeros((6, width), F32)
+
+
+def activate_back(where, d_down, w_down, slope, w_up, d_up, near, far, line):
+    rows, core = near.shape[0], where[1]
+    total = jnp.zeros(line.shape, F32)
+    for i in range(2):
+        block = slice(rows * i, rows * (i + 1))
+        low = (dot(d_down[block, :], w_down[...], NT) * slope[block, :]).astype(BF16)
+        d_up[block, :] = low
+        total += jnp.sum(low.astype(F32), axis=0, keepdims=True)
+    line[...] = total
+    near[...] = dot(d_up[core_rows(core, rows), :], w_up[...], NT)
+    far[...] = dot(d_up[core_rows(1 - core, rows), :], w_up[...], NT).astype(BF16)
+
+
+def second_back(where, near, far, d_result, second, vectors, w_output, *outs):
+    d_second, d_attn, lines, sent = outs
+    rows = near.shape[0]
+    d_two = near[...] + far[core_rows(1 - where[1], rows), :].astype(F32)
+    unit, inverse = unit_rows(second[...])
+    total = d_result[...] + unit_back(d_two, vectors[3:4, :], unit, inverse)
+    d_second[...] = total
+    low = total.astype(BF16)
+    d_attn[...] = low
+    lines[0:1, :] = jnp.sum(low.astype(F32), axis=0, keepdims=True)
+    lines[1:2, :] = jnp.sum(d_two * unit, axis=0, keepdims=True)
+    lines[2:3, :] = jnp.sum(d_two, axis=0, keepdims=True)
+    lines[3:, :] = jnp.zeros((5, lines.shape[1]), F32)
+    feat = sent.shape[1]
+    for k in range(4):
+        part = w_output[feat * k : feat * (k + 1), :]
+        sent[rows * k : rows * (k + 1), :] = dot(low, part, NT).astype(BF16)
+
+
+def output_grads(where, mixed, d_attn, kept, given):
+    core = where[1]
+    rows, width = d_attn.shape
+    feat, units = mixed.shape[1], width // 2
+    mine = d_attn[:, rows_at(units * core, units, 128)]
+    others = d_attn[:, rows_at(units * (1 - core), units, 128)]
+    for k in range(4):
+        at = slice(feat * k, feat * (k + 1))
+        piece = mixed[(rows + 16) * k : (rows + 16) * k + rows, :]
+        kept[at, :] = dot(piece, mine, TN)
+        given[at, :] = dot(piece, others, TN).astype(BF16)
+
+
+def split_chips(chip, block, outs, count):
+    own, to_x, to_y, then_x, then_y = outs
+    for p in range(4):
+        own[count * p : count * (p + 1), :] = block(chip, p)
+    for p in (0, 1):
+        low, high = slice(count * p, count * (p + 1)), slice(count * (p + 2), count * (p + 3))
+        to_x[low, :] = block(chip ^ 1, p).astype(BF16)
+        to_x[high, :] = block(chip ^ 3, p).astype(BF16)
+        to_y[low, :] = block(chip ^ 2, p + 2).astype(BF16)
+        to_y[high, :] = block(chip ^ 3, p + 2).astype(BF16)
+        then_x[low, :] = block(chip ^ 1, p + 2)
+        then_y[low, :] = block(chip ^ 2, p)
+
+
+def pass_on(where, from_x, from_y, then_x, then_y, to_x, to_y):
+    half = to_x.shape[0]
+    to_x[...] = (then_x[...] + from_y[half:, :].astype(F32)).astype(BF16)
+    to_y[...] = (then_y[...] + from_x[half:, :].astype(F32)).astype(BF16)
+
+
+def add_chips(own, from_x, from_y, last_x, last_y):
+    half = last_x.shape[0]
+    low = own[:half, :] + from_x[:half, :].astype(F32) + last_y[...].astype(F32)
+    high = own[half:, :] + from_y[:half, :].astype(F32) + last_x[...].astype(F32)
+    return low, high
+
+
+def down_grads(where, act, d_down, *refs):
+    outs, total = refs[:5], refs[5]
+    count = outs[0].shape[0] // 4
+    total[...] = dot(act[...], d_down[...], TN)
+
+    def block(j, p):
+        return total[rows_at(4 * count * p + count * j, count, 32), :]
+
+    split_chips(where[0], block, outs, count)
+
+
+def up_grads(where, h_pair, d_up, kept, given, *refs):
+    outs, total = refs[:5], refs[5]
+    count, units = outs[0].shape[0] // 4, d_up.shape[1]
+    total[:, :units] = dot(h_pair[...], d_up[...], TN)
+    total[:, units:] = kept[...] + given[...].astype(F32)
+
+    def block(j, p):
+        return total[rows_at(4 * count * p + count * j, count, 16), :]
+
+    split_chips(where[0], block, outs, count)
+
+
+def send_planes(where, own, from_x, from_y, last_x, last_y, *refs):
+    outs, total = refs[:4], refs[4]
+    part, half = outs[0].shape[0], last_x.shape[0]
+    total[:half, :], total[half:, :] = add_chips(own, from_x, from_y, last_x, last_y)
+    for s, out in enumerate(outs):
+        out[...] = total[rows_at(part * (where[2] ^ s), part, 16), :].astype(out.dtype)
+
+
+def sum_pieces(where, own, p1, p2, p3, out):
+    total = own[...].astype(F32)
+    for piece in (p1, p2, p3):
+        total = total + piece[...].astype(F32)
+    out[...] = total.astype(out.dtype)
+
+
+def finish_down(where, n0, n1, n2, n3, far, out):
+    chip, core = where[0], where[1]
+    both = n0.shape[0]
+    part = both // 2
+    for k, piece in enumerate((n0, n1, n2, n3)):
+        at = part * (chip ^ k)
+        out[rows_at(4 * part * core + at, part, 32), :] = piece[part:, :].astype(F32)
+        out[rows_at(4 * part * (1 - core) + at, part, 32), :] = far[
+            both * k + part : both * (k + 1), :
+        ].astype(F32)
+
+
+def finish_up(where, n0, n1, n2, n3, far, out, out_half):
+    chip, core = where[0], where[1]
+    part, units = n0.shape[0], n0.shape[1] // 5
+    for k, near in enumerate((n0, n1, n2, n3)):
+        rows = rows_at(part * (chip ^ k), part, 16)
+        for piece, side in ((near[...], core), (far[part * k : part * (k + 1), :], 1 - core)):
+            full = piece.astype(F32)
+            for i in range(4):
+                at = rows_at(2 * units * i + units * side, units, 128)
+                out[rows, at] = full[:, units * i : units * (i + 1)]
+            out_half[rows, rows_at(units * side, units, 128)] = full[:, 4 * units :]
+
+
+def pack_gradients(
+    where, kept, given, from_attention, from_second, from_result, up_line, own, *refs
+):
+    out = refs[4]
+    chip = where[0]
+    half, width = out.shape[0] // 8, out.shape[1]
+    feat = width // 4
+    down = add_chips(own, *refs[:4])
+    for p in range(4):
+        cut = slice(feat * p, feat * (p + 1))
+        owner = jnp.where(chip == p, 1.0, 0.0)
+        lines = [
+            from_attention[0:1, cut],
+            from_attention[1:2, cut],
+            from_second[0:1, cut],
+            from_second[1:2, cut],
+            from_second[2:3, cut],
+            from_result[0:1, cut],
+            up_line[:, 2 * feat * p : 2 * feat * p + feat],
+            up_line[:, 2 * feat * p + feat : 2 * feat * (p + 1)],
+            from_attention[2:3, :feat] * owner,
+            from_attention[3:4, :feat] * owner,
+            from_result[1:2, :feat],
+            jnp.zeros((half - 11, feat), F32),
+        ]
+        small = jnp.concatenate(lines, axis=0).astype(BF16)
+        block = slice(half * p, half * (p + 1))
+        arrived = given[rows_at(4 * half * (1 - where[1]) + half * p, half, 32), :]
+        total = (kept[block, :] + arrived.astype(F32)).astype(BF16)
+        start = 2 * half * p
+        out[start : start + half, : 3 * feat] = total
+        out[start : start + half, 3 * feat :] = small
+        out[start + half : start + 2 * half, :] = down[p // 2][
+            half * (p % 2) : half * (p % 2 + 1), :
+        ].astype(BF16)
+
+
+def sum_planes(where, arrived, out):
+    both, width = out.shape
+    half, feat = both // 2, width // 4
+    total = arrived[:both, :].astype(F32)
+    for p in (1, 2, 3):
+        total = total + arrived[both * p : both * (p + 1), :].astype(F32)
+    out[half:, :] = total[half:, :].astype(BF16)
+    out[:half, : 3 * feat] = total[:half, : 3 * feat].astype(BF16)
+    small = total[:16, 3 * feat :]
+    total = jnp.sum(small[10:11, :3], axis=1, keepdims=True)
+    high = total.astype(BF16).astype(F32)
+    middle = (total - high).astype(BF16).astype(F32)
+    line = lax.broadcasted_iota(jnp.int32, small.shape, 0)
+    side = lax.broadcasted_iota(jnp.int32, small.shape, 1)
+    parts = jnp.where(side == 0, high, jnp.where(side == 1, middle, total - high - middle))
+    small = jnp.where((line == 10) & (side < 3), parts, small)
+    out[:16, 3 * feat :] = small.astype(BF16)
+    out[16:half, 3 * feat :] = jnp.zeros((half - 16, feat), BF16)
+
+
+def finish_projections(where, n0, n1, n2, n3, far, count, *outs):
+    query, key, value, loss = outs[:4]
+    flat, up_line, held, whole_line = outs[4:12], outs[12], outs[13], outs[14]
+    chip, core = where[0], where[1]
+    both, width = n0.shape
+    half, feat = both // 2, width // 4
+    near = (n0, n1, n2, n3)
+    for k, piece in enumerate(near):
+        held[2 * (chip ^ k) + core] = piece[:16, 3 * feat :].astype(F32)
+        held[2 * (chip ^ k) + 1 - core] = far[both * k : both * k + 16, 3 * feat :].astype(F32)
+    for j in range(4):
+
+        @pl.when(chip == j)
+        def _():
+            for k, piece in enumerate(near):
+                columns = slice(feat * (j ^ k), feat * ((j ^ k) + 1))
+                for i, out in enumerate((query, key, value)):
+                    cut = slice(feat * i, feat * (i + 1))
+                    out[rows_at(half * core, half, 32), columns] = piece[:half, cut].astype(F32)
+                    out[rows_at(half * (1 - core), half, 32), columns] = far[
+                        both * k : both * k + half, cut
+                    ].astype(F32)
+
+    total = held[0]
+    for i in range(1, 8):
+        total = total + held[i]
+    for i, line in enumerate((0, 1, 2, 3, 4, 5, 8, 9)):
+        flat[i][...] = total[line]
+    even = held[0] + held[2] + held[4] + held[6]
+    odd = held[1] + held[3] + held[5] + held[7]
+    for side, part in enumerate((even, odd)):
+        for i in range(2):
+            at = 2 * feat * side + feat * i
+            whole_line[0:1, at : at + feat] = part[6 + i : 7 + i, :]
+    up_line[...] = whole_line[0]
+    error = jnp.sum(total[10:11, :3], axis=1, keepdims=True)
+    loss[0, 0] = jnp.sum(error / (width * count[0:1, 0:1]))
+
+
+def layer(
+    tokens,
+    segment_ids,
+    valid_rows,
+    teacher,
+    cotangent,
+    first_gain,
+    first_shift,
+    query_weight,
+    query_bias,
+    key_weight,
+    value_weight,
+    value_bias,
+    output_weight,
+    output_bias,
+    second_gain,
+    second_shift,
+    up_weight,
+    up_bias,
+    down_weight,
+    down_bias,
+):
+    rows, width = tokens.shape[1], tokens.shape[2]
+    shard = query_weight.shape[0]
+    half, quarter = shard // 2, shard // 4
+    hidden = up_weight.shape[1]
+    units = hidden // 2
+    own_units = down_weight.shape[0]
+    core_units = own_units // 2
+    part_units = core_units // 4
+    feat = width // 4
+    heads = feat // HEAD_DIM
+    group = 4 * rows
+    every = 2 * group
+    steps = (1, 2, 3)
+
+    place, plane = lax.axis_index("ctx"), lax.axis_index("fsdp")
+    where = jnp.stack([place // 2, place % 2, plane]).astype(jnp.int32)
+    dma = pltpu.SemaphoreType.DMA
+
+    last = []
+
+    def step(body, outs, args, **options):
+        made = local_call(body, outs, where, args, after=tuple(last), **options)
+        last[:] = [min(jax.tree.leaves(made), key=lambda a: a.size * a.dtype.itemsize)]
+        return made
+
+    def stack(pieces, cost=0):
+        shape = len(pieces) * pieces[0].shape[0], pieces[0].shape[1]
+        return step(stack_rows, shaped(*shape), pieces, cost=cost)
+
+    own = tokens[0]
+    smalls = (
+        first_gain,
+        first_shift,
+        query_bias,
+        value_bias,
+        output_bias,
+        second_gain,
+        second_shift,
+        down_bias,
+    )
+    up_piece, down_piece = step(
+        pack_blocks,
+        (shaped(quarter, 5 * core_units), shaped(part_units, width)),
+        (up_weight, output_weight, down_weight),
+        far=range(3),
+        scratch=[dma((6,))],
+    )
+    up_far = [swap_planes(up_piece, s) for s in steps]
+    near_tokens = trade_chips(
+        step(pack_tokens, shaped(4 * (rows + 16), width), (own, segment_ids, valid_rows), cost=50)
+    )
+    projections = step(
+        pack_projections,
+        shaped(half, width),
+        (query_weight, key_weight, value_weight, *smalls, up_bias, valid_rows),
+        far=range(12),
+        scratch=[
+            pltpu.VMEM((3, half, width), BF16),
+            *[pltpu.VMEM((feat,), BF16)] * 8,
+            pltpu.VMEM((own_units,), BF16),
+            dma((12,)),
+        ],
+    )
+    near_weights = [projections] + [swap_planes(projections, s) for s in steps]
+    far_tokens = swap_cores(near_tokens)
+    up_far = stack(up_far, cost=50)
+    unit_one, key_row, query_column = step(
+        normalize_tokens,
+        (wide(every, width), wide(8, every), wide(group, 128)),
+        (near_tokens, far_tokens),
+        cost=50,
+    )
+    far_weights = swap_cores(stack(near_weights))
+
+    def all_chips(piece, cut):
+        from_x, from_y = swap_chips(piece, 1), swap_chips(piece, 2)
+        count, lanes = piece.shape
+        to_x, to_y = step(
+            cross_halves, (shaped(cut, lanes), shaped(count - cut, lanes)), (from_x, from_y), cost=50
+        )
+        return piece, from_x, from_y, swap_chips(to_x, 1), swap_chips(to_y, 2)
+
+    up_all = all_chips(up_far, up_far.shape[0] // 32 * 16 + 16)
+    down_far = [swap_planes(down_piece, s) for s in steps]
+
+    h_one, w_three, projected, probs, mixed, sent, vectors, b_up = step(
+        attend,
+        (
+            shaped(every, width),
+            shaped(width, 3 * feat),
+            shaped(every, 3 * feat),
+            shaped(heads, group, every),
+            wide(group, feat),
+            shaped(4 * (rows + 16), feat),
+            wide(8, width),
+            wide(1, units),
+        ),
+        (unit_one, key_row, query_column, *near_weights, far_weights),
+        scratch=[pltpu.VMEM((4, 16, feat), F32), pltpu.VMEM((group, every), F32)],
+        vmem=24,
+        cost=50,
+    )
+    mixed_low = trade_chips(sent)
+    down_far = stack(down_far)
+    out_near = step(build_half, shaped(width, core_units), (output_weight, *up_all))
+    out_far = swap_cores(out_near)
+    w_up = step(
+        build_up, shaped(width, units), (up_weight, *up_all), far=(0,), scratch=[dma((4,))], cost=50
+    )
+    w_output = step(build_output, shaped(width, width), (out_near, out_far))
+
+    second, h_two, count = step(
+        project_output,
+        (wide(rows, width), shaped(rows, width), wide(8, 128)),
+        (mixed_low, w_output, own, vectors),
+    )
+    h_pair = both_cores(h_two)
+    down_all = all_chips(down_far, down_far.shape[0] // 2)
+    act, slope = step(
+        activate,
+        (shaped(2 * rows, units), wide(2 * rows, units)),
+        (h_pair, w_up, b_up),
+    )
+    w_down = step(
+        build_down, shaped(units, width), (down_weight, *down_all), far=(0,), scratch=[dma]
+    )
+    down_near, down_other = step(
+        project_down, (wide(rows, width), shaped(rows, width)), (act, w_down)
+    )
+    layer_output, d_result, d_down, from_result = step(
+        compare,
+        (shaped(rows, width), wide(rows, width), shaped(rows, width), wide(8, width)),
+        (
+            second,
+            down_near,
+            both_cores(down_other),
+            vectors,
+            teacher[0],
+            cotangent[0],
+            valid_rows,
+            count,
+        ),
+    )
+    d_down = both_cores(d_down)
+
+    def five(count, lanes):
+        both = (shaped(4 * count, lanes),) * 2
+        return (wide(4 * count, lanes),) + both + (wide(2 * count, lanes),) * 2
+
+    def onward(parts, arrived):
+        count, lanes = parts[3].shape
+        to_x, to_y = step(pass_on, (shaped(count, lanes),) * 2, (*arrived, *parts[3:]), cost=50)
+        return (parts[0], *arrived, swap_chips(to_x, 1), swap_chips(to_y, 2))
+
+    down_parts = step(
+        down_grads,
+        five(part_units, width),
+        (act, d_down),
+        scratch=[pltpu.VMEM((units, width), F32)],
+        vmem=24,
+    )
+    down_arrived = swap_chips(down_parts[1], 1), swap_chips(down_parts[2], 2)
+    d_up, two_near, two_other, up_line = step(
+        activate_back,
+        (shaped(2 * rows, units), wide(rows, width), shaped(rows, width), wide(1, units)),
+        (d_down, w_down, slope, w_up),
+        cost=50,
+    )
+    d_second, d_attn, from_second, d_sent = step(
+        second_back,
+        (wide(rows, width), shaped(rows, width), wide(8, width), shaped(group, feat)),
+        (two_near, both_cores(two_other), d_result, second, vectors, w_output),
+    )
+    d_mixed = trade_chips(d_sent)
+
+    kept_out, given_out = step(
+        output_grads,
+        (wide(width, core_units), shaped(width, core_units)),
+        (mixed_low, d_attn),
+    )
+    given_out = swap_cores(given_out)
+    down_sums = onward(down_parts, down_arrived)
+    up_parts = step(
+        up_grads,
+        five(quarter, 5 * core_units),
+        (h_pair, d_up, kept_out, given_out),
+        scratch=[pltpu.VMEM((width, 5 * core_units), F32)],
+        vmem=24,
+    )
+    up_arrived = swap_chips(up_parts[1], 1), swap_chips(up_parts[2], 2)
+
+    d_three, kept, given, from_attention = step(
+        attend_back,
+        (
+            shaped(every, 3 * feat),
+            wide(4 * half, 3 * feat),
+            shaped(4 * half, 3 * feat),
+            wide(8, width),
+        ),
+        (d_mixed, probs, projected, mixed, h_one, w_three, vectors),
+        scratch=[pltpu.VMEM((group, every), BF16), pltpu.VMEM((width, 3 * feat), F32)],
+        vmem=24,
+        cost=50,
+    )
+    given = both_cores(given)
+    d_near, d_far = step(
+        inputs_back, (wide(group, width), shaped(group, width)), (d_three, w_three)
+    )
+    d_far = swap_cores(d_far)
+    arrived = trade_planes(
+        step(
+            pack_gradients,
+            shaped(8 * half, width),
+            (kept, given, from_attention, from_second, from_result, up_line, *down_sums),
+        )
+    )
+    up_sums = onward(up_parts, up_arrived)
+    shares = step(
+        share_inputs, (wide(rows, width),) + (shaped(rows, width),) * 3, (d_near, d_far)
+    )
+    shares = [shares[0]] + [swap_chips(shares[k], k) for k in steps]
+
+    def spread(piece):
+        return [piece] + [swap_chips(piece, k) for k in steps]
+
+    def whole(near):
+        return (*near, swap_cores(stack(near)))
+
+    up_planes = step(
+        send_planes,
+        (wide(quarter, 5 * core_units),) + (shaped(quarter, 5 * core_units),) * 3,
+        up_sums,
+        scratch=[pltpu.VMEM((4 * quarter, 5 * core_units), F32)],
+    )
+    up_planes = [up_planes[0]] + [swap_planes(up_planes[s], s) for s in steps]
+    grad_tokens = step(finish_inputs, shaped(rows, width), (*shares, own, d_second, vectors), cost=3)
+    both = spread(step(sum_planes, shaped(2 * half, width), (arrived,)))
+    up_near = spread(step(sum_pieces, shaped(quarter, 5 * core_units), up_planes))
+    both = whole(both)
+    finished = step(
+        finish_projections,
+        (wide(shard, width),) * 3
+        + (wide(1, 1),)
+        + (wide(shard),) * 8
+        + (wide(own_units),),
+        (*both, count),
+        scratch=[pltpu.VMEM((8, 16, feat), F32), pltpu.VMEM((8, own_units), F32)],
+        scalar=3,
+    )
+    grad_down_weight = step(finish_down, wide(own_units, width), both)
+    grad_up_weight, grad_output_weight = step(
+        finish_up, (wide(shard, hidden), wide(shard, width)), whole(up_near)
+    )
+    sums, two = finished[4:10], finished[10:12]
+    return (
+        layer_output[None],
+        finished[3].reshape(()),
+        grad_tokens[None],
+        sums[0],
+        sums[1],
+        finished[0],
+        two[0],
+        finished[1],
+        finished[2],
+        two[1],
+        grad_output_weight,
+        sums[2],
+        sums[3],
+        sums[4],
+        grad_up_weight,
+        finished[12],
+        grad_down_weight,
+        sums[5],
+    )
+
+
 def solution(mesh):
+    body = layer if (mesh.shape["ctx"], mesh.shape["fsdp"]) == (8, 4) else shards
     placed = (
         P("fsdp", "ctx", None),
         P("fsdp", "ctx"),
@@ -386,7 +1374,7 @@
         P("fsdp"),
     )
     return jax.shard_map(
-        shards,
+        body,
         mesh=mesh,
         in_specs=placed,
         out_specs=(

time: 1040 us -> 243 us (0.23)
  waiting for transfers between devices: 608 us -> 48.2 us
  blocking collectives: 244 us -> 11.6 us
  matrix products: 87 us -> 0 us
  Pallas kernels: 0 us -> 77.5 us
  starting transfers between devices: 0.9 us -> 74.3 us
  local copies, waits for them, and re-layouts: 58.1 us -> 28.2 us
  other arithmetic: 19.9 us -> 0.08 us
  between operations: 19.8 us -> 1.54 us
    reduce_scatter x6 -> x0, waiting for transfers between devices: 259 us -> none  [the longest x1 88 us: shards(): lax.psum_scatter(grad_down_weight.astype(jnp.bfloat16), 'fsdp', scatter_d...]
    all_gather x8 -> x0, waiting for transfers between devices: 253 us -> none  [the longest x1 84.9 us: shards(): lax.all_gather(down_weight, 'fsdp', axis=0, tiled=True)]
    psum x2 -> x0, blocking collectives: 184 us -> none  [the longest x1 145 us: shards(): lax.psum((shares[0], shares[1], shares[2], shares[3], shares[4], shares[5...]
    unnamed x18 -> x0, waiting for transfers between devices: 96.1 us -> none
    dot_general x32 -> x0, matrix products: 87 us -> none  [the longest x6 15.6 us: left_product(): jnp.einsum('rd,rf->df', left, right, preferred_element_type=jnp.float32)]
    pallas_call x0 -> x38, Pallas kernels: none -> 77.5 us  [local_call(): pl.pallas_call(kernel, out_shape=outs, in_specs=[pl.BlockSpec(memory_spac...]
    ppermute x0 -> x44, starting transfers between devices: none -> 56.6 us  [the longest x25 29.3 us: swap_chips(): return lax.ppermute(value, 'ctx', [(i, i ^ 2 * step) for i in range(size)])]
    unnamed x2 -> x0, blocking collectives: 38.4 us -> none
  transfers between devices with their start and end apart: 16 -> 48, of which waited for: 15 -> 17; matrix products, arithmetic and copies ran while one was open for 9% -> 0% of each run, Pallas kernels for 0% -> 26%
where the time goes in v1:
time: 243 us; the launch traced here: 241 us
  Pallas kernels  77.5 us (32%)
  starting transfers between devices  74.3 us (31%)
  waiting for transfers between devices  48.2 us (20%)
  local copies, waits for them, and re-layouts  28.2 us (12%)
  blocking collectives  11.6 us (5%)
    pallas_call x38, Pallas kernels, local_call(): pl.pallas_call(kernel, out_shape=outs, in_specs=[pl.BlockSpec(memory_spac...  77.5 us
    ppermute x25, starting transfers between devices, swap_chips(): return lax.ppermute(value, 'ctx', [(i, i ^ 2 * step) for i in range(size)])  29.3 us
    unnamed x150, local copies, waits for them, and re-layouts  28.2 us
    ppermute x12, starting transfers between devices, swap_planes(): return lax.ppermute(value, 'fsdp', [(i, i ^ step) for i in range(size)])  26.9 us
    ppermute x25, waiting for transfers between devices, swap_chips(): return lax.ppermute(value, 'ctx', [(i, i ^ 2 * step) for i in range(size)])  18.9 us
    ppermute x12, waiting for transfers between devices, swap_planes(): return lax.ppermute(value, 'fsdp', [(i, i ^ step) for i in range(size)])  16 us
    all_to_all x3, starting transfers between devices, trade_chips(): lax.all_to_all(value, 'ctx', 0, 0, axis_index_groups=groups, tiled=True)  13.3 us
    all_gather x5, blocking collectives, both_cores(): lax.all_gather(value, 'ctx', axis=0, tiled=True, axis_index_groups=pairs)  11.6 us
  transfers between devices with their start and end apart: 48, of which 17 were waited for; matrix products, arithmetic and copies ran while one was open for 0% of the time, Pallas kernels for 26%

profile of v1, /device:TPU:0, one launch (start us, length us, event | category | flops | bytes accessed | tf_op | source)
XLA Modules:
  0.0 241.5 jit_solution(8170766969720045266)
XLA Ops:
  6.9 5.3 %all-to-all-start = ((bf16[4,160,768]{2,1,0:T(8,128)(2,1)}), bf16[4,160,768]{2,1,0:T(8,128)(2,1)S(1)}, u32[]{:S(2)}, u32[]{:S(2)}) async-start(bf16[4,160,768]{2,1,0:T(8,128)(2,1)} %bitcast.4), calls=%async_computation | async-start | bytes 1966080 | tf_op jit(solution)/shard_map/all_to_all | solution.py:400
  12.2 3.6 %collective-permute-start.3 = (bf16[48,1920]{1,0:T(8,128)(2,1)S(1)}, bf16[48,1920]{1,0:T(8,128)(2,1)S(1)}, u32[]{:S(2)}, u32[]{:S(2)}) collective-permute-start(bf16[48,1920]{1,0:T(8,128)(2,1)S(1)} %get-tuple-element.100), channel_id=1, source_target_pairs={{0,3},{1,2},{2,1},{3,0},{4,7},{5,6},{6,5},{7,4},{8,11},{9,10},{10,... | collective-permute-start | bytes 552968 | tf_op jit(solution)/shard_map/ppermute | solution.py:394
  18.2 3.7 %collective-permute-start.6 = (bf16[96,768]{1,0:T(8,128)(2,1)S(1)}, bf16[96,768]{1,0:T(8,128)(2,1)S(1)}, u32[]{:S(2)}, u32[]{:S(2)}) collective-permute-start(bf16[96,768]{1,0:T(8,128)(2,1)S(1)} %shard_map.333.refs_3_.refs_0_), channel_id=1, source_target_pairs={{0,3},{1,2},{2,1},{3,0},{4,7},{5,6},{6,5},{7,4},{8,11},{9,10},{10,... | collective-permute-start | bytes 442376 | tf_op jit(solution)/shard_map/ppermute | solution.py:394
  21.9 8.2 %collective-permute-start.4 = (bf16[96,768]{1,0:T(8,128)(2,1)S(1)}, bf16[96,768]{1,0:T(8,128)(2,1)S(1)}, u32[]{:S(2)}, u32[]{:S(2)}) collective-permute-start(bf16[96,768]{1,0:T(8,128)(2,1)S(1)} %shard_map.333.refs_3_.refs_0_), channel_id=1, source_target_pairs={{0,1},{1,0},{2,3},{3,2},{4,5},{5,4},{6,7},{7,6},{8,9},{9,8},{10,11... | collective-permute-start | bytes 442376 | tf_op jit(solution)/shard_map/ppermute | solution.py:394
  30.1 8.5 %collective-permute-done.2.refs_1_ = bf16[48,1920]{1,0:T(8,128)(2,1)S(1)} collective-permute-done((bf16[48,1920]{1,0:T(8,128)(2,1)S(1)}, bf16[48,1920]{1,0:T(8,128)(2,1)S(1)}, u32[]{:S(2)}, u32[]{:S(2)}) %collective-permute-start.2) | collective-permute-done | bytes 184352 | tf_op jit(solution)/shard_map/ppermute | solution.py:394
  44.7 3.2 %collective-permute-start.14 = (bf16[96,768]{1,0:T(8,128)(2,1)S(1)}, bf16[96,768]{1,0:T(8,128)(2,1)S(1)}, u32[]{:S(2)}, u32[]{:S(2)}) collective-permute-start(bf16[96,768]{1,0:T(8,128)(2,1)S(1)} %copy-done.65), channel_id=1, source_target_pairs={{0,3},{1,2},{2,1},{3,0},{4,7},{5,6},{6,5},{7,4},{8,11},{9,10},{10,... | collective-permute-start | bytes 442376 | tf_op jit(solution)/shard_map/ppermute | solution.py:394
  49.7 4.5 %collective-permute-done.9.refs_1_.refs_3_ = bf16[144,1920]{1,0:T(8,128)(2,1)S(1)} collective-permute-done((bf16[144,1920]{1,0:T(8,128)(2,1)S(1)}, bf16[144,1920]{1,0:T(8,128)(2,1)S(1)}, u32[]{:S(2)}, u32[]{:S(2)}) %collective-permute-start.9) | collective-permute-done | bytes 552992 | tf_op jit(solution)/shard_map/ppermute | solution.py:389
  60.3 9.4 %shard_map.338 = (bf16[1152,768]{1,0:T(8,128)(2,1)S(1)}, bf16[768,576]{1,0:T(8,128)(2,1)S(1)}, bf16[1152,576]{1,0:T(8,128)(2,1)S(1)}, bf16[3,576,1152]{2,1,0:T(8...) custom-call(s32[3]{0:T(128)S(1)} %pad_add_fusion.where_ref, ...), custom_call_target="tpu_custom_call" | custom-call | flops 49999998976 | bytes 50000000 | tf_op jit(solution)/shard_map/pallas_call | solution.py:422
  77.8 4.3 %all-to-all-start.1 = ((bf16[4,160,192]{2,1,0:T(8,128)(2,1)}), bf16[4,160,192]{2,1,0:T(8,128)(2,1)}, u32[]{:S(2)}, u32[]{:S(2)}) async-start(bf16[4,160,192]{2,1,0:T(8,128)(2,1)} %bitcast.6), calls=%async_computation.1 | async-start | bytes 655360 | tf_op jit(solution)/shard_map/all_to_all | solution.py:400
  88.0 3.9 %all-to-all-done.1 = bf16[4,160,192]{2,1,0:T(8,128)(2,1)} async-done(((bf16[4,160,192]{2,1,0:T(8,128)(2,1)}), bf16[4,160,192]{2,1,0:T(8,128)(2,1)}, u32[]{:S(2)}, u32[]{:S(2)}) %all-to-all-start.1) | async-done | bytes 245792 | tf_op jit(solution)/shard_map/all_to_all | solution.py:400
  106.8 2.1 all_gather.16.refs_2_
  112.5 3.2 %shard_map.349 = (f32[384,768]{1,0:T(8,128)S(1)}, bf16[384,768]{1,0:T(8,128)(2,1)}, bf16[384,768]{1,0:T(8,128)(2,1)}, f32[192,768]{1,0:T(8,128)S(1)}, f32[192,768]{1,0:T(8,128)S(1)}) custom-call(s32[3]{0:T(128)S(1)} %pad_add_fusion.where_ref, bf16[288,1536]{1,0:T(8,128)(2,1)S(1)} %get-tuple-element.113.refs_6_.refs_0_, ...), custom_call_target="tpu_custom_call" | custom-call | tf_op jit(solution)/shard_map/pallas_call | solution.py:422
  117.7 3.9 %shard_map.350 = (bf16[288,1536]{1,0:T(8,128)(2,1)S(1)}, f32[144,768]{1,0:T(8,128)S(1)}, bf16[144,768]{1,0:T(8,128)(2,1)S(1)}, f32[1,1536]{1,0:T(1,128)S(1)}) custom-call(s32[3]{0:T(128)S(1)} %pad_add_fusion.where_ref, bf16[288,768]{1,0:T(8,128)(2,1)S(1)} %all_gather.17.refs_1_.refs_0_, bf16[1536,768]{1,0:T(8,128)(2,1)S(1)} %shard_map.346.refs_1_.refs_2_, ...), custom_call_target="tpu_custom_call" | custom-call | flops 49999998976 | bytes 50000000 | tf_op jit(solution)/shard_map/pallas_call | solution.py:422
  121.7 2.1 all_gather.18.refs_1_
  126.6 3.7 %all-to-all-start.2 = ((bf16[4,144,192]{2,1,0:T(8,128)(2,1)}), bf16[4,144,192]{2,1,0:T(8,128)(2,1)S(1)}, u32[]{:S(2)}, u32[]{:S(2)}) async-start(bf16[4,144,192]{2,1,0:T(8,128)(2,1)} %bitcast.11), calls=%async_computation.2 | async-start | bytes 589824 | tf_op jit(solution)/shard_map/all_to_all | solution.py:400
  132.2 2.2 shard_map.353
  137.6 3.4 %shard_map.354 = (f32[192,1920]{1,0:T(8,128)S(1)}, bf16[192,1920]{1,0:T(8,128)(2,1)}, bf16[192,1920]{1,0:T(8,128)(2,1)}, f32[96,1920]{1,0:T(8,128)S(1)}, f32[96,1920]{1,0:T(8,128)S(1)}) custom-call(s32[3]{0:T(128)S(1)} %pad_add_fusion.where_ref, bf16[288,768]{1,0:T(8,128)(2,1)S(1)} %copy-done.4, bf16[288,1536]{1,0:T(8,128)(2,1)S(1)} %copy-done.16, ...), custom_call_target="tpu_custom_call" | custom-call | tf_op jit(solution)/shard_map/pallas_call | solution.py:422
  144.9 2.1 copy-done.68
  149.6 8.7 %shard_map.355 = (bf16[1152,576]{1,0:T(8,128)(2,1)S(1)}, f32[384,576]{1,0:T(8,128)S(1)}, bf16[384,576]{1,0:T(8,128)(2,1)S(1)}, f32[8,768]{1,0:T(8,128)S(1)}) custom-call(s32[3]{0:T(128)S(1)} %pad_add_fusion.where_ref, bf16[576,192]{1,0:T(8,128)(2,1)S(1)} %bitcast.20, bf16[3,576,1152]{2,1,0:T(8,128)(2,1)S(1)} %copy-done.68, bf16[1152,576]{1,0:T(8,128)(2,1)S(1)} %copy-done.72, ...), custom_call_target="tpu_custom_call" | custom-call | flops 49999998976 | bytes 50000000 | tf_op jit(solution)/shard_map/pallas_call | solution.py:422
  158.4 3.0 %shard_map.356 = (f32[576,768]{1,0:T(8,128)S(1)}, bf16[576,768]{1,0:T(8,128)(2,1)}) custom-call(s32[3]{0:T(128)S(1)} %pad_add_fusion.where_ref, bf16[1152,576]{1,0:T(8,128)(2,1)S(1)} %get-tuple-element.147.refs_0_, bf16[768,576]{1,0:T(8,128)(2,1)S(1)} %copy-done.14, f32[8,768]{1,0:T(8,128)S(1)} %get-tuple-element.144.refs_2_), custom_call_target="tpu_custom_call" | custom-call | tf_op jit(solution)/shard_map/pallas_call | solution.py:422
  161.4 3.1 %all_gather.19.refs_1_ = bf16[768,576]{1,0:T(8,128)(2,1)S(1)} all-gather(bf16[384,576]{1,0:T(8,128)(2,1)S(1)} %get-tuple-element.143), channel_id=1, replica_groups={{0,4},{8,12},{16,20},{24,28},{1,5},{9,13},{17,21},{25,29},{2,6},{10,14}..., dimensions={0}, use_global_device_ids=true | all-gather | bytes 1327104 | tf_op jit(solution)/shard_map/all_gather | solution.py:384
  164.6 2.8 %shard_map.357.refs_4_ = bf16[768,768]{1,0:T(8,128)(2,1)} custom-call(s32[3]{0:T(128)S(1)} %pad_add_fusion.where_ref, f32[384,576]{1,0:T(8,128)S(1)} %get-tuple-element.142.refs_0_, bf16[768,576]{1,0:T(8,128)(2,1)S(1)} %all_gather.19.refs_1_, f32[8,768]{1,0:T(8,128)S(1)} %get-tuple-element.144.refs_2_, f32[8,768]{1,0:T(8,128)S(1)} %copy-done.40, ...), custom_call_target="tpu_custom_call" | custom-call | tf_op jit(solution)/shard_map/pallas_call | solution.py:422
  167.3 4.4 %all-to-all-start.3 = ((bf16[4,192,768]{2,1,0:T(8,128)(2,1)}), bf16[4,192,768]{2,1,0:T(8,128)(2,1)S(1)}, u32[]{:S(2)}, u32[]{:S(2)}) async-start(bf16[4,192,768]{2,1,0:T(8,128)(2,1)} %bitcast.13), calls=%async_computation.3 | async-start | bytes 2359296 | tf_op jit(solution)/shard_map/all_to_all | solution.py:404
  183.7 4.7 %collective-permute-done.32.refs_4_ = bf16[96,1920]{1,0:T(8,128)(2,1)S(1)} collective-permute-done((bf16[96,1920]{1,0:T(8,128)(2,1)S(1)}, bf16[96,1920]{1,0:T(8,128)(2,1)S(1)}, u32[]{:S(2)}, u32[]{:S(2)}) %collective-permute-start.32) | collective-permute-done | bytes 368672 | tf_op jit(solution)/shard_map/ppermute | solution.py:389
  190.6 4.6 %collective-permute-start.37 = (bf16[48,1920]{1,0:T(8,128)(2,1)S(1)}, bf16[48,1920]{1,0:T(8,128)(2,1)S(1)}, u32[]{:S(2)}, u32[]{:S(2)}) collective-permute-start(bf16[48,1920]{1,0:T(8,128)(2,1)S(1)} %get-tuple-element.163), channel_id=1, source_target_pairs={{0,2},{1,3},{2,0},{3,1},{4,6},{5,7},{6,4},{7,5},{8,10},{9,11},{10,... | collective-permute-start | bytes 552968 | tf_op jit(solution)/shard_map/ppermute | solution.py:394
  198.5 7.1 %all-to-all-done.3 = bf16[4,192,768]{2,1,0:T(8,128)(2,1)S(1)} async-done(((bf16[4,192,768]{2,1,0:T(8,128)(2,1)}), bf16[4,192,768]{2,1,0:T(8,128)(2,1)S(1)}, u32[]{:S(2)}, u32[]{:S(2)}) %all-to-all-start.3) | async-done | bytes 1179680 | tf_op jit(solution)/shard_map/all_to_all | solution.py:404
  207.4 2.6 %collective-permute-start.35 = (bf16[192,768]{1,0:T(8,128)(2,1)S(1)}, bf16[192,768]{1,0:T(8,128)(2,1)S(1)}, u32[]{:S(2)}, u32[]{:S(2)}) collective-permute-start(bf16[192,768]{1,0:T(8,128)(2,1)S(1)} %shard_map.362.refs_4_.refs_0_), channel_id=1, source_target_pairs={{0,24},{4,28},{8,16},{12,20},{16,8},{20,12},{24,0},{28,4},{1,25},{... | collective-permute-start | bytes 884744 | tf_op jit(solution)/shard_map/ppermute | solution.py:389
  212.5 6.1 %collective-permute-done.38.refs_3_ = bf16[48,1920]{1,0:T(8,128)(2,1)S(1)} collective-permute-done((bf16[48,1920]{1,0:T(8,128)(2,1)S(1)}, bf16[48,1920]{1,0:T(8,128)(2,1)S(1)}, u32[]{:S(2)}, u32[]{:S(2)}) %collective-permute-start.38) | collective-permute-done | bytes 184352 | tf_op jit(solution)/shard_map/ppermute | solution.py:394
  228.3 2.8 %shard_map.366.refs_4_ = f32[768,768]{1,0:T(8,128)} custom-call(s32[3]{0:T(128)S(1)} %pad_add_fusion.where_ref, bf16[192,768]{1,0:T(8,128)(2,1)S(1)} %shard_map.362.refs_4_.refs_0_, bf16[192,768]{1,0:T(8,128)(2,1)S(1)} %collective-permute-done.33.refs_1_, bf16[192,768]{1,0:T(8,128)(2,1)S(1)} %collective-permute-done.34.refs_2_, ...), custom_call_target="tpu_custom_call" | custom-call | tf_op jit(solution)/shard_map/pallas_call | solution.py:422
  231.1 3.5 %collective-permute-done.41.refs_2_ = bf16[48,1920]{1,0:T(8,128)(2,1)S(1)} collective-permute-done((bf16[48,1920]{1,0:T(8,128)(2,1)S(1)}, bf16[48,1920]{1,0:T(8,128)(2,1)S(1)}, u32[]{:S(2)}, u32[]{:S(2)}) %collective-permute-start.41) | collective-permute-done | bytes 184352 | tf_op jit(solution)/shard_map/ppermute | solution.py:389
  236.9 2.2 collective-permute-done.43.refs_4_
  239.1 2.4 shard_map.368
  (258 shorter events, 104.6 us)
Async XLA Ops:
  6.9 31.7 %all-to-all-start = ((bf16[4,160,768]{2,1,0:T(8,128)(2,1)}), bf16[4,160,768]{2,1,0:T(8,128)(2,1)S(1)}, u32[]{:S(2)}, u32[]{:S(2)}) async-start(bf16[4,160,768]{2,1,0:T(8,128)(2,1)} %bitcast.4), calls=%async_computation | async-start | bytes 1966080 | tf_op jit(solution)/shard_map/all_to_all | solution.py:400
  15.8 22.8 %collective-permute-start.2 = (bf16[48,1920]{1,0:T(8,128)(2,1)S(1)}, bf16[48,1920]{1,0:T(8,128)(2,1)S(1)}, u32[]{:S(2)}, u32[]{:S(2)}) collective-permute-start(bf16[48,1920]{1,0:T(8,128)(2,1)S(1)} %get-tuple-element.100), channel_id=1, source_target_pairs={{0,2},{1,3},{2,0},{3,1},{4,6},{5,7},{6,4},{7,5},{8,10},{9,11},{10,... | collective-permute-start | bytes 552968 | tf_op jit(solution)/shard_map/ppermute | solution.py:394
  15.8 22.8 %collective-permute-start.1 = (bf16[48,1920]{1,0:T(8,128)(2,1)S(1)}, bf16[48,1920]{1,0:T(8,128)(2,1)S(1)}, u32[]{:S(2)}, u32[]{:S(2)}) collective-permute-start(bf16[48,1920]{1,0:T(8,128)(2,1)S(1)} %get-tuple-element.100), channel_id=1, source_target_pairs={{0,1},{1,0},{2,3},{3,2},{4,5},{5,4},{6,7},{7,6},{8,9},{9,8},{10,11... | collective-permute-start | bytes 552968 | tf_op jit(solution)/shard_map/ppermute | solution.py:394
  18.2 26.5 %collective-permute-start.6 = (bf16[96,768]{1,0:T(8,128)(2,1)S(1)}, bf16[96,768]{1,0:T(8,128)(2,1)S(1)}, u32[]{:S(2)}, u32[]{:S(2)}) collective-permute-start(bf16[96,768]{1,0:T(8,128)(2,1)S(1)} %shard_map.333.refs_3_.refs_0_), channel_id=1, source_target_pairs={{0,3},{1,2},{2,1},{3,0},{4,7},{5,6},{6,5},{7,4},{8,11},{9,10},{10,... | collective-permute-start | bytes 442376 | tf_op jit(solution)/shard_map/ppermute | solution.py:394
  21.8 26.1 %collective-permute-start.5 = (bf16[96,768]{1,0:T(8,128)(2,1)S(1)}, bf16[96,768]{1,0:T(8,128)(2,1)S(1)}, u32[]{:S(2)}, u32[]{:S(2)}) collective-permute-start(bf16[96,768]{1,0:T(8,128)(2,1)S(1)} %shard_map.333.refs_3_.refs_0_), channel_id=1, source_target_pairs={{0,2},{1,3},{2,0},{3,1},{4,6},{5,7},{6,4},{7,5},{8,10},{9,11},{10,... | collective-permute-start | bytes 442376 | tf_op jit(solution)/shard_map/ppermute | solution.py:394
  21.9 26.1 %collective-permute-start.4 = (bf16[96,768]{1,0:T(8,128)(2,1)S(1)}, bf16[96,768]{1,0:T(8,128)(2,1)S(1)}, u32[]{:S(2)}, u32[]{:S(2)}) collective-permute-start(bf16[96,768]{1,0:T(8,128)(2,1)S(1)} %shard_map.333.refs_3_.refs_0_), channel_id=1, source_target_pairs={{0,1},{1,0},{2,3},{3,2},{4,5},{5,4},{6,7},{7,6},{8,9},{9,8},{10,11... | collective-permute-start | bytes 442376 | tf_op jit(solution)/shard_map/ppermute | solution.py:394
  39.2 15.0 %collective-permute-start.9 = (bf16[144,1920]{1,0:T(8,128)(2,1)S(1)}, bf16[144,1920]{1,0:T(8,128)(2,1)S(1)}, u32[]{:S(2)}, u32[]{:S(2)}) collective-permute-start(bf16[144,1920]{1,0:T(8,128)(2,1)S(1)} %shard_map.334.refs_2_.refs_1_), channel_id=1, source_target_pairs={{0,16},{4,20},{8,24},{12,28},{16,0},{20,4},{24,8},{28,12},{1,17},{... | collective-permute-start | bytes 1658888 | tf_op jit(solution)/shard_map/ppermute | solution.py:389
  41.2 14.6 %collective-permute-start.8 = (bf16[144,1920]{1,0:T(8,128)(2,1)S(1)}, bf16[144,1920]{1,0:T(8,128)(2,1)S(1)}, u32[]{:S(2)}, u32[]{:S(2)}) collective-permute-start(bf16[144,1920]{1,0:T(8,128)(2,1)S(1)} %shard_map.334.refs_2_.refs_1_), channel_id=1, source_target_pairs={{0,8},{4,12},{8,0},{12,4},{16,24},{20,28},{24,16},{28,20},{1,9},{5... | collective-permute-start | bytes 1658888 | tf_op jit(solution)/shard_map/ppermute | solution.py:389
  44.7 30.9 %collective-permute-start.14 = (bf16[96,768]{1,0:T(8,128)(2,1)S(1)}, bf16[96,768]{1,0:T(8,128)(2,1)S(1)}, u32[]{:S(2)}, u32[]{:S(2)}) collective-permute-start(bf16[96,768]{1,0:T(8,128)(2,1)S(1)} %copy-done.65), channel_id=1, source_target_pairs={{0,3},{1,2},{2,1},{3,0},{4,7},{5,6},{6,5},{7,4},{8,11},{9,10},{10,... | collective-permute-start | bytes 442376 | tf_op jit(solution)/shard_map/ppermute | solution.py:394
  47.9 27.6 %collective-permute-start.13 = (bf16[96,768]{1,0:T(8,128)(2,1)S(1)}, bf16[96,768]{1,0:T(8,128)(2,1)S(1)}, u32[]{:S(2)}, u32[]{:S(2)}) collective-permute-start(bf16[96,768]{1,0:T(8,128)(2,1)S(1)} %copy-done.65), channel_id=1, source_target_pairs={{0,2},{1,3},{2,0},{3,1},{4,6},{5,7},{6,4},{7,5},{8,10},{9,11},{10,... | collective-permute-start | bytes 442376 | tf_op jit(solution)/shard_map/ppermute | solution.py:394
  47.9 27.6 %collective-permute-start.12 = (bf16[96,768]{1,0:T(8,128)(2,1)S(1)}, bf16[96,768]{1,0:T(8,128)(2,1)S(1)}, u32[]{:S(2)}, u32[]{:S(2)}) collective-permute-start(bf16[96,768]{1,0:T(8,128)(2,1)S(1)} %copy-done.65), channel_id=1, source_target_pairs={{0,1},{1,0},{2,3},{3,2},{4,5},{5,4},{6,7},{7,6},{8,9},{9,8},{10,11... | collective-permute-start | bytes 442376 | tf_op jit(solution)/shard_map/ppermute | solution.py:394
  57.1 25.0 %collective-permute-start.11 = (bf16[64,1920]{1,0:T(8,128)(2,1)}, bf16[64,1920]{1,0:T(8,128)(2,1)S(1)}, u32[]{:S(2)}, u32[]{:S(2)}) collective-permute-start(bf16[64,1920]{1,0:T(8,128)(2,1)} %get-tuple-element.104.refs_8_), channel_id=1, source_target_pairs={{0,16},{4,20},{8,24},{12,28},{16,0},{20,4},{24,8},{28,12},{1,17},{... | collective-permute-start | bytes 737288 | tf_op jit(solution)/shard_map/ppermute | solution.py:389
  58.8 23.3 %collective-permute-start.10 = (bf16[80,1920]{1,0:T(8,128)(2,1)}, bf16[80,1920]{1,0:T(8,128)(2,1)S(1)}, u32[]{:S(2)}, u32[]{:S(2)}) collective-permute-start(bf16[80,1920]{1,0:T(8,128)(2,1)} %get-tuple-element.106), channel_id=1, source_target_pairs={{0,8},{4,12},{8,0},{12,4},{16,24},{20,28},{24,16},{28,20},{1,9},{5... | collective-permute-start | bytes 921608 | tf_op jit(solution)/shard_map/ppermute | solution.py:389
  76.9 18.2 %collective-permute-start.17 = (bf16[288,768]{1,0:T(8,128)(2,1)}, bf16[288,768]{1,0:T(8,128)(2,1)}, u32[]{:S(2)}, u32[]{:S(2)}) collective-permute-start(bf16[288,768]{1,0:T(8,128)(2,1)} %shard_map.339.refs_6_.refs_1_), channel_id=1, source_target_pairs={{0,16},{4,20},{8,24},{12,28},{16,0},{20,4},{24,8},{28,12},{1,17},{... | collective-permute-start | bytes 1327112 | tf_op jit(solution)/shard_map/ppermute | solution.py:389
  77.5 17.7 %collective-permute-start.16 = (bf16[288,768]{1,0:T(8,128)(2,1)}, bf16[288,768]{1,0:T(8,128)(2,1)}, u32[]{:S(2)}, u32[]{:S(2)}) collective-permute-start(bf16[288,768]{1,0:T(8,128)(2,1)} %shard_map.339.refs_6_.refs_1_), channel_id=1, source_target_pairs={{0,8},{4,12},{8,0},{12,4},{16,24},{20,28},{24,16},{28,20},{1,9},{5... | collective-permute-start | bytes 1327112 | tf_op jit(solution)/shard_map/ppermute | solution.py:389
  77.8 14.0 %all-to-all-start.1 = ((bf16[4,160,192]{2,1,0:T(8,128)(2,1)}), bf16[4,160,192]{2,1,0:T(8,128)(2,1)}, u32[]{:S(2)}, u32[]{:S(2)}) async-start(bf16[4,160,192]{2,1,0:T(8,128)(2,1)} %bitcast.6), calls=%async_computation.1 | async-start | bytes 655360 | tf_op jit(solution)/shard_map/all_to_all | solution.py:400
  115.7 16.4 %collective-permute-start.22 = (bf16[384,768]{1,0:T(8,128)(2,1)}, bf16[384,768]{1,0:T(8,128)(2,1)}, u32[]{:S(2)}, u32[]{:S(2)}) collective-permute-start(bf16[384,768]{1,0:T(8,128)(2,1)} %get-tuple-element.137), channel_id=1, source_target_pairs={{0,16},{4,20},{8,24},{12,28},{16,0},{20,4},{24,8},{28,12},{1,17},{... | collective-permute-start | bytes 1769480 | tf_op jit(solution)/shard_map/ppermute | solution.py:389
  116.3 15.8 %collective-permute-start.21 = (bf16[384,768]{1,0:T(8,128)(2,1)}, bf16[384,768]{1,0:T(8,128)(2,1)}, u32[]{:S(2)}, u32[]{:S(2)}) collective-permute-start(bf16[384,768]{1,0:T(8,128)(2,1)} %get-tuple-element.121.refs_4_), channel_id=1, source_target_pairs={{0,8},{4,12},{8,0},{12,4},{16,24},{20,28},{24,16},{28,20},{1,9},{5... | collective-permute-start | bytes 1769480 | tf_op jit(solution)/shard_map/ppermute | solution.py:389
  126.6 18.3 %all-to-all-start.2 = ((bf16[4,144,192]{2,1,0:T(8,128)(2,1)}), bf16[4,144,192]{2,1,0:T(8,128)(2,1)S(1)}, u32[]{:S(2)}, u32[]{:S(2)}) async-start(bf16[4,144,192]{2,1,0:T(8,128)(2,1)} %bitcast.11), calls=%async_computation.2 | async-start | bytes 589824 | tf_op jit(solution)/shard_map/all_to_all | solution.py:400
  134.4 30.1 %collective-permute-start.24 = (bf16[192,768]{1,0:T(8,128)(2,1)}, bf16[192,768]{1,0:T(8,128)(2,1)S(1)}, u32[]{:S(2)}, u32[]{:S(2)}) collective-permute-start(bf16[192,768]{1,0:T(8,128)(2,1)} %get-tuple-element.146), channel_id=1, source_target_pairs={{0,16},{4,20},{8,24},{12,28},{16,0},{20,4},{24,8},{28,12},{1,17},{... | collective-permute-start | bytes 884744 | tf_op jit(solution)/shard_map/ppermute | solution.py:389
  136.1 28.4 %collective-permute-start.23 = (bf16[192,768]{1,0:T(8,128)(2,1)}, bf16[192,768]{1,0:T(8,128)(2,1)S(1)}, u32[]{:S(2)}, u32[]{:S(2)}) collective-permute-start(bf16[192,768]{1,0:T(8,128)(2,1)} %get-tuple-element.140.refs_4_), channel_id=1, source_target_pairs={{0,8},{4,12},{8,0},{12,4},{16,24},{20,28},{24,16},{28,20},{1,9},{5... | collective-permute-start | bytes 884744 | tf_op jit(solution)/shard_map/ppermute | solution.py:389
  144.0 27.8 %collective-permute-start.27 = (bf16[192,1920]{1,0:T(8,128)(2,1)}, bf16[192,1920]{1,0:T(8,128)(2,1)}, u32[]{:S(2)}, u32[]{:S(2)}) collective-permute-start(bf16[192,1920]{1,0:T(8,128)(2,1)} %get-tuple-element.150), channel_id=1, source_target_pairs={{0,16},{4,20},{8,24},{12,28},{16,0},{20,4},{24,8},{28,12},{1,17},{... | collective-permute-start | bytes 2211848 | tf_op jit(solution)/shard_map/ppermute | solution.py:389
  144.5 27.3 %collective-permute-start.26 = (bf16[192,1920]{1,0:T(8,128)(2,1)}, bf16[192,1920]{1,0:T(8,128)(2,1)}, u32[]{:S(2)}, u32[]{:S(2)}) collective-permute-start(bf16[192,1920]{1,0:T(8,128)(2,1)} %get-tuple-element.141.refs_7_), channel_id=1, source_target_pairs={{0,8},{4,12},{8,0},{12,4},{16,24},{20,28},{24,16},{28,20},{1,9},{5... | collective-permute-start | bytes 2211848 | tf_op jit(solution)/shard_map/ppermute | solution.py:389
  161.4 17.3 %collective-permute-start.25 = (bf16[576,768]{1,0:T(8,128)(2,1)}, bf16[576,768]{1,0:T(8,128)(2,1)}, u32[]{:S(2)}, u32[]{:S(2)}) collective-permute-start(bf16[576,768]{1,0:T(8,128)(2,1)} %get-tuple-element.148.refs_11_), channel_id=1, source_target_pairs={{0,4},{4,0},{8,12},{12,8},{16,20},{20,16},{24,28},{28,24},{1,5},{5... | collective-permute-start | bytes 2654216 | tf_op jit(solution)/shard_map/ppermute | solution.py:379
  167.3 38.2 %all-to-all-start.3 = ((bf16[4,192,768]{2,1,0:T(8,128)(2,1)}), bf16[4,192,768]{2,1,0:T(8,128)(2,1)S(1)}, u32[]{:S(2)}, u32[]{:S(2)}) async-start(bf16[4,192,768]{2,1,0:T(8,128)(2,1)} %bitcast.13), calls=%async_computation.3 | async-start | bytes 2359296 | tf_op jit(solution)/shard_map/all_to_all | solution.py:404
  175.5 12.9 %collective-permute-start.32 = (bf16[96,1920]{1,0:T(8,128)(2,1)S(1)}, bf16[96,1920]{1,0:T(8,128)(2,1)S(1)}, u32[]{:S(2)}, u32[]{:S(2)}) collective-permute-start(bf16[96,1920]{1,0:T(8,128)(2,1)S(1)} %get-tuple-element.160), channel_id=1, source_target_pairs={{0,16},{4,20},{8,24},{12,28},{16,0},{20,4},{24,8},{28,12},{1,17},{... | collective-permute-start | bytes 1105928 | tf_op jit(solution)/shard_map/ppermute | solution.py:389
  180.1 15.2 %collective-permute-start.29 = (bf16[144,768]{1,0:T(8,128)(2,1)S(1)}, bf16[144,768]{1,0:T(8,128)(2,1)S(1)}, u32[]{:S(2)}, u32[]{:S(2)}) collective-permute-start(bf16[144,768]{1,0:T(8,128)(2,1)S(1)} %get-tuple-element.156), channel_id=1, source_target_pairs={{0,16},{4,20},{8,24},{12,28},{16,0},{20,4},{24,8},{28,12},{1,17},{... | collective-permute-start | bytes 663560 | tf_op jit(solution)/shard_map/ppermute | solution.py:389
  180.8 14.6 %collective-permute-start.30 = (bf16[144,768]{1,0:T(8,128)(2,1)S(1)}, bf16[144,768]{1,0:T(8,128)(2,1)S(1)}, u32[]{:S(2)}, u32[]{:S(2)}) collective-permute-start(bf16[144,768]{1,0:T(8,128)(2,1)S(1)} %get-tuple-element.157), channel_id=1, source_target_pairs={{0,24},{4,28},{8,16},{12,20},{16,8},{20,12},{24,0},{28,4},{1,25},{... | collective-permute-start | bytes 663560 | tf_op jit(solution)/shard_map/ppermute | solution.py:389
  182.3 14.6 %collective-permute-start.28 = (bf16[144,768]{1,0:T(8,128)(2,1)S(1)}, bf16[144,768]{1,0:T(8,128)(2,1)S(1)}, u32[]{:S(2)}, u32[]{:S(2)}) collective-permute-start(bf16[144,768]{1,0:T(8,128)(2,1)S(1)} %get-tuple-element.155.refs_5_), channel_id=1, source_target_pairs={{0,8},{4,12},{8,0},{12,4},{16,24},{20,28},{24,16},{28,20},{1,9},{5... | collective-permute-start | bytes 663560 | tf_op jit(solution)/shard_map/ppermute | solution.py:389
  190.6 21.9 %collective-permute-start.37 = (bf16[48,1920]{1,0:T(8,128)(2,1)S(1)}, bf16[48,1920]{1,0:T(8,128)(2,1)S(1)}, u32[]{:S(2)}, u32[]{:S(2)}) collective-permute-start(bf16[48,1920]{1,0:T(8,128)(2,1)S(1)} %get-tuple-element.163), channel_id=1, source_target_pairs={{0,2},{1,3},{2,0},{3,1},{4,6},{5,7},{6,4},{7,5},{8,10},{9,11},{10,... | collective-permute-start | bytes 552968 | tf_op jit(solution)/shard_map/ppermute | solution.py:394
  207.4 13.3 %collective-permute-start.35 = (bf16[192,768]{1,0:T(8,128)(2,1)S(1)}, bf16[192,768]{1,0:T(8,128)(2,1)S(1)}, u32[]{:S(2)}, u32[]{:S(2)}) collective-permute-start(bf16[192,768]{1,0:T(8,128)(2,1)S(1)} %shard_map.362.refs_4_.refs_0_), channel_id=1, source_target_pairs={{0,24},{4,28},{8,16},{12,20},{16,8},{20,12},{24,0},{28,4},{1,25},{... | collective-permute-start | bytes 884744 | tf_op jit(solution)/shard_map/ppermute | solution.py:389
  210.0 11.7 %collective-permute-start.34 = (bf16[192,768]{1,0:T(8,128)(2,1)S(1)}, bf16[192,768]{1,0:T(8,128)(2,1)S(1)}, u32[]{:S(2)}, u32[]{:S(2)}) collective-permute-start(bf16[192,768]{1,0:T(8,128)(2,1)S(1)} %shard_map.362.refs_4_.refs_0_), channel_id=1, source_target_pairs={{0,16},{4,20},{8,24},{12,28},{16,0},{20,4},{24,8},{28,12},{1,17},{... | collective-permute-start | bytes 884744 | tf_op jit(solution)/shard_map/ppermute | solution.py:389
  (91 other events, 561.8 us)

commit v2 on v1

--- a/solution.py
+++ b/solution.py
@@ -367,6 +367,7 @@
 F32 = jnp.float32
 BF16 = jnp.bfloat16
 ANY = pl.BlockSpec(memory_space=pl.ANY)
+HBM = pl.BlockSpec(memory_space=pltpu.HBM)
 VMEM = pl.BlockSpec(memory_space=pltpu.VMEM)
 SMEM = pl.BlockSpec(memory_space=pltpu.SMEM)
 NT = (((1,), (1,)), ((), ()))
@@ -412,26 +413,42 @@
     return jax.ShapeDtypeStruct(shape, F32)
 
 
-def local_call(body, outs, where, args, far=(), scratch=(), after=(), scalar=None, vmem=12, cost=0):
-    args, after, many = list(args), list(after), isinstance(outs, tuple)
-    count = len(args)
+def local_call(
+    body, outs, where, args, far=(), far_outs=(), scalar=None, scratch=(), after=(), vmem=12, cost=0
+):
+    args = [
+        pltpu.with_memory_space_constraint(a, pltpu.HBM) if i in far else a
+        for i, a in enumerate(args)
+    ]
+    after = list(after)
+    many = isinstance(outs, tuple)
+    outs = outs if many else (outs,)
+    count, made = len(args), len(outs)
 
     def kernel(where_ref, *refs):
-        body(where_ref, *refs[:count], *refs[count + len(after) :])
-
-    return pl.pallas_call(
+        token = refs[count + len(after) + made]
+        token[...] = jnp.zeros(token.shape, token.dtype)
+        start = count + len(after)
+        body(where_ref, *refs[:count], *refs[start : start + made], *refs[start + made + 1 :])
+
+    def place(i):
+        return HBM if i in far_outs else SMEM if i == scalar else VMEM
+
+    results = pl.pallas_call(
         kernel,
-        out_shape=outs,
-        in_specs=[pl.BlockSpec(memory_space=pltpu.SMEM)]
-        + [ANY if i in far else VMEM for i in range(count)]
-        + [ANY] * len(after),
-        out_specs=tuple(SMEM if i == scalar else VMEM for i in range(len(outs))) if many else VMEM,
+        out_shape=(
+            *(pltpu.HBM(o.shape, o.dtype) if i in far_outs else o for i, o in enumerate(outs)),
+            wide(8, 128),
+        ),
+        in_specs=[SMEM] + [HBM if i in far else VMEM for i in range(count)] + [ANY] * len(after),
+        out_specs=(*(place(i) for i in range(made)), VMEM),
         scratch_shapes=scratch,
         compiler_params=pltpu.CompilerParams(vmem_limit_bytes=vmem << 20),
         cost_estimate=pl.CostEstimate(
             flops=cost * 10**9, transcendentals=0, bytes_accessed=cost * 10**6
         ),
     )(where, *args, *after)
+    return (results[:-1] if many else results[0]), results[-1]
 
 
 def core_rows(core, count):
@@ -482,12 +499,21 @@
         ids >> 7,
         jnp.where(line == 1, ids & 127, jnp.where(line == 2, valid[...], 0)),
     )
-    codes = codes.astype(F32).astype(out.dtype)
-    for i in range(4):
-        start = (rows + 16) * i
-        out[start : start + rows, :] = tokens[...]
-        out[start + rows : start + rows + 16, :] = jnp.zeros((16, width), out.dtype)
-        out[start + rows : start + rows + 16, :rows] = codes
+    out[:rows, :] = tokens[...]
+    out[rows:, :] = jnp.zeros((16, width), out.dtype)
+    out[rows:, :rows] = codes.astype(F32).astype(out.dtype)
+
+
+def order_chips(where, p0, p1, p2, p3, out):
+    rows = p0.shape[0]
+    for k, piece in enumerate((p0, p1, p2, p3)):
+        out[rows_at(rows * (where[0] ^ k), rows, 16), :] = piece[...]
+
+
+def far_planes(where, arrived, out):
+    part = arrived.shape[0] // 4
+    for s in (1, 2, 3):
+        out[part * (s - 1) : part * s, :] = arrived[rows_at(part * (where[2] ^ s), part, 16), :]
 
 
 def pack_projections(where, *refs):
@@ -518,20 +544,25 @@
 
 def pack_blocks(where, up, output, down, out_up, out_down, sems):
     chip, core = where[0], where[1]
-    part, units = out_up.shape[0], out_up.shape[1] // 5
+    part, units = out_up.shape[0] // 4, out_up.shape[1] // 5
     rows = rows_at(part * chip, part, 16)
     down_part = out_down.shape[0]
-    copies = [
-        (
-            up.at[rows, rows_at(2 * units * i + units * core, units, 128)],
-            out_up.at[:, units * i : units * (i + 1)],
+    copies = []
+    for p in range(4):
+        block = slice(part * p, part * (p + 1))
+        copies += [
+            (
+                up.at[rows, rows_at(2 * units * i + units * core, units, 128)],
+                out_up.at[block, units * i : units * (i + 1)],
+            )
+            for i in range(4)
+        ]
+        copies.append(
+            (output.at[rows, rows_at(units * core, units, 128)], out_up.at[block, 4 * units :])
         )
-        for i in range(4)
-    ]
-    copies += [
-        (output.at[rows, rows_at(units * core, units, 128)], out_up.at[:, 4 * units :]),
-        (down.at[rows_at(4 * down_part * core + down_part * chip, down_part, 32)], out_down),
-    ]
+    copies.append(
+        (down.at[rows_at(4 * down_part * core + down_part * chip, down_part, 32)], out_down)
+    )
     run_copies(copies, sems)
 
 
@@ -583,14 +614,20 @@
         copy.wait()
 
 
-def build_half(where, output, p0, p1, p2, p3, p4, out):
+def build_half(where, output, p0, p1, p2, p3, p4, out, sem):
     chip, core, plane = where[0], where[1], where[2]
     shard, units = output.shape[0], out.shape[1]
     part = shard // 4
-    out[rows_at(shard * plane, shard, 64), :] = output[:, rows_at(units * core, units, 128)]
+    own = pltpu.make_async_copy(
+        output.at[:, rows_at(units * core, units, 128)],
+        out.at[rows_at(shard * plane, shard, 64)],
+        sem,
+    )
+    own.start()
     for k, s, offset, count, piece, start in three_blocks((p0, p1, p2, p3, p4), part):
         at = rows_at(shard * (plane ^ s) + part * (chip ^ k) + offset, count, 16)
         out[at, :] = piece[start : start + count, 4 * units :]
+    own.wait()
 
 
 def build_down(where, down, p0, p1, p2, p3, p4, out, sem):
@@ -630,8 +667,13 @@
 
 def attend(where, *refs):
     units, key_row, query_column, weights, far_weights = refs[:3] + (refs[3:7], refs[7])
-    h_one, w_three, projected, probs, mixed, sent, vectors, long = refs[8:16]
-    small, bias = refs[16:]
+    saved, sent, vectors, long = refs[8:13], refs[13], refs[14], refs[15]
+    small, bias, h_one, w_three, projected, probs, mixed, sems = refs[16:]
+    kept = (h_one, w_three, projected, mixed)
+    copies = [
+        pltpu.make_async_copy(source, saved[i], sems.at[j])
+        for j, (i, source) in enumerate(zip((0, 1, 2, 4), kept))
+    ]
     core, plane = where[1], where[2]
     half, width = weights[0].shape
     feat = width // 4
@@ -657,7 +699,9 @@
         long[:, 2 * feat * p + feat : 2 * feat * (p + 1)] = pair[1:, :]
     gain, shift = vectors[0:1, :], vectors[1:2, :]
     short = small[where[0]]
+    copies[1].start()
     h_one[...] = (units[...] * gain + shift).astype(BF16)
+    copies[0].start()
     values = dot(h_one[...], w_three[...], NN)
     query = (values[:group, :feat] + short[2:3, :]).astype(BF16) * jnp.asarray(
         HEAD_DIM**-0.5, BF16
@@ -666,6 +710,7 @@
     projected[group:, :feat] = jnp.zeros((group, feat), BF16)
     projected[:, feat : 2 * feat] = values[:, feat : 2 * feat].astype(BF16)
     projected[:, 2 * feat :] = (values[:, 2 * feat :] + short[3:4, :]).astype(BF16)
+    copies[2].start()
     column = lax.broadcasted_iota(jnp.int32, (rows, 2 * group), 1)
     line = lax.broadcasted_iota(jnp.int32, (rows, 2 * group), 0)
     for k in range(4):
@@ -686,16 +731,30 @@
             result = dot(low, held, NN)
             mixed[block, at] = result
             sent[(rows + 16) * k : (rows + 16) * k + rows, at] = result.astype(BF16)
+        copies.append(pltpu.make_async_copy(probs.at[h], saved[3].at[h], sems.at[4 + h]))
+        copies[-1].start()
+    copies[3].start()
     high = jnp.floor(count / 128.0)
     side = lax.broadcasted_iota(jnp.int32, (16, feat), 1)
     digits = jnp.where(side == 0, high, jnp.where(side == 1, count - 128.0 * high, 0.0))
     for k in range(4):
         sent[(rows + 16) * k + rows : (rows + 16) * (k + 1), :] = digits.astype(BF16)
-
-
-def attend_back(where, d_all, probs, projected, mixed, h_one, w_three, vectors, *outs):
-    d_three, kept, given, lines, d_scores, grads = outs
+    for copy in copies:
+        copy.wait()
+
+
+def attend_back(where, d_all, vectors, *refs):
+    saved, (near, far, kept, given, lines) = refs[:5], refs[5:10]
+    d_three, d_scores, grads, h_one, w_three, projected, probs, mixed, sems = refs[10:]
     core = where[1]
+    pairs = [(saved[2], projected), (saved[4], mixed)]
+    pairs += [(saved[3].at[h], probs.at[h]) for h in range(probs.shape[0])]
+    pairs += [(saved[0], h_one), (saved[1], w_three)]
+    copies = [pltpu.make_async_copy(a, b, sems.at[i]) for i, (a, b) in enumerate(pairs)]
+    for copy in copies:
+        copy.start()
+    copies[0].wait()
+    copies[1].wait()
     group, feat = d_all.shape
     rows, width = group // 4, h_one.shape[1]
     scale = HEAD_DIM**-0.5
@@ -705,6 +764,7 @@
         key_at = slice(feat + HEAD_DIM * h, feat + HEAD_DIM * (h + 1))
         value_at = slice(2 * feat + HEAD_DIM * h, 2 * feat + HEAD_DIM * (h + 1))
         keys, held = projected[:, key_at], projected[:, value_at]
+        copies[2 + h].wait()
         for k in range(4):
             block = slice(rows * k, rows * (k + 1))
             d_mixed = d_all[block, at]
@@ -715,11 +775,15 @@
             d_three[block, at] = (dot(low, keys, NN) * scale).astype(BF16)
         d_three[:, key_at] = dot(d_scores[...], projected[:group, at], TN).astype(BF16)
         d_three[:, value_at] = dot(probs[h], d_all[:, at], TN).astype(BF16)
+    for copy in copies[2 + probs.shape[0] :]:
+        copy.wait()
     grads[...] = dot(h_one[...], d_three[...], TN)
+    near[...] = dot(d_three[:group, :], w_three[...], NT).astype(BF16)
+    far[...] = dot(d_three[group:, :], w_three[...], NT).astype(BF16)
     half = kept.shape[0] // 4
     for p in range(4):
         block = slice(half * p, half * (p + 1))
-        kept[block, :] = grads[rows_at(2 * half * p + half * core, half, 32), :]
+        kept[block, :] = grads[rows_at(2 * half * p + half * core, half, 32), :].astype(BF16)
         given[block, :] = grads[rows_at(2 * half * p + half * (1 - core), half, 32), :].astype(BF16)
     sums = jnp.sum(d_three[...].astype(F32), axis=0, keepdims=True)
     weight = w_three[...].astype(F32)
@@ -737,21 +801,15 @@
     lines[4:, :] = jnp.zeros((4, width), F32)
 
 
-def inputs_back(where, d_three, w_three, near, far):
-    group = near.shape[0]
-    near[...] = dot(d_three[:group, :], w_three[...], NT)
-    far[...] = dot(d_three[group:, :], w_three[...], NT).astype(BF16)
-
-
 def share_inputs(where, near, far, *outs):
     rows = outs[0].shape[0]
     for k, out in enumerate(outs):
         at = rows_at(rows * (where[0] ^ k), rows, 16)
-        out[...] = (near[at, :] + far[at, :].astype(F32)).astype(out.dtype)
+        out[...] = (near[at, :].astype(F32) + far[at, :].astype(F32)).astype(out.dtype)
 
 
 def finish_inputs(where, d0, d1, d2, d3, tokens, d_second, vectors, out):
-    total = d0[...]
+    total = d0[...].astype(F32)
     for piece in (d1, d2, d3):
         total = total + piece[...].astype(F32)
     unit, inverse = unit_rows(tokens[...].astype(F32))
@@ -852,43 +910,30 @@
         sent[rows * k : rows * (k + 1), :] = dot(low, part, NT).astype(BF16)
 
 
-def output_grads(where, mixed, d_attn, kept, given):
-    core = where[1]
-    rows, width = d_attn.shape
-    feat, units = mixed.shape[1], width // 2
-    mine = d_attn[:, rows_at(units * core, units, 128)]
-    others = d_attn[:, rows_at(units * (1 - core), units, 128)]
-    for k in range(4):
-        at = slice(feat * k, feat * (k + 1))
-        piece = mixed[(rows + 16) * k : (rows + 16) * k + rows, :]
-        kept[at, :] = dot(piece, mine, TN)
-        given[at, :] = dot(piece, others, TN).astype(BF16)
-
-
 def split_chips(chip, block, outs, count):
     own, to_x, to_y, then_x, then_y = outs
     for p in range(4):
-        own[count * p : count * (p + 1), :] = block(chip, p)
+        own[count * p : count * (p + 1), :] = block(chip, p).astype(BF16)
     for p in (0, 1):
         low, high = slice(count * p, count * (p + 1)), slice(count * (p + 2), count * (p + 3))
         to_x[low, :] = block(chip ^ 1, p).astype(BF16)
         to_x[high, :] = block(chip ^ 3, p).astype(BF16)
         to_y[low, :] = block(chip ^ 2, p + 2).astype(BF16)
         to_y[high, :] = block(chip ^ 3, p + 2).astype(BF16)
-        then_x[low, :] = block(chip ^ 1, p + 2)
-        then_y[low, :] = block(chip ^ 2, p)
+        then_x[low, :] = block(chip ^ 1, p + 2).astype(BF16)
+        then_y[low, :] = block(chip ^ 2, p).astype(BF16)
 
 
 def pass_on(where, from_x, from_y, then_x, then_y, to_x, to_y):
     half = to_x.shape[0]
-    to_x[...] = (then_x[...] + from_y[half:, :].astype(F32)).astype(BF16)
-    to_y[...] = (then_y[...] + from_x[half:, :].astype(F32)).astype(BF16)
+    to_x[...] = (then_x[...].astype(F32) + from_y[half:, :].astype(F32)).astype(BF16)
+    to_y[...] = (then_y[...].astype(F32) + from_x[half:, :].astype(F32)).astype(BF16)
 
 
 def add_chips(own, from_x, from_y, last_x, last_y):
     half = last_x.shape[0]
-    low = own[:half, :] + from_x[:half, :].astype(F32) + last_y[...].astype(F32)
-    high = own[half:, :] + from_y[:half, :].astype(F32) + last_x[...].astype(F32)
+    low = own[:half, :].astype(F32) + from_x[:half, :].astype(F32) + last_y[...].astype(F32)
+    high = own[half:, :].astype(F32) + from_y[:half, :].astype(F32) + last_x[...].astype(F32)
     return low, high
 
 
@@ -903,11 +948,19 @@
     split_chips(where[0], block, outs, count)
 
 
-def up_grads(where, h_pair, d_up, kept, given, *refs):
+def up_grads(where, h_pair, d_up, mixed, d_attn, *refs):
     outs, total = refs[:5], refs[5]
     count, units = outs[0].shape[0] // 4, d_up.shape[1]
     total[:, :units] = dot(h_pair[...], d_up[...], TN)
-    total[:, units:] = kept[...] + given[...].astype(F32)
+    rows, width = d_attn.shape[0] // 2, d_attn.shape[1]
+    feat = mixed.shape[1]
+    columns = d_attn[:, rows_at(width // 2 * where[1], width // 2, 128)]
+    for j in range(4):
+        product = 0.0
+        for i in range(2):
+            start = 4 * (rows + 16) * i + (rows + 16) * j
+            product += dot(mixed[start : start + rows, :], columns[rows * i : rows * (i + 1), :], TN)
+        total[feat * j : feat * (j + 1), units:] = product
 
     def block(j, p):
         return total[rows_at(4 * count * p + count * j, count, 16), :]
@@ -930,39 +983,60 @@
     out[...] = total.astype(out.dtype)
 
 
-def finish_down(where, n0, n1, n2, n3, far, out):
-    chip, core = where[0], where[1]
-    both = n0.shape[0]
+def finish_down(where, near, far, out, held, sems):
+    core = where[1]
+    both = near.shape[0] // 4
     part = both // 2
-    for k, piece in enumerate((n0, n1, n2, n3)):
-        at = part * (chip ^ k)
-        out[rows_at(4 * part * core + at, part, 32), :] = piece[part:, :].astype(F32)
-        out[rows_at(4 * part * (1 - core) + at, part, 32), :] = far[
-            both * k + part : both * (k + 1), :
-        ].astype(F32)
-
-
-def finish_up(where, n0, n1, n2, n3, far, out, out_half):
+    copies = []
+    for j in range(4):
+        block = slice(both * j + part, both * (j + 1))
+        for side, piece in ((core, near), (1 - core, far)):
+            at = rows_at(4 * part * side + part * j, part, 32)
+            held[at, :] = piece[block, :].astype(F32)
+            copies.append(pltpu.make_async_copy(held.at[at], out.at[at], sems.at[len(copies)]))
+            copies[-1].start()
+    for copy in copies:
+        copy.wait()
+
+
+def finish_up(where, n0, n1, n2, n3, far, out, out_half, held, held_half, sems):
     chip, core = where[0], where[1]
     part, units = n0.shape[0], n0.shape[1] // 5
+    copies = []
     for k, near in enumerate((n0, n1, n2, n3)):
         rows = rows_at(part * (chip ^ k), part, 16)
         for piece, side in ((near[...], core), (far[part * k : part * (k + 1), :], 1 - core)):
             full = piece.astype(F32)
             for i in range(4):
                 at = rows_at(2 * units * i + units * side, units, 128)
-                out[rows, at] = full[:, units * i : units * (i + 1)]
-            out_half[rows, rows_at(units * side, units, 128)] = full[:, 4 * units :]
+                held[rows, at] = full[:, units * i : units * (i + 1)]
+            held_half[rows, rows_at(units * side, units, 128)] = full[:, 4 * units :]
+        for source, target in ((held, out), (held_half, out_half)):
+            copies.append(
+                pltpu.make_async_copy(source.at[rows], target.at[rows], sems.at[len(copies)])
+            )
+            copies[-1].start()
+    for copy in copies:
+        copy.wait()
+
+
+def sum_chips(where, own, from_x, from_y, last_x, last_y, out):
+    half = last_x.shape[0]
+    low, high = add_chips(own, from_x, from_y, last_x, last_y)
+    out[:half, :], out[half:, :] = low.astype(BF16), high.astype(BF16)
 
 
 def pack_gradients(
-    where, kept, given, from_attention, from_second, from_result, up_line, own, *refs
+    where, kept, given, from_attention, from_second, from_result, up_line, down, out, down_sum
 ):
-    out = refs[4]
     chip = where[0]
-    half, width = out.shape[0] // 8, out.shape[1]
+    part = down_sum.shape[0]
+    arrived_down = down[:part, :].astype(F32)
+    for p in (1, 2, 3):
+        arrived_down = arrived_down + down[part * p : part * (p + 1), :].astype(F32)
+    down_sum[...] = arrived_down.astype(BF16)
+    half, width = out.shape[0] // 4, out.shape[1]
     feat = width // 4
-    down = add_chips(own, *refs[:4])
     for p in range(4):
         cut = slice(feat * p, feat * (p + 1))
         owner = jnp.where(chip == p, 1.0, 0.0)
@@ -983,58 +1057,48 @@
         small = jnp.concatenate(lines, axis=0).astype(BF16)
         block = slice(half * p, half * (p + 1))
         arrived = given[rows_at(4 * half * (1 - where[1]) + half * p, half, 32), :]
-        total = (kept[block, :] + arrived.astype(F32)).astype(BF16)
-        start = 2 * half * p
-        out[start : start + half, : 3 * feat] = total
-        out[start : start + half, 3 * feat :] = small
-        out[start + half : start + 2 * half, :] = down[p // 2][
-            half * (p % 2) : half * (p % 2 + 1), :
-        ].astype(BF16)
-
-
-def sum_planes(where, arrived, out):
-    both, width = out.shape
+        total = (kept[block, :].astype(F32) + arrived.astype(F32)).astype(BF16)
+        out[block, : 3 * feat] = total
+        out[block, 3 * feat :] = small
+
+
+def sum_planes(where, arrived, down, out):
+    both, width = out.shape[0] // 4, out.shape[1]
     half, feat = both // 2, width // 4
-    total = arrived[:both, :].astype(F32)
+    total = arrived[:half, :].astype(F32)
     for p in (1, 2, 3):
-        total = total + arrived[both * p : both * (p + 1), :].astype(F32)
-    out[half:, :] = total[half:, :].astype(BF16)
-    out[:half, : 3 * feat] = total[:half, : 3 * feat].astype(BF16)
+        total = total + arrived[half * p : half * (p + 1), :].astype(F32)
     small = total[:16, 3 * feat :]
-    total = jnp.sum(small[10:11, :3], axis=1, keepdims=True)
-    high = total.astype(BF16).astype(F32)
-    middle = (total - high).astype(BF16).astype(F32)
+    error = jnp.sum(small[10:11, :3], axis=1, keepdims=True)
+    high = error.astype(BF16).astype(F32)
+    middle = (error - high).astype(BF16).astype(F32)
     line = lax.broadcasted_iota(jnp.int32, small.shape, 0)
     side = lax.broadcasted_iota(jnp.int32, small.shape, 1)
-    parts = jnp.where(side == 0, high, jnp.where(side == 1, middle, total - high - middle))
+    parts = jnp.where(side == 0, high, jnp.where(side == 1, middle, error - high - middle))
     small = jnp.where((line == 10) & (side < 3), parts, small)
-    out[:16, 3 * feat :] = small.astype(BF16)
-    out[16:half, 3 * feat :] = jnp.zeros((half - 16, feat), BF16)
-
-
-def finish_projections(where, n0, n1, n2, n3, far, count, *outs):
+    for j in range(4):
+        start = both * j
+        out[start : start + half, : 3 * feat] = total[:, : 3 * feat].astype(BF16)
+        out[start : start + 16, 3 * feat :] = small.astype(BF16)
+        out[start + 16 : start + half, 3 * feat :] = jnp.zeros((half - 16, feat), BF16)
+        out[start + half : start + both, :] = down[...]
+
+
+def finish_projections(where, near, far, count, *outs):
     query, key, value, loss = outs[:4]
     flat, up_line, held, whole_line = outs[4:12], outs[12], outs[13], outs[14]
-    chip, core = where[0], where[1]
-    both, width = n0.shape
+    core = where[1]
+    both, width = near.shape[0] // 4, near.shape[1]
     half, feat = both // 2, width // 4
-    near = (n0, n1, n2, n3)
-    for k, piece in enumerate(near):
-        held[2 * (chip ^ k) + core] = piece[:16, 3 * feat :].astype(F32)
-        held[2 * (chip ^ k) + 1 - core] = far[both * k : both * k + 16, 3 * feat :].astype(F32)
     for j in range(4):
-
-        @pl.when(chip == j)
-        def _():
-            for k, piece in enumerate(near):
-                columns = slice(feat * (j ^ k), feat * ((j ^ k) + 1))
-                for i, out in enumerate((query, key, value)):
-                    cut = slice(feat * i, feat * (i + 1))
-                    out[rows_at(half * core, half, 32), columns] = piece[:half, cut].astype(F32)
-                    out[rows_at(half * (1 - core), half, 32), columns] = far[
-                        both * k : both * k + half, cut
-                    ].astype(F32)
-
+        start = both * j
+        for side, piece in ((core, near), (1 - core, far)):
+            held[2 * j + side] = piece[start : start + 16, 3 * feat :].astype(F32)
+            rows = rows_at(half * side, half, 32)
+            for i, out in enumerate((query, key, value)):
+                out[rows, feat * j : feat * (j + 1)] = piece[
+                    start : start + half, feat * i : feat * (i + 1)
+                ].astype(F32)
     total = held[0]
     for i in range(1, 8):
         total = total + held[i]
@@ -1094,8 +1158,8 @@
     last = []
 
     def step(body, outs, args, **options):
-        made = local_call(body, outs, where, args, after=tuple(last), **options)
-        last[:] = [min(jax.tree.leaves(made), key=lambda a: a.size * a.dtype.itemsize)]
+        made, token = local_call(body, outs, where, args, after=last, **options)
+        last[:] = [token]
         return made
 
     def stack(pieces, cost=0):
@@ -1115,15 +1179,14 @@
     )
     up_piece, down_piece = step(
         pack_blocks,
-        (shaped(quarter, 5 * core_units), shaped(part_units, width)),
+        (shaped(4 * quarter, 5 * core_units), shaped(part_units, width)),
         (up_weight, output_weight, down_weight),
         far=range(3),
-        scratch=[dma((6,))],
-    )
-    up_far = [swap_planes(up_piece, s) for s in steps]
-    near_tokens = trade_chips(
-        step(pack_tokens, shaped(4 * (rows + 16), width), (own, segment_ids, valid_rows), cost=50)
-    )
+        scratch=[dma((21,))],
+    )
+    up_far = trade_planes(up_piece)
+    bundle = step(pack_tokens, shaped(rows + 16, width), (own, segment_ids, valid_rows), cost=50)
+    near_tokens = [bundle] + [swap_chips(bundle, k) for k in steps]
     projections = step(
         pack_projections,
         shaped(half, width),
@@ -1135,27 +1198,30 @@
             pltpu.VMEM((own_units,), BF16),
             dma((12,)),
         ],
-    )
+        cost=0,
+    )
+    near_tokens = step(order_chips, shaped(4 * (rows + 16), width), near_tokens, cost=0)
+    far_tokens = swap_cores(near_tokens)
+    up_far = step(far_planes, shaped(3 * quarter, 5 * core_units), (up_far,), cost=0)
+    up_three = up_far, swap_chips(up_far, 1), swap_chips(up_far, 2)
     near_weights = [projections] + [swap_planes(projections, s) for s in steps]
-    far_tokens = swap_cores(near_tokens)
-    up_far = stack(up_far, cost=50)
     unit_one, key_row, query_column = step(
         normalize_tokens,
         (wide(every, width), wide(8, every), wide(group, 128)),
         (near_tokens, far_tokens),
-        cost=50,
+        cost=1,
     )
     far_weights = swap_cores(stack(near_weights))
 
-    def all_chips(piece, cut):
-        from_x, from_y = swap_chips(piece, 1), swap_chips(piece, 2)
-        count, lanes = piece.shape
-        to_x, to_y = step(
-            cross_halves, (shaped(cut, lanes), shaped(count - cut, lanes)), (from_x, from_y), cost=50
-        )
-        return piece, from_x, from_y, swap_chips(to_x, 1), swap_chips(to_y, 2)
-
-    up_all = all_chips(up_far, up_far.shape[0] // 32 * 16 + 16)
+    def first_chips(piece):
+        return piece, swap_chips(piece, 1), swap_chips(piece, 2)
+
+    def all_chips(three, cut):
+        count, lanes = three[0].shape
+        to_x, to_y = step(cross_halves, (shaped(cut, lanes), shaped(count - cut, lanes)), three[1:], cost=50)
+        return (*three, swap_chips(to_x, 1), swap_chips(to_y, 2))
+
+    up_all = all_chips(up_three, up_far.shape[0] // 32 * 16 + 16)
     down_far = [swap_planes(down_piece, s) for s in steps]
 
     h_one, w_three, projected, probs, mixed, sent, vectors, b_up = step(
@@ -1171,13 +1237,29 @@
             wide(1, units),
         ),
         (unit_one, key_row, query_column, *near_weights, far_weights),
-        scratch=[pltpu.VMEM((4, 16, feat), F32), pltpu.VMEM((group, every), F32)],
-        vmem=24,
+        far_outs=range(5),
+        scratch=[
+            pltpu.VMEM((4, 16, feat), F32),
+            pltpu.VMEM((group, every), F32),
+            pltpu.VMEM((every, width), BF16),
+            pltpu.VMEM((width, 3 * feat), BF16),
+            pltpu.VMEM((every, 3 * feat), BF16),
+            pltpu.VMEM((heads, group, every), BF16),
+            pltpu.VMEM((group, feat), F32),
+            dma((4 + heads,)),
+        ],
+        vmem=28,
         cost=50,
     )
     mixed_low = trade_chips(sent)
-    down_far = stack(down_far)
-    out_near = step(build_half, shaped(width, core_units), (output_weight, *up_all))
+    down_far = first_chips(stack(down_far))
+    out_near = step(
+        build_half,
+        shaped(width, core_units),
+        (output_weight, *up_all),
+        far=(0,),
+        scratch=[dma],
+    )
     out_far = swap_cores(out_near)
     w_up = step(
         build_up, shaped(width, units), (up_weight, *up_all), far=(0,), scratch=[dma((4,))], cost=50
@@ -1190,7 +1272,8 @@
         (mixed_low, w_output, own, vectors),
     )
     h_pair = both_cores(h_two)
-    down_all = all_chips(down_far, down_far.shape[0] // 2)
+    mixed_pair = both_cores(mixed_low)
+    down_all = all_chips(down_far, down_far[0].shape[0] // 2)
     act, slope = step(
         activate,
         (shaped(2 * rows, units), wide(2 * rows, units)),
@@ -1219,8 +1302,7 @@
     d_down = both_cores(d_down)
 
     def five(count, lanes):
-        both = (shaped(4 * count, lanes),) * 2
-        return (wide(4 * count, lanes),) + both + (wide(2 * count, lanes),) * 2
+        return (shaped(4 * count, lanes),) * 3 + (shaped(2 * count, lanes),) * 2
 
     def onward(parts, arrived):
         count, lanes = parts[3].shape
@@ -1248,70 +1330,75 @@
     )
     d_mixed = trade_chips(d_sent)
 
-    kept_out, given_out = step(
-        output_grads,
-        (wide(width, core_units), shaped(width, core_units)),
-        (mixed_low, d_attn),
-    )
-    given_out = swap_cores(given_out)
     down_sums = onward(down_parts, down_arrived)
+    attn_pair = both_cores(d_attn)
     up_parts = step(
         up_grads,
         five(quarter, 5 * core_units),
-        (h_pair, d_up, kept_out, given_out),
+        (h_pair, d_up, mixed_pair, attn_pair),
         scratch=[pltpu.VMEM((width, 5 * core_units), F32)],
         vmem=24,
+        cost=2,
     )
     up_arrived = swap_chips(up_parts[1], 1), swap_chips(up_parts[2], 2)
-
-    d_three, kept, given, from_attention = step(
+    down_planes = trade_planes(step(sum_chips, shaped(4 * part_units, width), down_sums))
+
+    d_near, d_far, kept, given, from_attention = step(
         attend_back,
         (
-            shaped(every, 3 * feat),
-            wide(4 * half, 3 * feat),
+            shaped(group, width),
+            shaped(group, width),
+            shaped(4 * half, 3 * feat),
             shaped(4 * half, 3 * feat),
             wide(8, width),
         ),
-        (d_mixed, probs, projected, mixed, h_one, w_three, vectors),
-        scratch=[pltpu.VMEM((group, every), BF16), pltpu.VMEM((width, 3 * feat), F32)],
-        vmem=24,
+        (d_mixed, vectors, h_one, w_three, projected, probs, mixed),
+        far=range(2, 7),
+        scratch=[
+            pltpu.VMEM((every, 3 * feat), BF16),
+            pltpu.VMEM((group, every), BF16),
+            pltpu.VMEM((width, 3 * feat), F32),
+            pltpu.VMEM((every, width), BF16),
+            pltpu.VMEM((width, 3 * feat), BF16),
+            pltpu.VMEM((every, 3 * feat), BF16),
+            pltpu.VMEM((heads, group, every), BF16),
+            pltpu.VMEM((group, feat), F32),
+            dma((4 + heads,)),
+        ],
+        vmem=28,
         cost=50,
     )
+    d_far = swap_cores(d_far)
+    up_sums = onward(up_parts, up_arrived)
     given = both_cores(given)
-    d_near, d_far = step(
-        inputs_back, (wide(group, width), shaped(group, width)), (d_three, w_three)
-    )
-    d_far = swap_cores(d_far)
-    arrived = trade_planes(
-        step(
-            pack_gradients,
-            shaped(8 * half, width),
-            (kept, given, from_attention, from_second, from_result, up_line, *down_sums),
-        )
-    )
-    up_sums = onward(up_parts, up_arrived)
-    shares = step(
-        share_inputs, (wide(rows, width),) + (shaped(rows, width),) * 3, (d_near, d_far)
-    )
-    shares = [shares[0]] + [swap_chips(shares[k], k) for k in steps]
+    arrived, down_planes = step(
+        pack_gradients,
+        (shaped(4 * half, width), shaped(part_units, width)),
+        (kept, given, from_attention, from_second, from_result, up_line, down_planes),
+        cost=1,
+    )
+    arrived = trade_planes(arrived)
 
     def spread(piece):
         return [piece] + [swap_chips(piece, k) for k in steps]
 
     def whole(near):
-        return (*near, swap_cores(stack(near)))
+        return (*near, swap_cores(stack(near, cost=1)))
 
     up_planes = step(
         send_planes,
-        (wide(quarter, 5 * core_units),) + (shaped(quarter, 5 * core_units),) * 3,
+        (shaped(quarter, 5 * core_units),) * 4,
         up_sums,
         scratch=[pltpu.VMEM((4 * quarter, 5 * core_units), F32)],
+        cost=50,
     )
     up_planes = [up_planes[0]] + [swap_planes(up_planes[s], s) for s in steps]
-    grad_tokens = step(finish_inputs, shaped(rows, width), (*shares, own, d_second, vectors), cost=3)
-    both = spread(step(sum_planes, shaped(2 * half, width), (arrived,)))
-    up_near = spread(step(sum_pieces, shaped(quarter, 5 * core_units), up_planes))
-    both = whole(both)
+    shares = step(share_inputs, (shaped(rows, width),) * 4, (d_near, d_far), cost=50)
+    shares = [shares[0]] + [swap_chips(shares[k], k) for k in steps]
+    both = trade_chips(step(sum_planes, shaped(8 * half, width), (arrived, down_planes), cost=50))
+    up_near = spread(step(sum_pieces, shaped(quarter, 5 * core_units), up_planes, cost=50))
+    grad_tokens = step(finish_inputs, shaped(rows, width), (*shares, own, d_second, vectors), cost=50)
+    both = (both, swap_cores(both))
     finished = step(
         finish_projections,
         (wide(shard, width),) * 3
@@ -1321,10 +1408,21 @@
         (*both, count),
         scratch=[pltpu.VMEM((8, 16, feat), F32), pltpu.VMEM((8, own_units), F32)],
         scalar=3,
-    )
-    grad_down_weight = step(finish_down, wide(own_units, width), both)
+        cost=50,
+    )
+    grad_down_weight = step(
+        finish_down,
+        wide(own_units, width),
+        both,
+        far_outs=(0,),
+        scratch=[pltpu.VMEM((own_units, width), F32), dma((8,))],
+    )
     grad_up_weight, grad_output_weight = step(
-        finish_up, (wide(shard, hidden), wide(shard, width)), whole(up_near)
+        finish_up,
+        (wide(shard, hidden), wide(shard, width)),
+        whole(up_near),
+        far_outs=(0, 1),
+        scratch=[pltpu.VMEM((shard, hidden), F32), pltpu.VMEM((shard, width), F32), dma((8,))],
     )
     sums, two = finished[4:10], finished[10:12]
     return (

time: 243 us -> 238 us (0.979)
  local copies, waits for them, and re-layouts: 28.2 us -> 14.1 us
  Pallas kernels: 77.5 us -> 85.2 us
  blocking collectives: 11.6 us -> 16 us
    all_to_all x1 -> x3, starting transfers between devices: 4.44 us -> 22 us  [trade_planes(): return lax.all_to_all(value, 'fsdp', 0, 0, tiled=True)]
    ppermute x12 -> x9, starting transfers between devices: 26.9 us -> 10.4 us  [swap_planes(): return lax.ppermute(value, 'fsdp', [(i, i ^ step) for i in range(size)])]
    unnamed x150 -> x82, local copies, waits for them, and re-layouts: 28.2 us -> 14.1 us
    pallas_call x38 -> x37, Pallas kernels: 77.5 us -> 85.2 us  [local_call(): pl.pallas_call(kernel, out_shape=(*(pltpu.HBM(o.shape, o.dtype) if i in f...]
    all_to_all x3, waiting for transfers between devices: 3.87 us -> 9.89 us  [trade_chips(): lax.all_to_all(value, 'ctx', 0, 0, axis_index_groups=groups, tiled=True)]
    ppermute x12 -> x9, waiting for transfers between devices: 16 us -> 10.2 us  [swap_planes(): return lax.ppermute(value, 'fsdp', [(i, i ^ step) for i in range(size)])]
    all_gather x5 -> x7, blocking collectives: 11.6 us -> 16 us  [both_cores(): lax.all_gather(value, 'ctx', axis=0, tiled=True, axis_index_groups=pairs)]
    ppermute x25, waiting for transfers between devices: 18.9 us -> 16 us  [swap_chips(): return lax.ppermute(value, 'ctx', [(i, i ^ 2 * step) for i in range(size)])]
  transfers between devices with their start and end apart: 48 -> 46, of which waited for: 17 -> 12; matrix products, arithmetic and copies ran while one was open for 0% -> 0% of each run, Pallas kernels for 26% -> 29%
where the time goes in v2:
time: 238 us; the launch traced here: 236 us
  Pallas kernels  85.2 us (36%)
  starting transfers between devices  72.9 us (31%)
  waiting for transfers between devices  46.4 us (19%)
  blocking collectives  16 us (7%)
  local copies, waits for them, and re-layouts  14.1 us (6%)
    pallas_call x37, Pallas kernels, local_call(): pl.pallas_call(kernel, out_shape=(*(pltpu.HBM(o.shape, o.dtype) if i in f...  85.2 us
    ppermute x25, starting transfers between devices, swap_chips(): return lax.ppermute(value, 'ctx', [(i, i ^ 2 * step) for i in range(size)])  29.5 us
    all_to_all x3, starting transfers between devices, trade_planes(): return lax.all_to_all(value, 'fsdp', 0, 0, tiled=True)  22 us
    all_gather x7, blocking collectives, both_cores(): lax.all_gather(value, 'ctx', axis=0, tiled=True, axis_index_groups=pairs)  16 us
    ppermute x25, waiting for transfers between devices, swap_chips(): return lax.ppermute(value, 'ctx', [(i, i ^ 2 * step) for i in range(size)])  16 us
    unnamed x82, local copies, waits for them, and re-layouts  14.1 us
    all_to_all x3, starting transfers between devices, trade_chips(): lax.all_to_all(value, 'ctx', 0, 0, axis_index_groups=groups, tiled=True)  10.7 us
    ppermute x9, starting transfers between devices, swap_planes(): return lax.ppermute(value, 'fsdp', [(i, i ^ step) for i in range(size)])  10.4 us
  transfers between devices with their start and end apart: 46, of which 12 were waited for; matrix products, arithmetic and copies ran while one was open for 0% of the time, Pallas kernels for 29%

profile of v2, /device:TPU:0, one launch (start us, length us, event | category | flops | bytes accessed | tf_op | source)
XLA Modules:
  0.0 236.2 jit_solution(13396255649121483999)
XLA Ops:
  0.8 2.9 %shard_map.331 = (bf16[192,1920]{1,0:T(8,128)(2,1)}, bf16[96,768]{1,0:T(8,128)(2,1)}, f32[8,128]{1,0:T(8,128)S(1)}) custom-call(s32[3]{0:T(128)S(1)} %pad_add_fusion.where_ref, bf16[192,3072]{1,0:T(8,128)(2,1)} %refs_0_.8, bf16[192,768]{1,0:T(8,128)(2,1)} %refs_0_.7, bf16[768,768]{1,0:T(8,128)(2,1)} %refs_0_.9), custom_call_target="tpu_custom_call" | custom-call | tf_op jit(solution)/shard_map/pallas_call | solution.py:437
  3.7 6.3 %all-to-all-start = ((bf16[4,48,1920]{2,1,0:T(8,128)(2,1)}), bf16[4,48,1920]{2,1,0:T(8,128)(2,1)S(1)}, u32[]{:S(2)}, u32[]{:S(2)}) async-start(bf16[4,48,1920]{2,1,0:T(8,128)(2,1)} %bitcast.4), calls=%async_computation | async-start | bytes 1474560 | tf_op jit(solution)/shard_map/all_to_all | solution.py:405
  16.1 3.4 %collective-permute-done.refs_1_ = bf16[160,768]{1,0:T(8,128)(2,1)S(1)} collective-permute-done((bf16[160,768]{1,0:T(8,128)(2,1)S(1)}, bf16[160,768]{1,0:T(8,128)(2,1)S(1)}, u32[]{:S(2)}, u32[]{:S(2)}) %collective-permute-start) | collective-permute-done | bytes 245792 | tf_op jit(solution)/shard_map/ppermute | solution.py:390
  19.6 5.1 %collective-permute-done.1.refs_2_ = bf16[160,768]{1,0:T(8,128)(2,1)S(1)} collective-permute-done((bf16[160,768]{1,0:T(8,128)(2,1)S(1)}, bf16[160,768]{1,0:T(8,128)(2,1)S(1)}, u32[]{:S(2)}, u32[]{:S(2)}) %collective-permute-start.1) | collective-permute-done | bytes 245792 | tf_op jit(solution)/shard_map/ppermute | solution.py:390
  25.3 3.8 %all-to-all-done = bf16[4,48,1920]{2,1,0:T(8,128)(2,1)S(1)} async-done(((bf16[4,48,1920]{2,1,0:T(8,128)(2,1)}), bf16[4,48,1920]{2,1,0:T(8,128)(2,1)S(1)}, u32[]{:S(2)}, u32[]{:S(2)}) %all-to-all-start) | async-done | bytes 737312 | tf_op jit(solution)/shard_map/all_to_all | solution.py:405
  34.8 2.4 %collective-permute-start.6 = (bf16[96,768]{1,0:T(8,128)(2,1)S(1)}, bf16[96,768]{1,0:T(8,128)(2,1)S(1)}, u32[]{:S(2)}, u32[]{:S(2)}) collective-permute-start(bf16[96,768]{1,0:T(8,128)(2,1)S(1)} %get-tuple-element.161.refs_0_.refs_3_), channel_id=1, source_target_pairs={{0,3},{1,2},{2,1},{3,0},{4,7},{5,6},{6,5},{7,4},{8,11},{9,10},{10,... | collective-permute-start | bytes 442376 | tf_op jit(solution)/shard_map/ppermute | solution.py:395
  37.1 2.4 %shard_map.336 = (f32[1152,768]{1,0:T(8,128)S(1)}, f32[8,1152]{1,0:T(8,128)S(1)}, f32[576,128]{1,0:T(8,128)S(1)}, f32[8,128]{1,0:T(8,128)S(1)}) custom-call(s32[3]{0:T(128)S(1)} %pad_add_fusion.where_ref, bf16[640,768]{1,0:T(8,128)(2,1)S(1)} %get-tuple-element.154.refs_0_, bf16[640,768]{1,0:T(8,128)(2,1)} %collective-permute-done.3.refs_1_, ...), custom_call_target="tpu_custom_call" | custom-call | flops 1000000000 | bytes 1000000 | tf_op jit(solution)/shard_map/pallas_call | solution.py:437
  39.7 7.1 %collective-permute-done.5.refs_2_.refs_5_ = bf16[96,768]{1,0:T(8,128)(2,1)S(1)} collective-permute-done((bf16[96,768]{1,0:T(8,128)(2,1)S(1)}, bf16[96,768]{1,0:T(8,128)(2,1)S(1)}, u32[]{:S(2)}, u32[]{:S(2)}) %collective-permute-start.5) | collective-permute-done | bytes 147488 | tf_op jit(solution)/shard_map/ppermute | solution.py:395
  51.5 10.5 %shard_map.339 = (bf16[1152,768]{1,0:T(8,128)(2,1)}, bf16[768,576]{1,0:T(8,128)(2,1)}, bf16[1152,576]{1,0:T(8,128)(2,1)}, bf16[3,576,1152]{2,1,0:T(8,128)(2,1)},...) custom-call(s32[3]{0:T(128)S(1)} %pad_add_fusion.where_ref, ...), custom_call_target="tpu_custom_call" | custom-call | flops 49999998976 | bytes 50000000 | tf_op jit(solution)/shard_map/pallas_call | solution.py:437
  65.5 3.6 %all-to-all-start.1 = ((bf16[4,160,192]{2,1,0:T(8,128)(2,1)}), bf16[4,160,192]{2,1,0:T(8,128)(2,1)S(1)}, u32[]{:S(2)}, u32[]{:S(2)}) async-start(bf16[4,160,192]{2,1,0:T(8,128)(2,1)} %bitcast.6), calls=%async_computation.1 | async-start | bytes 655360 | tf_op jit(solution)/shard_map/all_to_all | solution.py:401
  71.1 2.1 shard_map.342
  75.4 4.0 %all-to-all-done.1 = bf16[4,160,192]{2,1,0:T(8,128)(2,1)S(1)} async-done(((bf16[4,160,192]{2,1,0:T(8,128)(2,1)}), bf16[4,160,192]{2,1,0:T(8,128)(2,1)S(1)}, u32[]{:S(2)}, u32[]{:S(2)}) %all-to-all-start.1) | async-done | bytes 245792 | tf_op jit(solution)/shard_map/all_to_all | solution.py:401
  84.8 2.3 all_gather.25.refs_2_
  100.5 3.1 %shard_map.350 = (bf16[384,768]{1,0:T(8,128)(2,1)S(1)}, bf16[384,768]{1,0:T(8,128)(2,1)}, bf16[384,768]{1,0:T(8,128)(2,1)}, bf16[192,768]{1,0:T(8,128)(2,1)S(1)}...) custom-call(s32[3]{0:T(128)S(1)} %pad_add_fusion.where_ref, bf16[288,1536]{1,0:T(8,128)(2,1)S(1)} %get-tuple-element.186.refs_0_, ...), custom_call_target="tpu_custom_call" | custom-call | tf_op jit(solution)/shard_map/pallas_call | solution.py:437
  105.6 3.9 %shard_map.351 = (bf16[288,1536]{1,0:T(8,128)(2,1)S(1)}, f32[144,768]{1,0:T(8,128)S(1)}, bf16[144,768]{1,0:T(8,128)(2,1)S(1)}, f32[1,1536]{1,0:T(1,128)S(1)}, f32[8,128]{1,0:T(8,128)S(1)}) custom-call(s32[3]{0:T(128)S(1)} %pad_add_fusion.where_ref, bf16[288,768]{1,0:T(8,128)(2,1)S(1)} %all_gather.23.refs_1_.refs_0_, ...), custom_call_target="tpu_custom_call" | custom-call | flops 49999998976 | bytes 50000000 | tf_op jit(solution)/shard_map/pallas_call | solution.py:437
  115.2 3.5 %all-to-all-start.2 = ((bf16[4,144,192]{2,1,0:T(8,128)(2,1)}), bf16[4,144,192]{2,1,0:T(8,128)(2,1)S(1)}, u32[]{:S(2)}, u32[]{:S(2)}) async-start(bf16[4,144,192]{2,1,0:T(8,128)(2,1)} %bitcast.30), calls=%async_computation.2 | async-start | bytes 589824 | tf_op jit(solution)/shard_map/all_to_all | solution.py:401
  127.6 3.7 %shard_map.354 = (bf16[192,1920]{1,0:T(8,128)(2,1)S(1)}, bf16[192,1920]{1,0:T(8,128)(2,1)}, bf16[192,1920]{1,0:T(8,128)(2,1)}, bf16[96,1920]{1,0:T(8,128)(2,1)S(...) custom-call(s32[3]{0:T(128)S(1)} %pad_add_fusion.where_ref, bf16[288,768]{1,0:T(8,128)(2,1)S(1)} %all_gather.21.refs_0_, ...), custom_call_target="tpu_custom_call" | custom-call | flops 2000000000 | bytes 2000000 | tf_op jit(solution)/shard_map/pallas_call | solution.py:437
  138.1 10.6 %all-to-all-start.3 = ((bf16[4,96,768]{2,1,0:T(8,128)(2,1)}), bf16[4,96,768]{2,1,0:T(8,128)(2,1)S(1)}, u32[]{:S(2)}, u32[]{:S(2)}) async-start(bf16[4,96,768]{2,1,0:T(8,128)(2,1)} %bitcast.13), calls=%async_computation.3 | async-start | bytes 1179648 | tf_op jit(solution)/shard_map/all_to_all | solution.py:405
  148.7 12.1 %shard_map.356 = (bf16[576,768]{1,0:T(8,128)(2,1)S(1)}, bf16[576,768]{1,0:T(8,128)(2,1)S(1)}, bf16[384,576]{1,0:T(8,128)(2,1)S(1)}, bf16[384,576]{1,0:T(8,128)(2...) custom-call(s32[3]{0:T(128)S(1)} %pad_add_fusion.where_ref, bf16[576,192]{1,0:T(8,128)(2,1)S(1)} %bitcast.29, ...), custom_call_target="tpu_custom_call" | custom-call | flops 49999998976 | bytes 50000000 | tf_op jit(solution)/shard_map/pallas_call | solution.py:437
  160.9 2.7 %shard_map.357 = (bf16[96,1920]{1,0:T(8,128)(2,1)}, bf16[96,1920]{1,0:T(8,128)(2,1)}, f32[8,128]{1,0:T(8,128)S(1)}) custom-call(s32[3]{0:T(128)S(1)} %pad_add_fusion.where_ref, bf16[192,1920]{1,0:T(8,128)(2,1)} %collective-permute-done.24.refs_0_.refs_1_, bf16[192,1920]{1,0:T(8,128)(2,1)} %collective-permute-done.25.refs_1_.refs_2_, ...), custom_call_target="tpu_custom_call" | custom-call | flops 49999998976 | bytes 50000000 | tf_op jit(solution)/shard_map/pallas_call | solution.py:437
  165.5 3.1 %all_gather.27.refs_1_ = bf16[768,576]{1,0:T(8,128)(2,1)S(1)} all-gather(bf16[384,576]{1,0:T(8,128)(2,1)S(1)} %get-tuple-element.225), channel_id=1, replica_groups={{0,4},{8,12},{16,20},{24,28},{1,5},{9,13},{17,21},{25,29},{2,6},{10,14}..., dimensions={0}, use_global_device_ids=true | all-gather | bytes 1327104 | tf_op jit(solution)/shard_map/all_gather | solution.py:385
  172.7 5.1 %all-to-all-start.4 = ((bf16[4,96,768]{2,1,0:T(8,128)(2,1)}), bf16[4,96,768]{2,1,0:T(8,128)(2,1)S(1)}, u32[]{:S(2)}, u32[]{:S(2)}) async-start(bf16[4,96,768]{2,1,0:T(8,128)(2,1)} %bitcast.15), calls=%async_computation.4 | async-start | bytes 1179648 | tf_op jit(solution)/shard_map/all_to_all | solution.py:405
  179.0 2.7 %shard_map.359 = (bf16[48,1920]{1,0:T(8,128)(2,1)S(1)}, bf16[48,1920]{1,0:T(8,128)(2,1)}, bf16[48,1920]{1,0:T(8,128)(2,1)S(1)}, bf16[48,1920]{1,0:T(8,128)(2,1)S(1)}, f32[8,128]{1,0:T(8,128)S(1)}) custom-call(s32[3]{0:T(128)S(1)} %pad_add_fusion.where_ref, bf16[192,1920]{1,0:T(8,128)(2,1)S(1)} %copy-done.28, ...), custom_call_target="tpu_custom_call" | custom-call | flops 49999998976 | bytes 50000000 | tf_op jit(solution)/shard_map/pallas_call | solution.py:437
  183.6 2.4 %collective-permute-start.34 = (bf16[48,1920]{1,0:T(8,128)(2,1)S(1)}, bf16[48,1920]{1,0:T(8,128)(2,1)S(1)}, u32[]{:S(2)}, u32[]{:S(2)}) collective-permute-start(bf16[48,1920]{1,0:T(8,128)(2,1)S(1)} %get-tuple-element.255), channel_id=1, source_target_pairs={{0,2},{1,3},{2,0},{3,1},{4,6},{5,7},{6,4},{7,5},{8,10},{9,11},{10,... | collective-permute-start | bytes 552968 | tf_op jit(solution)/shard_map/ppermute | solution.py:395
  191.0 4.4 %all-to-all-done.4 = bf16[4,96,768]{2,1,0:T(8,128)(2,1)S(1)} async-done(((bf16[4,96,768]{2,1,0:T(8,128)(2,1)}), bf16[4,96,768]{2,1,0:T(8,128)(2,1)S(1)}, u32[]{:S(2)}, u32[]{:S(2)}) %all-to-all-start.4) | async-done | bytes 589856 | tf_op jit(solution)/shard_map/all_to_all | solution.py:405
  197.2 3.7 %all-to-all-start.5 = ((bf16[4,192,768]{2,1,0:T(8,128)(2,1)}), bf16[4,192,768]{2,1,0:T(8,128)(2,1)S(1)}, u32[]{:S(2)}, u32[]{:S(2)}) async-start(bf16[4,192,768]{2,1,0:T(8,128)(2,1)} %bitcast.17), calls=%async_computation.5 | async-start | bytes 2359296 | tf_op jit(solution)/shard_map/all_to_all | solution.py:401
  200.9 2.9 %collective-permute-start.32 = (bf16[144,768]{1,0:T(8,128)(2,1)S(1)}, bf16[144,768]{1,0:T(8,128)(2,1)}, u32[]{:S(2)}, u32[]{:S(2)}) collective-permute-start(bf16[144,768]{1,0:T(8,128)(2,1)S(1)} %get-tuple-element.251), channel_id=1, source_target_pairs={{0,24},{4,28},{8,16},{12,20},{16,8},{20,12},{24,0},{28,4},{1,25},{... | collective-permute-start | bytes 663560 | tf_op jit(solution)/shard_map/ppermute | solution.py:390
  203.8 3.1 %collective-permute-done.34.refs_2_ = bf16[48,1920]{1,0:T(8,128)(2,1)S(1)} collective-permute-done((bf16[48,1920]{1,0:T(8,128)(2,1)S(1)}, bf16[48,1920]{1,0:T(8,128)(2,1)S(1)}, u32[]{:S(2)}, u32[]{:S(2)}) %collective-permute-start.34) | collective-permute-done | bytes 184352 | tf_op jit(solution)/shard_map/ppermute | solution.py:395
  211.6 5.9 %all-to-all-done.5 = bf16[4,192,768]{2,1,0:T(8,128)(2,1)S(1)} async-done(((bf16[4,192,768]{2,1,0:T(8,128)(2,1)}), bf16[4,192,768]{2,1,0:T(8,128)(2,1)S(1)}, u32[]{:S(2)}, u32[]{:S(2)}) %all-to-all-start.5) | async-done | bytes 1179680 | tf_op jit(solution)/shard_map/all_to_all | solution.py:401
  217.5 5.6 %collective-permute-done.32.refs_3_ = bf16[144,768]{1,0:T(8,128)(2,1)} collective-permute-done((bf16[144,768]{1,0:T(8,128)(2,1)S(1)}, bf16[144,768]{1,0:T(8,128)(2,1)}, u32[]{:S(2)}, u32[]{:S(2)}) %collective-permute-start.32) | collective-permute-done | bytes 221216 | tf_op jit(solution)/shard_map/ppermute | solution.py:390
  231.0 2.2 collective-permute-done.39.refs_4_
  233.2 2.9 %shard_map.367 = (f32[192,3072]{1,0:T(8,128)}, f32[192,768]{1,0:T(8,128)}, f32[8,128]{1,0:T(8,128)}) custom-call(s32[3]{0:T(128)S(1)} %pad_add_fusion.where_ref, bf16[48,1920]{1,0:T(8,128)(2,1)S(1)} %get-tuple-element.269.refs_0_, bf16[48,1920]{1,0:T(8,128)(2,1)S(1)} %collective-permute-done.36.refs_1_, ...), custom_call_target="tpu_custom_call" | custom-call | tf_op jit(solution)/shard_map/pallas_call | solution.py:437
  (187 shorter events, 95.4 us)
Async XLA Ops:
  3.7 25.4 %all-to-all-start = ((bf16[4,48,1920]{2,1,0:T(8,128)(2,1)}), bf16[4,48,1920]{2,1,0:T(8,128)(2,1)S(1)}, u32[]{:S(2)}, u32[]{:S(2)}) async-start(bf16[4,48,1920]{2,1,0:T(8,128)(2,1)} %bitcast.4), calls=%async_computation | async-start | bytes 1474560 | tf_op jit(solution)/shard_map/all_to_all | solution.py:405
  29.7 19.2 %collective-permute-start.8 = (bf16[144,1920]{1,0:T(8,128)(2,1)S(1)}, bf16[144,1920]{1,0:T(8,128)(2,1)S(1)}, u32[]{:S(2)}, u32[]{:S(2)}) collective-permute-start(bf16[144,1920]{1,0:T(8,128)(2,1)S(1)} %get-tuple-element.164.refs_1_), channel_id=1, source_target_pairs={{0,8},{4,12},{8,0},{12,4},{16,24},{20,28},{24,16},{28,20},{1,9},{5... | collective-permute-start | bytes 1658888 | tf_op jit(solution)/shard_map/ppermute | solution.py:390
  31.3 17.7 %collective-permute-start.9 = (bf16[144,1920]{1,0:T(8,128)(2,1)S(1)}, bf16[144,1920]{1,0:T(8,128)(2,1)S(1)}, u32[]{:S(2)}, u32[]{:S(2)}) collective-permute-start(bf16[144,1920]{1,0:T(8,128)(2,1)S(1)} %get-tuple-element.164.refs_1_), channel_id=1, source_target_pairs={{0,16},{4,20},{8,24},{12,28},{16,0},{20,4},{24,8},{28,12},{1,17},{... | collective-permute-start | bytes 1658888 | tf_op jit(solution)/shard_map/ppermute | solution.py:390
  32.7 14.0 %collective-permute-start.5 = (bf16[96,768]{1,0:T(8,128)(2,1)S(1)}, bf16[96,768]{1,0:T(8,128)(2,1)S(1)}, u32[]{:S(2)}, u32[]{:S(2)}) collective-permute-start(bf16[96,768]{1,0:T(8,128)(2,1)S(1)} %get-tuple-element.161.refs_0_.refs_3_), channel_id=1, source_target_pairs={{0,2},{1,3},{2,0},{3,1},{4,6},{5,7},{6,4},{7,5},{8,10},{9,11},{10,... | collective-permute-start | bytes 442376 | tf_op jit(solution)/shard_map/ppermute | solution.py:395
  39.6 22.4 %collective-permute-start.12 = (bf16[96,768]{1,0:T(8,128)(2,1)}, bf16[96,768]{1,0:T(8,128)(2,1)S(1)}, u32[]{:S(2)}, u32[]{:S(2)}) collective-permute-start(bf16[96,768]{1,0:T(8,128)(2,1)} %get-tuple-element.170), channel_id=1, source_target_pairs={{0,1},{1,0},{2,3},{3,2},{4,5},{5,4},{6,7},{7,6},{8,9},{9,8},{10,11... | collective-permute-start | bytes 442376 | tf_op jit(solution)/shard_map/ppermute | solution.py:395
  46.8 15.2 %collective-permute-start.13 = (bf16[96,768]{1,0:T(8,128)(2,1)}, bf16[96,768]{1,0:T(8,128)(2,1)S(1)}, u32[]{:S(2)}, u32[]{:S(2)}) collective-permute-start(bf16[96,768]{1,0:T(8,128)(2,1)} %get-tuple-element.170), channel_id=1, source_target_pairs={{0,2},{1,3},{2,0},{3,1},{4,6},{5,7},{6,4},{7,5},{8,10},{9,11},{10,... | collective-permute-start | bytes 442376 | tf_op jit(solution)/shard_map/ppermute | solution.py:395
  46.8 15.2 %collective-permute-start.14 = (bf16[96,768]{1,0:T(8,128)(2,1)}, bf16[96,768]{1,0:T(8,128)(2,1)S(1)}, u32[]{:S(2)}, u32[]{:S(2)}) collective-permute-start(bf16[96,768]{1,0:T(8,128)(2,1)} %get-tuple-element.170), channel_id=1, source_target_pairs={{0,3},{1,2},{2,1},{3,0},{4,7},{5,6},{6,5},{7,4},{8,11},{9,10},{10,... | collective-permute-start | bytes 442376 | tf_op jit(solution)/shard_map/ppermute | solution.py:395
  50.3 18.8 %collective-permute-start.10 = (bf16[80,1920]{1,0:T(8,128)(2,1)}, bf16[80,1920]{1,0:T(8,128)(2,1)S(1)}, u32[]{:S(2)}, u32[]{:S(2)}) collective-permute-start(bf16[80,1920]{1,0:T(8,128)(2,1)} %get-tuple-element.168), channel_id=1, source_target_pairs={{0,8},{4,12},{8,0},{12,4},{16,24},{20,28},{24,16},{28,20},{1,9},{5... | collective-permute-start | bytes 921608 | tf_op jit(solution)/shard_map/ppermute | solution.py:390
  51.0 18.2 %collective-permute-start.11 = (bf16[64,1920]{1,0:T(8,128)(2,1)}, bf16[64,1920]{1,0:T(8,128)(2,1)}, u32[]{:S(2)}, u32[]{:S(2)}) collective-permute-start(bf16[64,1920]{1,0:T(8,128)(2,1)} %get-tuple-element.169), channel_id=1, source_target_pairs={{0,16},{4,20},{8,24},{12,28},{16,0},{20,4},{24,8},{28,12},{1,17},{... | collective-permute-start | bytes 737288 | tf_op jit(solution)/shard_map/ppermute | solution.py:390
  62.6 18.8 %collective-permute-start.16 = (bf16[288,768]{1,0:T(8,128)(2,1)S(1)}, bf16[288,768]{1,0:T(8,128)(2,1)S(1)}, u32[]{:S(2)}, u32[]{:S(2)}) collective-permute-start(bf16[288,768]{1,0:T(8,128)(2,1)S(1)} %get-tuple-element.183.refs_1_), channel_id=1, source_target_pairs={{0,8},{4,12},{8,0},{12,4},{16,24},{20,28},{24,16},{28,20},{1,9},{5... | collective-permute-start | bytes 1327112 | tf_op jit(solution)/shard_map/ppermute | solution.py:390
  64.1 17.3 %collective-permute-start.17 = (bf16[288,768]{1,0:T(8,128)(2,1)S(1)}, bf16[288,768]{1,0:T(8,128)(2,1)}, u32[]{:S(2)}, u32[]{:S(2)}) collective-permute-start(bf16[288,768]{1,0:T(8,128)(2,1)S(1)} %get-tuple-element.183.refs_1_), channel_id=1, source_target_pairs={{0,16},{4,20},{8,24},{12,28},{16,0},{20,4},{24,8},{28,12},{1,17},{... | collective-permute-start | bytes 1327112 | tf_op jit(solution)/shard_map/ppermute | solution.py:390
  65.5 13.8 %all-to-all-start.1 = ((bf16[4,160,192]{2,1,0:T(8,128)(2,1)}), bf16[4,160,192]{2,1,0:T(8,128)(2,1)S(1)}, u32[]{:S(2)}, u32[]{:S(2)}) async-start(bf16[4,160,192]{2,1,0:T(8,128)(2,1)} %bitcast.6), calls=%async_computation.1 | async-start | bytes 655360 | tf_op jit(solution)/shard_map/all_to_all | solution.py:401
  103.7 15.6 %collective-permute-start.20 = (bf16[384,768]{1,0:T(8,128)(2,1)}, bf16[384,768]{1,0:T(8,128)(2,1)S(1)}, u32[]{:S(2)}, u32[]{:S(2)}) collective-permute-start(bf16[384,768]{1,0:T(8,128)(2,1)} %get-tuple-element.212), channel_id=1, source_target_pairs={{0,8},{4,12},{8,0},{12,4},{16,24},{20,28},{24,16},{28,20},{1,9},{5... | collective-permute-start | bytes 1769480 | tf_op jit(solution)/shard_map/ppermute | solution.py:390
  105.0 15.4 %collective-permute-start.21 = (bf16[384,768]{1,0:T(8,128)(2,1)}, bf16[384,768]{1,0:T(8,128)(2,1)}, u32[]{:S(2)}, u32[]{:S(2)}) collective-permute-start(bf16[384,768]{1,0:T(8,128)(2,1)} %get-tuple-element.213), channel_id=1, source_target_pairs={{0,16},{4,20},{8,24},{12,28},{16,0},{20,4},{24,8},{28,12},{1,17},{... | collective-permute-start | bytes 1769480 | tf_op jit(solution)/shard_map/ppermute | solution.py:390
  115.2 22.9 %all-to-all-start.2 = ((bf16[4,144,192]{2,1,0:T(8,128)(2,1)}), bf16[4,144,192]{2,1,0:T(8,128)(2,1)S(1)}, u32[]{:S(2)}, u32[]{:S(2)}) async-start(bf16[4,144,192]{2,1,0:T(8,128)(2,1)} %bitcast.30), calls=%async_computation.2 | async-start | bytes 589824 | tf_op jit(solution)/shard_map/all_to_all | solution.py:401
  133.7 27.2 %collective-permute-start.24 = (bf16[192,1920]{1,0:T(8,128)(2,1)}, bf16[192,1920]{1,0:T(8,128)(2,1)}, u32[]{:S(2)}, u32[]{:S(2)}) collective-permute-start(bf16[192,1920]{1,0:T(8,128)(2,1)} %get-tuple-element.231), channel_id=1, source_target_pairs={{0,8},{4,12},{8,0},{12,4},{16,24},{20,28},{24,16},{28,20},{1,9},{5... | collective-permute-start | bytes 2211848 | tf_op jit(solution)/shard_map/ppermute | solution.py:390
  134.6 26.3 %collective-permute-start.25 = (bf16[192,1920]{1,0:T(8,128)(2,1)}, bf16[192,1920]{1,0:T(8,128)(2,1)}, u32[]{:S(2)}, u32[]{:S(2)}) collective-permute-start(bf16[192,1920]{1,0:T(8,128)(2,1)} %get-tuple-element.232), channel_id=1, source_target_pairs={{0,16},{4,20},{8,24},{12,28},{16,0},{20,4},{24,8},{28,12},{1,17},{... | collective-permute-start | bytes 2211848 | tf_op jit(solution)/shard_map/ppermute | solution.py:390
  138.1 30.5 %all-to-all-start.3 = ((bf16[4,96,768]{2,1,0:T(8,128)(2,1)}), bf16[4,96,768]{2,1,0:T(8,128)(2,1)S(1)}, u32[]{:S(2)}, u32[]{:S(2)}) async-start(bf16[4,96,768]{2,1,0:T(8,128)(2,1)} %bitcast.13), calls=%async_computation.3 | async-start | bytes 1179648 | tf_op jit(solution)/shard_map/all_to_all | solution.py:405
  163.7 14.2 %collective-permute-start.27 = (bf16[96,1920]{1,0:T(8,128)(2,1)}, bf16[96,1920]{1,0:T(8,128)(2,1)S(1)}, u32[]{:S(2)}, u32[]{:S(2)}) collective-permute-start(bf16[96,1920]{1,0:T(8,128)(2,1)} %get-tuple-element.242), channel_id=1, source_target_pairs={{0,8},{4,12},{8,0},{12,4},{16,24},{20,28},{24,16},{28,20},{1,9},{5... | collective-permute-start | bytes 1105928 | tf_op jit(solution)/shard_map/ppermute | solution.py:390
  164.4 13.4 %collective-permute-start.28 = (bf16[96,1920]{1,0:T(8,128)(2,1)}, bf16[96,1920]{1,0:T(8,128)(2,1)}, u32[]{:S(2)}, u32[]{:S(2)}) collective-permute-start(bf16[96,1920]{1,0:T(8,128)(2,1)} %get-tuple-element.243), channel_id=1, source_target_pairs={{0,16},{4,20},{8,24},{12,28},{16,0},{20,4},{24,8},{28,12},{1,17},{... | collective-permute-start | bytes 1105928 | tf_op jit(solution)/shard_map/ppermute | solution.py:390
  165.5 20.5 %collective-permute-start.26 = (bf16[576,768]{1,0:T(8,128)(2,1)S(1)}, bf16[576,768]{1,0:T(8,128)(2,1)}, u32[]{:S(2)}, u32[]{:S(2)}) collective-permute-start(bf16[576,768]{1,0:T(8,128)(2,1)S(1)} %get-tuple-element.240), channel_id=1, source_target_pairs={{0,4},{4,0},{8,12},{12,8},{16,20},{20,16},{24,28},{28,24},{1,5},{5... | collective-permute-start | bytes 2654216 | tf_op jit(solution)/shard_map/ppermute | solution.py:380
  172.7 22.6 %all-to-all-start.4 = ((bf16[4,96,768]{2,1,0:T(8,128)(2,1)}), bf16[4,96,768]{2,1,0:T(8,128)(2,1)S(1)}, u32[]{:S(2)}, u32[]{:S(2)}) async-start(bf16[4,96,768]{2,1,0:T(8,128)(2,1)} %bitcast.15), calls=%async_computation.4 | async-start | bytes 1179648 | tf_op jit(solution)/shard_map/all_to_all | solution.py:405
  181.6 19.3 %collective-permute-start.33 = (bf16[48,1920]{1,0:T(8,128)(2,1)}, bf16[48,1920]{1,0:T(8,128)(2,1)S(1)}, u32[]{:S(2)}, u32[]{:S(2)}) collective-permute-start(bf16[48,1920]{1,0:T(8,128)(2,1)} %get-tuple-element.254), channel_id=1, source_target_pairs={{0,1},{1,0},{2,3},{3,2},{4,5},{5,4},{6,7},{7,6},{8,9},{9,8},{10,11... | collective-permute-start | bytes 552968 | tf_op jit(solution)/shard_map/ppermute | solution.py:395
  183.6 23.2 %collective-permute-start.34 = (bf16[48,1920]{1,0:T(8,128)(2,1)S(1)}, bf16[48,1920]{1,0:T(8,128)(2,1)S(1)}, u32[]{:S(2)}, u32[]{:S(2)}) collective-permute-start(bf16[48,1920]{1,0:T(8,128)(2,1)S(1)} %get-tuple-element.255), channel_id=1, source_target_pairs={{0,2},{1,3},{2,0},{3,1},{4,6},{5,7},{6,4},{7,5},{8,10},{9,11},{10,... | collective-permute-start | bytes 552968 | tf_op jit(solution)/shard_map/ppermute | solution.py:395
  186.0 20.9 %collective-permute-start.35 = (bf16[48,1920]{1,0:T(8,128)(2,1)S(1)}, bf16[48,1920]{1,0:T(8,128)(2,1)}, u32[]{:S(2)}, u32[]{:S(2)}) collective-permute-start(bf16[48,1920]{1,0:T(8,128)(2,1)S(1)} %get-tuple-element.256), channel_id=1, source_target_pairs={{0,3},{1,2},{2,1},{3,0},{4,7},{5,6},{6,5},{7,4},{8,11},{9,10},{10,... | collective-permute-start | bytes 552968 | tf_op jit(solution)/shard_map/ppermute | solution.py:395
  188.7 21.7 %collective-permute-start.30 = (bf16[144,768]{1,0:T(8,128)(2,1)}, bf16[144,768]{1,0:T(8,128)(2,1)S(1)}, u32[]{:S(2)}, u32[]{:S(2)}) collective-permute-start(bf16[144,768]{1,0:T(8,128)(2,1)} %get-tuple-element.249), channel_id=1, source_target_pairs={{0,8},{4,12},{8,0},{12,4},{16,24},{20,28},{24,16},{28,20},{1,9},{5... | collective-permute-start | bytes 663560 | tf_op jit(solution)/shard_map/ppermute | solution.py:390
  189.5 22.0 %collective-permute-start.31 = (bf16[144,768]{1,0:T(8,128)(2,1)S(1)}, bf16[144,768]{1,0:T(8,128)(2,1)S(1)}, u32[]{:S(2)}, u32[]{:S(2)}) collective-permute-start(bf16[144,768]{1,0:T(8,128)(2,1)S(1)} %get-tuple-element.250), channel_id=1, source_target_pairs={{0,16},{4,20},{8,24},{12,28},{16,0},{20,4},{24,8},{28,12},{1,17},{... | collective-permute-start | bytes 663560 | tf_op jit(solution)/shard_map/ppermute | solution.py:390
  197.2 20.3 %all-to-all-start.5 = ((bf16[4,192,768]{2,1,0:T(8,128)(2,1)}), bf16[4,192,768]{2,1,0:T(8,128)(2,1)S(1)}, u32[]{:S(2)}, u32[]{:S(2)}) async-start(bf16[4,192,768]{2,1,0:T(8,128)(2,1)} %bitcast.17), calls=%async_computation.5 | async-start | bytes 2359296 | tf_op jit(solution)/shard_map/all_to_all | solution.py:401
  200.9 22.3 %collective-permute-start.32 = (bf16[144,768]{1,0:T(8,128)(2,1)S(1)}, bf16[144,768]{1,0:T(8,128)(2,1)}, u32[]{:S(2)}, u32[]{:S(2)}) collective-permute-start(bf16[144,768]{1,0:T(8,128)(2,1)S(1)} %get-tuple-element.251), channel_id=1, source_target_pairs={{0,24},{4,28},{8,16},{12,20},{16,8},{20,12},{24,0},{28,4},{1,25},{... | collective-permute-start | bytes 663560 | tf_op jit(solution)/shard_map/ppermute | solution.py:390
  208.0 22.3 %collective-permute-start.36 = (bf16[48,1920]{1,0:T(8,128)(2,1)S(1)}, bf16[48,1920]{1,0:T(8,128)(2,1)S(1)}, u32[]{:S(2)}, u32[]{:S(2)}) collective-permute-start(bf16[48,1920]{1,0:T(8,128)(2,1)S(1)} %get-tuple-element.269.refs_0_), channel_id=1, source_target_pairs={{0,8},{4,12},{8,0},{12,4},{16,24},{20,28},{24,16},{28,20},{1,9},{5... | collective-permute-start | bytes 552968 | tf_op jit(solution)/shard_map/ppermute | solution.py:390
  208.9 21.3 %collective-permute-start.37 = (bf16[48,1920]{1,0:T(8,128)(2,1)S(1)}, bf16[48,1920]{1,0:T(8,128)(2,1)S(1)}, u32[]{:S(2)}, u32[]{:S(2)}) collective-permute-start(bf16[48,1920]{1,0:T(8,128)(2,1)S(1)} %get-tuple-element.269.refs_0_), channel_id=1, source_target_pairs={{0,16},{4,20},{8,24},{12,28},{16,0},{20,4},{24,8},{28,12},{1,17},{... | collective-permute-start | bytes 552968 | tf_op jit(solution)/shard_map/ppermute | solution.py:390
  210.4 19.9 %collective-permute-start.38 = (bf16[48,1920]{1,0:T(8,128)(2,1)S(1)}, bf16[48,1920]{1,0:T(8,128)(2,1)S(1)}, u32[]{:S(2)}, u32[]{:S(2)}) collective-permute-start(bf16[48,1920]{1,0:T(8,128)(2,1)S(1)} %get-tuple-element.269.refs_0_), channel_id=1, source_target_pairs={{0,24},{4,28},{8,16},{12,20},{16,8},{20,12},{24,0},{28,4},{1,25},{... | collective-permute-start | bytes 552968 | tf_op jit(solution)/shard_map/ppermute | solution.py:390
  (55 other events, 316.5 us)

commit v3 on v2

--- a/solution.py
+++ b/solution.py
@@ -414,35 +414,79 @@
 
 
 def local_call(
-    body, outs, where, args, far=(), far_outs=(), scalar=None, scratch=(), after=(), vmem=12, cost=0
+    body,
+    outs,
+    where,
+    args,
+    far=(),
+    far_outs=(),
+    fetch=(),
+    store=(),
+    scalar=None,
+    scratch=(),
+    after=(),
+    vmem=14,
+    cost=0,
 ):
+    fetch, store = list(fetch), list(store)
     args = [
-        pltpu.with_memory_space_constraint(a, pltpu.HBM) if i in far else a
+        pltpu.with_memory_space_constraint(a, pltpu.HBM) if i in far or i in fetch else a
         for i, a in enumerate(args)
     ]
     after = list(after)
     many = isinstance(outs, tuple)
     outs = outs if many else (outs,)
-    count, made = len(args), len(outs)
+    count, made, moved = len(args), len(outs), len(fetch) + len(store)
+    held = [pltpu.VMEM(args[i].shape, args[i].dtype) for i in fetch]
+    held += [pltpu.VMEM(outs[i].shape, outs[i].dtype) for i in store]
+    if moved:
+        held.append(pltpu.SemaphoreType.DMA((moved,)))
 
     def kernel(where_ref, *refs):
-        token = refs[count + len(after) + made]
+        start = count + len(after)
+        given, results = list(refs[:count]), list(refs[start : start + made])
+        token, extra = refs[start + made], refs[start + made + 1 :]
+        extra, copied = extra[: len(extra) - len(held)], extra[len(extra) - len(held) :]
         token[...] = jnp.zeros(token.shape, token.dtype)
-        start = count + len(after)
-        body(where_ref, *refs[:count], *refs[start : start + made], *refs[start + made + 1 :])
+        into = [
+            pltpu.make_async_copy(given[i], copied[n], copied[-1].at[n])
+            for n, i in enumerate(fetch)
+        ]
+        out_of = [
+            pltpu.make_async_copy(copied[n], results[i], copied[-1].at[n])
+            for n, i in enumerate(store, len(fetch))
+        ]
+        for copy in into:
+            copy.start()
+        for n, i in enumerate(fetch):
+            given[i] = copied[n]
+        for n, i in enumerate(store, len(fetch)):
+            results[i] = copied[n]
+        for copy in into:
+            copy.wait()
+        body(where_ref, *given, *results, *extra)
+        for copy in out_of:
+            copy.start()
+        for copy in out_of:
+            copy.wait()
 
     def place(i):
-        return HBM if i in far_outs else SMEM if i == scalar else VMEM
+        return HBM if i in far_outs or i in store else SMEM if i == scalar else VMEM
 
     results = pl.pallas_call(
         kernel,
         out_shape=(
-            *(pltpu.HBM(o.shape, o.dtype) if i in far_outs else o for i, o in enumerate(outs)),
+            *(
+                pltpu.HBM(o.shape, o.dtype) if i in far_outs or i in store else o
+                for i, o in enumerate(outs)
+            ),
             wide(8, 128),
         ),
-        in_specs=[SMEM] + [HBM if i in far else VMEM for i in range(count)] + [ANY] * len(after),
+        in_specs=[SMEM]
+        + [HBM if i in far or i in fetch else VMEM for i in range(count)]
+        + [ANY] * len(after),
         out_specs=(*(place(i) for i in range(made)), VMEM),
-        scratch_shapes=scratch,
+        scratch_shapes=[*scratch, *held],
         compiler_params=pltpu.CompilerParams(vmem_limit_bytes=vmem << 20),
         cost_estimate=pl.CostEstimate(
             flops=cost * 10**9, transcendentals=0, bytes_accessed=cost * 10**6
@@ -542,28 +586,29 @@
     out[:, 3 * feat :] = jnp.concatenate(lines, axis=0).astype(out.dtype)
 
 
-def pack_blocks(where, up, output, down, out_up, out_down, sems):
+def pack_down(where, down, out, sem):
+    part = out.shape[0]
+    rows = rows_at(4 * part * where[1] + part * where[0], part, 32)
+    copy = pltpu.make_async_copy(down.at[rows], out, sem)
+    copy.start()
+    copy.wait()
+
+
+def pack_blocks(where, up, output, out_up, sems):
     chip, core = where[0], where[1]
     part, units = out_up.shape[0] // 4, out_up.shape[1] // 5
     rows = rows_at(part * chip, part, 16)
-    down_part = out_down.shape[0]
-    copies = []
-    for p in range(4):
-        block = slice(part * p, part * (p + 1))
-        copies += [
-            (
-                up.at[rows, rows_at(2 * units * i + units * core, units, 128)],
-                out_up.at[block, units * i : units * (i + 1)],
-            )
-            for i in range(4)
-        ]
-        copies.append(
-            (output.at[rows, rows_at(units * core, units, 128)], out_up.at[block, 4 * units :])
+    pairs = [
+        (
+            up.at[rows, rows_at(2 * units * i + units * core, units, 128)],
+            out_up.at[:part, units * i : units * (i + 1)],
         )
-    copies.append(
-        (down.at[rows_at(4 * down_part * core + down_part * chip, down_part, 32)], out_down)
-    )
-    run_copies(copies, sems)
+        for i in range(4)
+    ]
+    pairs.append((output.at[rows, rows_at(units * core, units, 128)], out_up.at[:part, 4 * units :]))
+    run_copies(pairs, sems)
+    for p in (1, 2, 3):
+        out_up[part * p : part * (p + 1), :] = out_up[:part, :]
 
 
 def stack_rows(where, *refs):
@@ -597,37 +642,33 @@
     units, shard = up.shape[1] // 8, up.shape[0]
     part = shard // 4
     own = rows_at(shard * plane, shard, 64)
-    copies = [
-        pltpu.make_async_copy(
+    pairs = [
+        (
             up.at[:, rows_at(2 * units * i + units * core, units, 128)],
             out.at[own, units * i : units * (i + 1)],
-            sems.at[i],
         )
         for i in range(4)
     ]
-    for copy in copies:
-        copy.start()
     for k, s, offset, count, piece, start in three_blocks((p0, p1, p2, p3, p4), part):
         at = rows_at(shard * (plane ^ s) + part * (chip ^ k) + offset, count, 16)
-        out[at, :] = piece[start : start + count, : 4 * units]
-    for copy in copies:
-        copy.wait()
-
-
-def build_half(where, output, p0, p1, p2, p3, p4, out, sem):
+        pairs.append((piece.at[start : start + count, : 4 * units], out.at[at]))
+    run_copies(pairs, sems)
+
+
+def build_half(where, output, p0, p1, p2, p3, p4, out, sems):
     chip, core, plane = where[0], where[1], where[2]
     shard, units = output.shape[0], out.shape[1]
     part = shard // 4
-    own = pltpu.make_async_copy(
-        output.at[:, rows_at(units * core, units, 128)],
-        out.at[rows_at(shard * plane, shard, 64)],
-        sem,
-    )
-    own.start()
+    pairs = [
+        (
+            output.at[:, rows_at(units * core, units, 128)],
+            out.at[rows_at(shard * plane, shard, 64)],
+        )
+    ]
     for k, s, offset, count, piece, start in three_blocks((p0, p1, p2, p3, p4), part):
         at = rows_at(shard * (plane ^ s) + part * (chip ^ k) + offset, count, 16)
-        out[at, :] = piece[start : start + count, 4 * units :]
-    own.wait()
+        pairs.append((piece.at[start : start + count, 4 * units :], out.at[at]))
+    run_copies(pairs, sems)
 
 
 def build_down(where, down, p0, p1, p2, p3, p4, out, sem):
@@ -940,7 +981,7 @@
 def down_grads(where, act, d_down, *refs):
     outs, total = refs[:5], refs[5]
     count = outs[0].shape[0] // 4
-    total[...] = dot(act[...], d_down[...], TN)
+    total[...] = dot(act[...], d_down[...], TN).astype(BF16)
 
     def block(j, p):
         return total[rows_at(4 * count * p + count * j, count, 32), :]
@@ -948,19 +989,24 @@
     split_chips(where[0], block, outs, count)
 
 
-def up_grads(where, h_pair, d_up, mixed, d_attn, *refs):
+def output_grads(where, mixed, d_attn, kept, given):
+    core = where[1]
+    rows, width = d_attn.shape
+    feat, units = mixed.shape[1], width // 2
+    mine = d_attn[:, rows_at(units * core, units, 128)]
+    others = d_attn[:, rows_at(units * (1 - core), units, 128)]
+    for j in range(4):
+        at = slice(feat * j, feat * (j + 1))
+        piece = mixed[(rows + 16) * j : (rows + 16) * j + rows, :]
+        kept[at, :] = dot(piece, mine, TN).astype(BF16)
+        given[at, :] = dot(piece, others, TN).astype(BF16)
+
+
+def up_grads(where, h_pair, d_up, kept, given, *refs):
     outs, total = refs[:5], refs[5]
     count, units = outs[0].shape[0] // 4, d_up.shape[1]
-    total[:, :units] = dot(h_pair[...], d_up[...], TN)
-    rows, width = d_attn.shape[0] // 2, d_attn.shape[1]
-    feat = mixed.shape[1]
-    columns = d_attn[:, rows_at(width // 2 * where[1], width // 2, 128)]
-    for j in range(4):
-        product = 0.0
-        for i in range(2):
-            start = 4 * (rows + 16) * i + (rows + 16) * j
-            product += dot(mixed[start : start + rows, :], columns[rows * i : rows * (i + 1), :], TN)
-        total[feat * j : feat * (j + 1), units:] = product
+    total[:, :units] = dot(h_pair[...], d_up[...], TN).astype(BF16)
+    total[:, units:] = (kept[...].astype(F32) + given[...].astype(F32)).astype(BF16)
 
     def block(j, p):
         return total[rows_at(4 * count * p + count * j, count, 16), :]
@@ -1056,8 +1102,7 @@
         ]
         small = jnp.concatenate(lines, axis=0).astype(BF16)
         block = slice(half * p, half * (p + 1))
-        arrived = given[rows_at(4 * half * (1 - where[1]) + half * p, half, 32), :]
-        total = (kept[block, :].astype(F32) + arrived.astype(F32)).astype(BF16)
+        total = (kept[block, :].astype(F32) + given[block, :].astype(F32)).astype(BF16)
         out[block, : 3 * feat] = total
         out[block, 3 * feat :] = small
 
@@ -1177,12 +1222,12 @@
         second_shift,
         down_bias,
     )
-    up_piece, down_piece = step(
+    up_piece = step(
         pack_blocks,
-        (shaped(4 * quarter, 5 * core_units), shaped(part_units, width)),
-        (up_weight, output_weight, down_weight),
-        far=range(3),
-        scratch=[dma((21,))],
+        shaped(4 * quarter, 5 * core_units),
+        (up_weight, output_weight),
+        far=range(2),
+        scratch=[dma((5,))],
     )
     up_far = trade_planes(up_piece)
     bundle = step(pack_tokens, shaped(rows + 16, width), (own, segment_ids, valid_rows), cost=50)
@@ -1222,6 +1267,9 @@
         return (*three, swap_chips(to_x, 1), swap_chips(to_y, 2))
 
     up_all = all_chips(up_three, up_far.shape[0] // 32 * 16 + 16)
+    down_piece = step(
+        pack_down, shaped(part_units, width), (down_weight,), far=(0,), scratch=[dma]
+    )
     down_far = [swap_planes(down_piece, s) for s in steps]
 
     h_one, w_three, projected, probs, mixed, sent, vectors, b_up = step(
@@ -1257,12 +1305,12 @@
         build_half,
         shaped(width, core_units),
         (output_weight, *up_all),
-        far=(0,),
-        scratch=[dma],
+        far=range(6),
+        scratch=[dma((20,))],
     )
     out_far = swap_cores(out_near)
     w_up = step(
-        build_up, shaped(width, units), (up_weight, *up_all), far=(0,), scratch=[dma((4,))], cost=50
+        build_up, shaped(width, units), (up_weight, *up_all), far=range(6), scratch=[dma((20,))], cost=50
     )
     w_output = step(build_output, shaped(width, width), (out_near, out_far))
 
@@ -1272,7 +1320,6 @@
         (mixed_low, w_output, own, vectors),
     )
     h_pair = both_cores(h_two)
-    mixed_pair = both_cores(mixed_low)
     down_all = all_chips(down_far, down_far[0].shape[0] // 2)
     act, slope = step(
         activate,
@@ -1304,16 +1351,18 @@
     def five(count, lanes):
         return (shaped(4 * count, lanes),) * 3 + (shaped(2 * count, lanes),) * 2
 
-    def onward(parts, arrived):
+    def onward(parts, arrived, fetch):
         count, lanes = parts[3].shape
-        to_x, to_y = step(pass_on, (shaped(count, lanes),) * 2, (*arrived, *parts[3:]), cost=50)
+        to_x, to_y = step(
+            pass_on, (shaped(count, lanes),) * 2, (*arrived, *parts[3:]), fetch=fetch, cost=50
+        )
         return (parts[0], *arrived, swap_chips(to_x, 1), swap_chips(to_y, 2))
 
     down_parts = step(
         down_grads,
         five(part_units, width),
         (act, d_down),
-        scratch=[pltpu.VMEM((units, width), F32)],
+        scratch=[pltpu.VMEM((units, width), BF16)],
         vmem=24,
     )
     down_arrived = swap_chips(down_parts[1], 1), swap_chips(down_parts[2], 2)
@@ -1330,15 +1379,22 @@
     )
     d_mixed = trade_chips(d_sent)
 
-    down_sums = onward(down_parts, down_arrived)
-    attn_pair = both_cores(d_attn)
+    kept_out, given_out = step(
+        output_grads,
+        (shaped(width, core_units), shaped(width, core_units)),
+        (mixed_low, d_attn),
+        cost=1,
+    )
+    given_out = swap_cores(given_out)
+    down_sums = onward(down_parts, down_arrived, ())
     up_parts = step(
         up_grads,
         five(quarter, 5 * core_units),
-        (h_pair, d_up, mixed_pair, attn_pair),
-        scratch=[pltpu.VMEM((width, 5 * core_units), F32)],
+        (h_pair, d_up, kept_out, given_out),
+        store=(0, 3, 4),
+        scratch=[pltpu.VMEM((width, 5 * core_units), BF16)],
         vmem=24,
-        cost=2,
+        cost=5,
     )
     up_arrived = swap_chips(up_parts[1], 1), swap_chips(up_parts[2], 2)
     down_planes = trade_planes(step(sum_chips, shaped(4 * part_units, width), down_sums))
@@ -1354,6 +1410,7 @@
         ),
         (d_mixed, vectors, h_one, w_three, projected, probs, mixed),
         far=range(2, 7),
+        store=(2, 3),
         scratch=[
             pltpu.VMEM((every, 3 * feat), BF16),
             pltpu.VMEM((group, every), BF16),
@@ -1368,13 +1425,13 @@
         vmem=28,
         cost=50,
     )
-    d_far = swap_cores(d_far)
-    up_sums = onward(up_parts, up_arrived)
-    given = both_cores(given)
+    given, d_far = swap_cores(given), swap_cores(d_far)
+    up_sums = onward(up_parts, up_arrived, (2, 3))
     arrived, down_planes = step(
         pack_gradients,
         (shaped(4 * half, width), shaped(part_units, width)),
         (kept, given, from_attention, from_second, from_result, up_line, down_planes),
+        fetch=(0, 1),
         cost=1,
     )
     arrived = trade_planes(arrived)
@@ -1389,15 +1446,18 @@
         send_planes,
         (shaped(quarter, 5 * core_units),) * 4,
         up_sums,
+        fetch=(0,),
         scratch=[pltpu.VMEM((4 * quarter, 5 * core_units), F32)],
         cost=50,
     )
     up_planes = [up_planes[0]] + [swap_planes(up_planes[s], s) for s in steps]
-    shares = step(share_inputs, (shaped(rows, width),) * 4, (d_near, d_far), cost=50)
+    shares = step(share_inputs, (shaped(rows, width),) * 4, (d_near, d_far), store=(0,), cost=50)
     shares = [shares[0]] + [swap_chips(shares[k], k) for k in steps]
     both = trade_chips(step(sum_planes, shaped(8 * half, width), (arrived, down_planes), cost=50))
     up_near = spread(step(sum_pieces, shaped(quarter, 5 * core_units), up_planes, cost=50))
-    grad_tokens = step(finish_inputs, shaped(rows, width), (*shares, own, d_second, vectors), cost=50)
+    grad_tokens = step(
+        finish_inputs, shaped(rows, width), (*shares, own, d_second, vectors), fetch=(0, 4), cost=50
+    )
     both = (both, swap_cores(both))
     finished = step(
         finish_projections,
@@ -1408,7 +1468,6 @@
         (*both, count),
         scratch=[pltpu.VMEM((8, 16, feat), F32), pltpu.VMEM((8, own_units), F32)],
         scalar=3,
-        cost=50,
     )
     grad_down_weight = step(
         finish_down,

time: 238 us -> 226 us (0.950)
  local copies, waits for them, and re-layouts: 14.1 us -> 5.49 us
  Pallas kernels: 85.2 us -> 93.4 us
  blocking collectives: 16 us -> 8.47 us
    unnamed x82 -> x78, local copies, waits for them, and re-layouts: 14.1 us -> 5.49 us
    pallas_call x37 -> x39, Pallas kernels: 85.2 us -> 93.4 us  [local_call(): pl.pallas_call(kernel, out_shape=(*(pltpu.HBM(o.shape, o.dtype) if i in f...]
    all_gather x7 -> x4, blocking collectives: 16 us -> 8.47 us  [both_cores(): lax.all_gather(value, 'ctx', axis=0, tiled=True, axis_index_groups=pairs)]
    all_to_all x3, starting transfers between devices: 22 us -> 14.9 us  [trade_planes(): return lax.all_to_all(value, 'fsdp', 0, 0, tiled=True)]
    ppermute x9, starting transfers between devices: 10.4 us -> 13.3 us  [swap_planes(): return lax.ppermute(value, 'fsdp', [(i, i ^ step) for i in range(size)])]
    all_to_all x3, waiting for transfers between devices: 9.89 us -> 12.6 us  [trade_chips(): lax.all_to_all(value, 'ctx', 0, 0, axis_index_groups=groups, tiled=True)]
  transfers between devices with their start and end apart: 46 -> 48, of which waited for: 12 -> 18; matrix products, arithmetic and copies ran while one was open for 0% -> 0% of each run, Pallas kernels for 29% -> 35%
where the time goes in v3:
time: 226 us; the launch traced here: 225 us
  Pallas kernels  93.4 us (41%)
  starting transfers between devices  72 us (32%)
  waiting for transfers between devices  44.1 us (20%)
  blocking collectives  8.47 us (4%)
  local copies, waits for them, and re-layouts  5.49 us (2%)
    pallas_call x39, Pallas kernels, local_call(): pl.pallas_call(kernel, out_shape=(*(pltpu.HBM(o.shape, o.dtype) if i in f...  93.4 us
    ppermute x25, starting transfers between devices, swap_chips(): return lax.ppermute(value, 'ctx', [(i, i ^ 2 * step) for i in range(size)])  31.7 us
    all_to_all x3, starting transfers between devices, trade_planes(): return lax.all_to_all(value, 'fsdp', 0, 0, tiled=True)  14.9 us
    ppermute x25, waiting for transfers between devices, swap_chips(): return lax.ppermute(value, 'ctx', [(i, i ^ 2 * step) for i in range(size)])  14 us
    ppermute x9, starting transfers between devices, swap_planes(): return lax.ppermute(value, 'fsdp', [(i, i ^ step) for i in range(size)])  13.3 us
    all_to_all x3, waiting for transfers between devices, trade_chips(): lax.all_to_all(value, 'ctx', 0, 0, axis_index_groups=groups, tiled=True)  12.6 us
    all_to_all x3, starting transfers between devices, trade_chips(): lax.all_to_all(value, 'ctx', 0, 0, axis_index_groups=groups, tiled=True)  11.4 us
    ppermute x9, waiting for transfers between devices, swap_planes(): return lax.ppermute(value, 'fsdp', [(i, i ^ step) for i in range(size)])  9.44 us
  transfers between devices with their start and end apart: 48, of which 18 were waited for; matrix products, arithmetic and copies ran while one was open for 0% of the time, Pallas kernels for 35%

profile of v3, /device:TPU:0, one launch (start us, length us, event | category | flops | bytes accessed | tf_op | source)
XLA Modules:
  0.0 225.2 jit_solution(11450538179851324787)
XLA Ops:
  0.8 2.3 %shard_map.331 = (bf16[192,1920]{1,0:T(8,128)(2,1)}, f32[8,128]{1,0:T(8,128)S(1)}) custom-call(s32[3]{0:T(128)S(1)} %pad_add_fusion.where_ref, bf16[192,3072]{1,0:T(8,128)(2,1)} %refs_0_.10, bf16[192,768]{1,0:T(8,128)(2,1)} %refs_0_.9), custom_call_target="tpu_custom_call" | custom-call | tf_op jit(solution)/shard_map/pallas_call | solution.py:476
  3.1 6.3 %all-to-all-start = ((bf16[4,48,1920]{2,1,0:T(8,128)(2,1)}), bf16[4,48,1920]{2,1,0:T(8,128)(2,1)S(1)}, u32[]{:S(2)}, u32[]{:S(2)}) async-start(bf16[4,48,1920]{2,1,0:T(8,128)(2,1)} %bitcast.4), calls=%async_computation | async-start | bytes 1474560 | tf_op jit(solution)/shard_map/all_to_all | solution.py:405
  10.0 2.5 %collective-permute-start.2 = (bf16[160,768]{1,0:T(8,128)(2,1)S(1)}, bf16[160,768]{1,0:T(8,128)(2,1)S(1)}, u32[]{:S(2)}, u32[]{:S(2)}) collective-permute-start(bf16[160,768]{1,0:T(8,128)(2,1)S(1)} %get-tuple-element.155.refs_0_), channel_id=1, source_target_pairs={{0,24},{4,28},{8,16},{12,20},{16,8},{20,12},{24,0},{28,4},{1,25},{... | collective-permute-start | bytes 737288 | tf_op jit(solution)/shard_map/ppermute | solution.py:390
  15.6 4.4 %collective-permute-done.2.refs_3_ = bf16[160,768]{1,0:T(8,128)(2,1)S(1)} collective-permute-done((bf16[160,768]{1,0:T(8,128)(2,1)S(1)}, bf16[160,768]{1,0:T(8,128)(2,1)S(1)}, u32[]{:S(2)}, u32[]{:S(2)}) %collective-permute-start.2) | collective-permute-done | bytes 245792 | tf_op jit(solution)/shard_map/ppermute | solution.py:390
  19.9 3.8 %collective-permute-done.1.refs_2_ = bf16[160,768]{1,0:T(8,128)(2,1)S(1)} collective-permute-done((bf16[160,768]{1,0:T(8,128)(2,1)S(1)}, bf16[160,768]{1,0:T(8,128)(2,1)S(1)}, u32[]{:S(2)}, u32[]{:S(2)}) %collective-permute-start.1) | collective-permute-done | bytes 245792 | tf_op jit(solution)/shard_map/ppermute | solution.py:390
  24.5 4.0 %all-to-all-done = bf16[4,48,1920]{2,1,0:T(8,128)(2,1)S(1)} async-done(((bf16[4,48,1920]{2,1,0:T(8,128)(2,1)}), bf16[4,48,1920]{2,1,0:T(8,128)(2,1)S(1)}, u32[]{:S(2)}, u32[]{:S(2)}) %all-to-all-start) | async-done | bytes 737312 | tf_op jit(solution)/shard_map/all_to_all | solution.py:405
  33.7 2.9 %collective-permute-start.4 = (bf16[96,768]{1,0:T(8,128)(2,1)S(1)}, bf16[96,768]{1,0:T(8,128)(2,1)S(1)}, u32[]{:S(2)}, u32[]{:S(2)}) collective-permute-start(bf16[96,768]{1,0:T(8,128)(2,1)S(1)} %get-tuple-element.165.refs_0_.refs_3_), channel_id=1, source_target_pairs={{0,1},{1,0},{2,3},{3,2},{4,5},{5,4},{6,7},{7,6},{8,9},{9,8},{10,11... | collective-permute-start | bytes 442376 | tf_op jit(solution)/shard_map/ppermute | solution.py:395
  36.6 2.4 %shard_map.336 = (f32[1152,768]{1,0:T(8,128)S(1)}, f32[8,1152]{1,0:T(8,128)S(1)}, f32[576,128]{1,0:T(8,128)S(1)}, f32[8,128]{1,0:T(8,128)S(1)}) custom-call(s32[3]{0:T(128)S(1)} %pad_add_fusion.where_ref, bf16[640,768]{1,0:T(8,128)(2,1)S(1)} %get-tuple-element.158.refs_0_, bf16[640,768]{1,0:T(8,128)(2,1)} %collective-permute-done.3.refs_1_, ...), custom_call_target="tpu_custom_call" | custom-call | flops 1000000000 | bytes 1000000 | tf_op jit(solution)/shard_map/pallas_call | solution.py:476
  40.8 4.2 %collective-permute-done.5.refs_2_.refs_5_ = bf16[96,768]{1,0:T(8,128)(2,1)S(1)} collective-permute-done((bf16[96,768]{1,0:T(8,128)(2,1)S(1)}, bf16[96,768]{1,0:T(8,128)(2,1)S(1)}, u32[]{:S(2)}, u32[]{:S(2)}) %collective-permute-start.5) | collective-permute-done | bytes 147488 | tf_op jit(solution)/shard_map/ppermute | solution.py:395
  53.6 10.5 %shard_map.340 = (bf16[1152,768]{1,0:T(8,128)(2,1)}, bf16[768,576]{1,0:T(8,128)(2,1)}, bf16[1152,576]{1,0:T(8,128)(2,1)}, bf16[3,576,1152]{2,1,0:T(8,128)(2,1)},...) custom-call(s32[3]{0:T(128)S(1)} %pad_add_fusion.where_ref, ...), custom_call_target="tpu_custom_call" | custom-call | flops 49999998976 | bytes 50000000 | tf_op jit(solution)/shard_map/pallas_call | solution.py:476
  69.1 4.3 %all-to-all-start.1 = ((bf16[4,160,192]{2,1,0:T(8,128)(2,1)}), bf16[4,160,192]{2,1,0:T(8,128)(2,1)}, u32[]{:S(2)}, u32[]{:S(2)}) async-start(bf16[4,160,192]{2,1,0:T(8,128)(2,1)} %bitcast.6), calls=%async_computation.1 | async-start | bytes 655360 | tf_op jit(solution)/shard_map/all_to_all | solution.py:401
  76.1 2.4 %shard_map.343 = (bf16[768,1536]{1,0:T(8,128)(2,1)S(1)}, f32[8,128]{1,0:T(8,128)S(1)}) custom-call(s32[3]{0:T(128)S(1)} %pad_add_fusion.where_ref, bf16[192,3072]{1,0:T(8,128)(2,1)} %refs_0_.10, bf16[144,1920]{1,0:T(8,128)(2,1)} %copy-done.4, bf16[144,1920]{1,0:T(8,128)(2,1)} %copy-done.6, bf16[144,1920]{1,0:T(8,128)(2,1)} %copy-done.5, ...), custom_call_target="tpu_custom_call" | custom-call | flops 49999998976 | bytes 50000000 | tf_op jit(solution)/shard_map/pallas_call | solution.py:476
  79.2 3.1 %all-to-all-done.1 = bf16[4,160,192]{2,1,0:T(8,128)(2,1)} async-done(((bf16[4,160,192]{2,1,0:T(8,128)(2,1)}), bf16[4,160,192]{2,1,0:T(8,128)(2,1)}, u32[]{:S(2)}, u32[]{:S(2)}) %all-to-all-start.1) | async-done | bytes 245792 | tf_op jit(solution)/shard_map/all_to_all | solution.py:401
  94.3 2.4 %shard_map.348 = (bf16[1536,768]{1,0:T(8,128)(2,1)S(1)}, f32[8,128]{1,0:T(8,128)S(1)}) custom-call(s32[3]{0:T(128)S(1)} %pad_add_fusion.where_ref, bf16[768,768]{1,0:T(8,128)(2,1)} %refs_0_.11, bf16[288,768]{1,0:T(8,128)(2,1)} %get-tuple-element.188.refs_1_, bf16[288,768]{1,0:T(8,128)(2,1)} %collective-permute-done.16.refs_0_.refs_2_, ...), custom_call_target="tpu_custom_call" | custom-call | tf_op jit(solution)/shard_map/pallas_call | solution.py:476
  103.8 3.1 %shard_map.351 = (bf16[384,768]{1,0:T(8,128)(2,1)S(1)}, bf16[384,768]{1,0:T(8,128)(2,1)}, bf16[384,768]{1,0:T(8,128)(2,1)}, bf16[192,768]{1,0:T(8,128)(2,1)S(1)}...) custom-call(s32[3]{0:T(128)S(1)} %pad_add_fusion.where_ref, bf16[288,1536]{1,0:T(8,128)(2,1)S(1)} %get-tuple-element.191.refs_0_, ...), custom_call_target="tpu_custom_call" | custom-call | tf_op jit(solution)/shard_map/pallas_call | solution.py:476
  108.5 3.8 %shard_map.352 = (bf16[288,1536]{1,0:T(8,128)(2,1)S(1)}, f32[144,768]{1,0:T(8,128)S(1)}, bf16[144,768]{1,0:T(8,128)(2,1)S(1)}, f32[1,1536]{1,0:T(1,128)S(1)}, f32[8,128]{1,0:T(8,128)S(1)}) custom-call(s32[3]{0:T(128)S(1)} %pad_add_fusion.where_ref, bf16[288,768]{1,0:T(8,128)(2,1)S(1)} %all_gather.14.refs_1_.refs_0_, ...), custom_call_target="tpu_custom_call" | custom-call | flops 49999998976 | bytes 50000000 | tf_op jit(solution)/shard_map/pallas_call | solution.py:476
  117.4 3.5 %all-to-all-start.2 = ((bf16[4,144,192]{2,1,0:T(8,128)(2,1)}), bf16[4,144,192]{2,1,0:T(8,128)(2,1)S(1)}, u32[]{:S(2)}, u32[]{:S(2)}) async-start(bf16[4,144,192]{2,1,0:T(8,128)(2,1)} %bitcast.11), calls=%async_computation.2 | async-start | bytes 589824 | tf_op jit(solution)/shard_map/all_to_all | solution.py:401
  127.7 4.5 %shard_map.356 = (bf16[192,1920]{1,0:T(8,128)(2,1)}, bf16[192,1920]{1,0:T(8,128)(2,1)}, bf16[192,1920]{1,0:T(8,128)(2,1)}, bf16[96,1920]{1,0:T(8,128)(2,1)}, bf1...) custom-call(s32[3]{0:T(128)S(1)} %pad_add_fusion.where_ref, bf16[288,768]{1,0:T(8,128)(2,1)S(1)} %copy-done.1, ...), custom_call_target="tpu_custom_call" | custom-call | flops 5000000000 | bytes 5000000 | tf_op jit(solution)/shard_map/pallas_call | solution.py:476
  135.4 2.3 %shard_map.357 = (bf16[384,768]{1,0:T(8,128)(2,1)}, f32[8,128]{1,0:T(8,128)S(1)}) custom-call(s32[3]{0:T(128)S(1)} %pad_add_fusion.where_ref, bf16[384,768]{1,0:T(8,128)(2,1)S(1)} %copy-done.3, bf16[384,768]{1,0:T(8,128)(2,1)} %collective-permute-done.20.refs_0_.refs_1_, bf16[384,768]{1,0:T(8,128)(2,1)} %collective-permute-done.21.refs_1_.refs_2_, ...), custom_call_target="tpu_custom_call" | custom-call | tf_op jit(solution)/shard_map/pallas_call | solution.py:476
  137.6 3.7 %all-to-all-start.3 = ((bf16[4,96,768]{2,1,0:T(8,128)(2,1)}), bf16[4,96,768]{2,1,0:T(8,128)(2,1)S(1)}, u32[]{:S(2)}, u32[]{:S(2)}) async-start(bf16[4,96,768]{2,1,0:T(8,128)(2,1)} %bitcast.13), calls=%async_computation.3 | async-start | bytes 1179648 | tf_op jit(solution)/shard_map/all_to_all | solution.py:405
  141.4 12.4 %shard_map.358 = (bf16[576,768]{1,0:T(8,128)(2,1)S(1)}, bf16[576,768]{1,0:T(8,128)(2,1)S(1)}, bf16[384,576]{1,0:T(8,128)(2,1)}, bf16[384,576]{1,0:T(8,128)(2,1)}...) custom-call(s32[3]{0:T(128)S(1)} %pad_add_fusion.where_ref, bf16[576,192]{1,0:T(8,128)(2,1)S(1)} %bitcast.27, ...), custom_call_target="tpu_custom_call" | custom-call | flops 49999998976 | bytes 50000000 | tf_op jit(solution)/shard_map/pallas_call | solution.py:476
  153.9 2.7 %shard_map.359 = (bf16[96,1920]{1,0:T(8,128)(2,1)}, bf16[96,1920]{1,0:T(8,128)(2,1)}, f32[8,128]{1,0:T(8,128)S(1)}) custom-call(s32[3]{0:T(128)S(1)} %pad_add_fusion.where_ref, bf16[192,1920]{1,0:T(8,128)(2,1)S(1)} %collective-permute-done.26.refs_0_.refs_1_, bf16[192,1920]{1,0:T(8,128)(2,1)S(1)} %collective-permute-done.27.refs_1_.refs_2_, ...), custom_call_target="tpu_custom_call" | custom-call | flops 49999998976 | bytes 50000000 | tf_op jit(solution)/shard_map/pallas_call | solution.py:476
  159.1 2.9 %shard_map.360 = (bf16[384,768]{1,0:T(8,128)(2,1)}, bf16[96,768]{1,0:T(8,128)(2,1)S(1)}, f32[8,128]{1,0:T(8,128)S(1)}) custom-call(s32[3]{0:T(128)S(1)} %pad_add_fusion.where_ref, bf16[384,576]{1,0:T(8,128)(2,1)} %get-tuple-element.232.refs_0_, bf16[384,576]{1,0:T(8,128)(2,1)} %collective-permute-done.25.refs_1_, f32[8,768]{1,0:T(8,128)S(1)} %get-tuple-element.234.refs_2_, ...), custom_call_target="tpu_custom_call" | custom-call | flops 1000000000 | bytes 1000000 | tf_op jit(solution)/shard_map/pallas_call | solution.py:476
  162.0 4.8 %all-to-all-start.4 = ((bf16[4,96,768]{2,1,0:T(8,128)(2,1)}), bf16[4,96,768]{2,1,0:T(8,128)(2,1)S(1)}, u32[]{:S(2)}, u32[]{:S(2)}) async-start(bf16[4,96,768]{2,1,0:T(8,128)(2,1)} %bitcast.15), calls=%async_computation.4 | async-start | bytes 1179648 | tf_op jit(solution)/shard_map/all_to_all | solution.py:405
  169.6 3.5 %shard_map.361 = (bf16[48,1920]{1,0:T(8,128)(2,1)S(1)}, bf16[48,1920]{1,0:T(8,128)(2,1)}, bf16[48,1920]{1,0:T(8,128)(2,1)}, bf16[48,1920]{1,0:T(8,128)(2,1)}, f32[8,128]{1,0:T(8,128)S(1)}) custom-call(s32[3]{0:T(128)S(1)} %pad_add_fusion.where_ref, bf16[192,1920]{1,0:T(8,128)(2,1)} %get-tuple-element.249.refs_0_, ...), custom_call_target="tpu_custom_call" | custom-call | flops 49999998976 | bytes 50000000 | tf_op jit(solution)/shard_map/pallas_call | solution.py:476
  174.9 2.4 %collective-permute-start.36 = (bf16[48,1920]{1,0:T(8,128)(2,1)}, bf16[48,1920]{1,0:T(8,128)(2,1)}, u32[]{:S(2)}, u32[]{:S(2)}) collective-permute-start(bf16[48,1920]{1,0:T(8,128)(2,1)} %get-tuple-element.263), channel_id=1, source_target_pairs={{0,2},{1,3},{2,0},{3,1},{4,6},{5,7},{6,4},{7,5},{8,10},{9,11},{10,... | collective-permute-start | bytes 552968 | tf_op jit(solution)/shard_map/ppermute | solution.py:395
  186.1 3.7 %all-to-all-start.5 = ((bf16[4,192,768]{2,1,0:T(8,128)(2,1)}), bf16[4,192,768]{2,1,0:T(8,128)(2,1)S(1)}, u32[]{:S(2)}, u32[]{:S(2)}) async-start(bf16[4,192,768]{2,1,0:T(8,128)(2,1)} %bitcast.17), calls=%async_computation.5 | async-start | bytes 2359296 | tf_op jit(solution)/shard_map/all_to_all | solution.py:401
  189.7 2.9 %collective-permute-start.34 = (bf16[144,768]{1,0:T(8,128)(2,1)S(1)}, bf16[144,768]{1,0:T(8,128)(2,1)}, u32[]{:S(2)}, u32[]{:S(2)}) collective-permute-start(bf16[144,768]{1,0:T(8,128)(2,1)S(1)} %get-tuple-element.259), channel_id=1, source_target_pairs={{0,24},{4,28},{8,16},{12,20},{16,8},{20,12},{24,0},{28,4},{1,25},{... | collective-permute-start | bytes 663560 | tf_op jit(solution)/shard_map/ppermute | solution.py:390
  192.6 3.5 %collective-permute-done.36.refs_2_ = bf16[48,1920]{1,0:T(8,128)(2,1)} collective-permute-done((bf16[48,1920]{1,0:T(8,128)(2,1)}, bf16[48,1920]{1,0:T(8,128)(2,1)}, u32[]{:S(2)}, u32[]{:S(2)}) %collective-permute-start.36) | collective-permute-done | bytes 184352 | tf_op jit(solution)/shard_map/ppermute | solution.py:395
  200.9 9.5 %all-to-all-done.5 = bf16[4,192,768]{2,1,0:T(8,128)(2,1)S(1)} async-done(((bf16[4,192,768]{2,1,0:T(8,128)(2,1)}), bf16[4,192,768]{2,1,0:T(8,128)(2,1)S(1)}, u32[]{:S(2)}, u32[]{:S(2)}) %all-to-all-start.5) | async-done | bytes 1179680 | tf_op jit(solution)/shard_map/all_to_all | solution.py:401
  212.0 3.1 %shard_map.365 = (bf16[144,768]{1,0:T(8,128)(2,1)}, f32[8,128]{1,0:T(8,128)S(1)}) custom-call(s32[3]{0:T(128)S(1)} %pad_add_fusion.where_ref, bf16[144,768]{1,0:T(8,128)(2,1)} %get-tuple-element.256.refs_0_, bf16[144,768]{1,0:T(8,128)(2,1)S(1)} %collective-permute-done.32.refs_1_, bf16[144,768]{1,0:T(8,128)(2,1)S(1)} %collective-permute-done.33.refs_2_, ...), custom_call_target="tpu_custom_call" | custom-call | flops 49999998976 | bytes 50000000 | tf_op jit(solution)/shard_map/pallas_call | solution.py:476
  222.1 2.9 %shard_map.369 = (f32[192,3072]{1,0:T(8,128)}, f32[192,768]{1,0:T(8,128)}, f32[8,128]{1,0:T(8,128)}) custom-call(s32[3]{0:T(128)S(1)} %pad_add_fusion.where_ref, bf16[48,1920]{1,0:T(8,128)(2,1)S(1)} %get-tuple-element.277.refs_0_, bf16[48,1920]{1,0:T(8,128)(2,1)S(1)} %collective-permute-done.38.refs_1_, ...), custom_call_target="tpu_custom_call" | custom-call | tf_op jit(solution)/shard_map/pallas_call | solution.py:476
  (186 shorter events, 92.9 us)
Async XLA Ops:
  3.1 25.4 %all-to-all-start = ((bf16[4,48,1920]{2,1,0:T(8,128)(2,1)}), bf16[4,48,1920]{2,1,0:T(8,128)(2,1)S(1)}, u32[]{:S(2)}, u32[]{:S(2)}) async-start(bf16[4,48,1920]{2,1,0:T(8,128)(2,1)} %bitcast.4), calls=%async_computation | async-start | bytes 1474560 | tf_op jit(solution)/shard_map/all_to_all | solution.py:405
  29.1 16.6 %collective-permute-start.9 = (bf16[144,1920]{1,0:T(8,128)(2,1)S(1)}, bf16[144,1920]{1,0:T(8,128)(2,1)S(1)}, u32[]{:S(2)}, u32[]{:S(2)}) collective-permute-start(bf16[144,1920]{1,0:T(8,128)(2,1)S(1)} %get-tuple-element.168.refs_1_), channel_id=1, source_target_pairs={{0,16},{4,20},{8,24},{12,28},{16,0},{20,4},{24,8},{28,12},{1,17},{... | collective-permute-start | bytes 1658888 | tf_op jit(solution)/shard_map/ppermute | solution.py:390
  30.7 15.0 %collective-permute-start.8 = (bf16[144,1920]{1,0:T(8,128)(2,1)S(1)}, bf16[144,1920]{1,0:T(8,128)(2,1)S(1)}, u32[]{:S(2)}, u32[]{:S(2)}) collective-permute-start(bf16[144,1920]{1,0:T(8,128)(2,1)S(1)} %get-tuple-element.168.refs_1_), channel_id=1, source_target_pairs={{0,8},{4,12},{8,0},{12,4},{16,24},{20,28},{24,16},{28,20},{1,9},{5... | collective-permute-start | bytes 1658888 | tf_op jit(solution)/shard_map/ppermute | solution.py:390
  33.7 11.3 %collective-permute-start.5 = (bf16[96,768]{1,0:T(8,128)(2,1)S(1)}, bf16[96,768]{1,0:T(8,128)(2,1)S(1)}, u32[]{:S(2)}, u32[]{:S(2)}) collective-permute-start(bf16[96,768]{1,0:T(8,128)(2,1)S(1)} %get-tuple-element.165.refs_0_.refs_3_), channel_id=1, source_target_pairs={{0,2},{1,3},{2,0},{3,1},{4,6},{5,7},{6,4},{7,5},{8,10},{9,11},{10,... | collective-permute-start | bytes 442376 | tf_op jit(solution)/shard_map/ppermute | solution.py:395
  48.1 16.6 %collective-permute-start.14 = (bf16[96,768]{1,0:T(8,128)(2,1)S(1)}, bf16[96,768]{1,0:T(8,128)(2,1)S(1)}, u32[]{:S(2)}, u32[]{:S(2)}) collective-permute-start(bf16[96,768]{1,0:T(8,128)(2,1)S(1)} %get-tuple-element.175), channel_id=1, source_target_pairs={{0,3},{1,2},{2,1},{3,0},{4,7},{5,6},{6,5},{7,4},{8,11},{9,10},{10,... | collective-permute-start | bytes 442376 | tf_op jit(solution)/shard_map/ppermute | solution.py:395
  50.4 14.4 %collective-permute-start.13 = (bf16[96,768]{1,0:T(8,128)(2,1)S(1)}, bf16[96,768]{1,0:T(8,128)(2,1)S(1)}, u32[]{:S(2)}, u32[]{:S(2)}) collective-permute-start(bf16[96,768]{1,0:T(8,128)(2,1)S(1)} %get-tuple-element.175), channel_id=1, source_target_pairs={{0,2},{1,3},{2,0},{3,1},{4,6},{5,7},{6,4},{7,5},{8,10},{9,11},{10,... | collective-permute-start | bytes 442376 | tf_op jit(solution)/shard_map/ppermute | solution.py:395
  50.4 14.4 %collective-permute-start.12 = (bf16[96,768]{1,0:T(8,128)(2,1)S(1)}, bf16[96,768]{1,0:T(8,128)(2,1)S(1)}, u32[]{:S(2)}, u32[]{:S(2)}) collective-permute-start(bf16[96,768]{1,0:T(8,128)(2,1)S(1)} %get-tuple-element.175), channel_id=1, source_target_pairs={{0,1},{1,0},{2,3},{3,2},{4,5},{5,4},{6,7},{7,6},{8,9},{9,8},{10,11... | collective-permute-start | bytes 442376 | tf_op jit(solution)/shard_map/ppermute | solution.py:395
  52.6 20.8 %collective-permute-start.11 = (bf16[64,1920]{1,0:T(8,128)(2,1)S(1)}, bf16[64,1920]{1,0:T(8,128)(2,1)S(1)}, u32[]{:S(2)}, u32[]{:S(2)}) collective-permute-start(bf16[64,1920]{1,0:T(8,128)(2,1)S(1)} %get-tuple-element.174), channel_id=1, source_target_pairs={{0,16},{4,20},{8,24},{12,28},{16,0},{20,4},{24,8},{28,12},{1,17},{... | collective-permute-start | bytes 737288 | tf_op jit(solution)/shard_map/ppermute | solution.py:390
  53.1 20.3 %collective-permute-start.10 = (bf16[80,1920]{1,0:T(8,128)(2,1)S(1)}, bf16[80,1920]{1,0:T(8,128)(2,1)S(1)}, u32[]{:S(2)}, u32[]{:S(2)}) collective-permute-start(bf16[80,1920]{1,0:T(8,128)(2,1)S(1)} %get-tuple-element.173), channel_id=1, source_target_pairs={{0,8},{4,12},{8,0},{12,4},{16,24},{20,28},{24,16},{28,20},{1,9},{5... | collective-permute-start | bytes 921608 | tf_op jit(solution)/shard_map/ppermute | solution.py:390
  66.1 19.5 %collective-permute-start.17 = (bf16[288,768]{1,0:T(8,128)(2,1)}, bf16[288,768]{1,0:T(8,128)(2,1)}, u32[]{:S(2)}, u32[]{:S(2)}) collective-permute-start(bf16[288,768]{1,0:T(8,128)(2,1)} %get-tuple-element.188.refs_1_), channel_id=1, source_target_pairs={{0,16},{4,20},{8,24},{12,28},{16,0},{20,4},{24,8},{28,12},{1,17},{... | collective-permute-start | bytes 1327112 | tf_op jit(solution)/shard_map/ppermute | solution.py:390
  67.6 18.0 %collective-permute-start.16 = (bf16[288,768]{1,0:T(8,128)(2,1)}, bf16[288,768]{1,0:T(8,128)(2,1)}, u32[]{:S(2)}, u32[]{:S(2)}) collective-permute-start(bf16[288,768]{1,0:T(8,128)(2,1)} %get-tuple-element.188.refs_1_), channel_id=1, source_target_pairs={{0,8},{4,12},{8,0},{12,4},{16,24},{20,28},{24,16},{28,20},{1,9},{5... | collective-permute-start | bytes 1327112 | tf_op jit(solution)/shard_map/ppermute | solution.py:390
  69.1 13.2 %all-to-all-start.1 = ((bf16[4,160,192]{2,1,0:T(8,128)(2,1)}), bf16[4,160,192]{2,1,0:T(8,128)(2,1)}, u32[]{:S(2)}, u32[]{:S(2)}) async-start(bf16[4,160,192]{2,1,0:T(8,128)(2,1)} %bitcast.6), calls=%async_computation.1 | async-start | bytes 655360 | tf_op jit(solution)/shard_map/all_to_all | solution.py:401
  106.9 15.8 %collective-permute-start.20 = (bf16[384,768]{1,0:T(8,128)(2,1)}, bf16[384,768]{1,0:T(8,128)(2,1)}, u32[]{:S(2)}, u32[]{:S(2)}) collective-permute-start(bf16[384,768]{1,0:T(8,128)(2,1)} %get-tuple-element.217), channel_id=1, source_target_pairs={{0,8},{4,12},{8,0},{12,4},{16,24},{20,28},{24,16},{28,20},{1,9},{5... | collective-permute-start | bytes 1769480 | tf_op jit(solution)/shard_map/ppermute | solution.py:390
  107.5 15.4 %collective-permute-start.21 = (bf16[384,768]{1,0:T(8,128)(2,1)}, bf16[384,768]{1,0:T(8,128)(2,1)}, u32[]{:S(2)}, u32[]{:S(2)}) collective-permute-start(bf16[384,768]{1,0:T(8,128)(2,1)} %get-tuple-element.218), channel_id=1, source_target_pairs={{0,16},{4,20},{8,24},{12,28},{16,0},{20,4},{24,8},{28,12},{1,17},{... | collective-permute-start | bytes 1769480 | tf_op jit(solution)/shard_map/ppermute | solution.py:390
  117.4 20.2 %all-to-all-start.2 = ((bf16[4,144,192]{2,1,0:T(8,128)(2,1)}), bf16[4,144,192]{2,1,0:T(8,128)(2,1)S(1)}, u32[]{:S(2)}, u32[]{:S(2)}) async-start(bf16[4,144,192]{2,1,0:T(8,128)(2,1)} %bitcast.11), calls=%async_computation.2 | async-start | bytes 589824 | tf_op jit(solution)/shard_map/all_to_all | solution.py:401
  132.2 21.6 %collective-permute-start.26 = (bf16[192,1920]{1,0:T(8,128)(2,1)}, bf16[192,1920]{1,0:T(8,128)(2,1)S(1)}, u32[]{:S(2)}, u32[]{:S(2)}) collective-permute-start(bf16[192,1920]{1,0:T(8,128)(2,1)} %get-tuple-element.239), channel_id=1, source_target_pairs={{0,8},{4,12},{8,0},{12,4},{16,24},{20,28},{24,16},{28,20},{1,9},{5... | collective-permute-start | bytes 2211848 | tf_op jit(solution)/shard_map/ppermute | solution.py:390
  132.9 21.0 %collective-permute-start.27 = (bf16[192,1920]{1,0:T(8,128)(2,1)}, bf16[192,1920]{1,0:T(8,128)(2,1)S(1)}, u32[]{:S(2)}, u32[]{:S(2)}) collective-permute-start(bf16[192,1920]{1,0:T(8,128)(2,1)} %get-tuple-element.240), channel_id=1, source_target_pairs={{0,16},{4,20},{8,24},{12,28},{16,0},{20,4},{24,8},{28,12},{1,17},{... | collective-permute-start | bytes 2211848 | tf_op jit(solution)/shard_map/ppermute | solution.py:390
  137.6 21.5 %all-to-all-start.3 = ((bf16[4,96,768]{2,1,0:T(8,128)(2,1)}), bf16[4,96,768]{2,1,0:T(8,128)(2,1)S(1)}, u32[]{:S(2)}, u32[]{:S(2)}) async-start(bf16[4,96,768]{2,1,0:T(8,128)(2,1)} %bitcast.13), calls=%async_computation.3 | async-start | bytes 1179648 | tf_op jit(solution)/shard_map/all_to_all | solution.py:405
  156.6 11.3 %collective-permute-start.29 = (bf16[96,1920]{1,0:T(8,128)(2,1)}, bf16[96,1920]{1,0:T(8,128)(2,1)}, u32[]{:S(2)}, u32[]{:S(2)}) collective-permute-start(bf16[96,1920]{1,0:T(8,128)(2,1)} %get-tuple-element.250), channel_id=1, source_target_pairs={{0,8},{4,12},{8,0},{12,4},{16,24},{20,28},{24,16},{28,20},{1,9},{5... | collective-permute-start | bytes 1105928 | tf_op jit(solution)/shard_map/ppermute | solution.py:390
  157.0 11.5 %collective-permute-start.30 = (bf16[96,1920]{1,0:T(8,128)(2,1)}, bf16[96,1920]{1,0:T(8,128)(2,1)}, u32[]{:S(2)}, u32[]{:S(2)}) collective-permute-start(bf16[96,1920]{1,0:T(8,128)(2,1)} %get-tuple-element.251), channel_id=1, source_target_pairs={{0,16},{4,20},{8,24},{12,28},{16,0},{20,4},{24,8},{28,12},{1,17},{... | collective-permute-start | bytes 1105928 | tf_op jit(solution)/shard_map/ppermute | solution.py:390
  158.9 18.7 %collective-permute-start.28 = (bf16[576,768]{1,0:T(8,128)(2,1)S(1)}, bf16[576,768]{1,0:T(8,128)(2,1)S(1)}, u32[]{:S(2)}, u32[]{:S(2)}) collective-permute-start(bf16[576,768]{1,0:T(8,128)(2,1)S(1)} %get-tuple-element.248), channel_id=1, source_target_pairs={{0,4},{4,0},{8,12},{12,8},{16,20},{20,16},{24,28},{28,24},{1,5},{5... | collective-permute-start | bytes 2654216 | tf_op jit(solution)/shard_map/ppermute | solution.py:380
  162.0 22.2 %all-to-all-start.4 = ((bf16[4,96,768]{2,1,0:T(8,128)(2,1)}), bf16[4,96,768]{2,1,0:T(8,128)(2,1)S(1)}, u32[]{:S(2)}, u32[]{:S(2)}) async-start(bf16[4,96,768]{2,1,0:T(8,128)(2,1)} %bitcast.15), calls=%async_computation.4 | async-start | bytes 1179648 | tf_op jit(solution)/shard_map/all_to_all | solution.py:405
  173.1 16.6 %collective-permute-start.35 = (bf16[48,1920]{1,0:T(8,128)(2,1)}, bf16[48,1920]{1,0:T(8,128)(2,1)}, u32[]{:S(2)}, u32[]{:S(2)}) collective-permute-start(bf16[48,1920]{1,0:T(8,128)(2,1)} %get-tuple-element.262), channel_id=1, source_target_pairs={{0,1},{1,0},{2,3},{3,2},{4,5},{5,4},{6,7},{7,6},{8,9},{9,8},{10,11... | collective-permute-start | bytes 552968 | tf_op jit(solution)/shard_map/ppermute | solution.py:395
  174.9 21.2 %collective-permute-start.36 = (bf16[48,1920]{1,0:T(8,128)(2,1)}, bf16[48,1920]{1,0:T(8,128)(2,1)}, u32[]{:S(2)}, u32[]{:S(2)}) collective-permute-start(bf16[48,1920]{1,0:T(8,128)(2,1)} %get-tuple-element.263), channel_id=1, source_target_pairs={{0,2},{1,3},{2,0},{3,1},{4,6},{5,7},{6,4},{7,5},{8,10},{9,11},{10,... | collective-permute-start | bytes 552968 | tf_op jit(solution)/shard_map/ppermute | solution.py:395
  177.3 18.8 %collective-permute-start.37 = (bf16[48,1920]{1,0:T(8,128)(2,1)}, bf16[48,1920]{1,0:T(8,128)(2,1)}, u32[]{:S(2)}, u32[]{:S(2)}) collective-permute-start(bf16[48,1920]{1,0:T(8,128)(2,1)} %get-tuple-element.264), channel_id=1, source_target_pairs={{0,3},{1,2},{2,1},{3,0},{4,7},{5,6},{6,5},{7,4},{8,11},{9,10},{10,... | collective-permute-start | bytes 552968 | tf_op jit(solution)/shard_map/ppermute | solution.py:395
  178.9 21.8 %collective-permute-start.32 = (bf16[144,768]{1,0:T(8,128)(2,1)S(1)}, bf16[144,768]{1,0:T(8,128)(2,1)S(1)}, u32[]{:S(2)}, u32[]{:S(2)}) collective-permute-start(bf16[144,768]{1,0:T(8,128)(2,1)S(1)} %get-tuple-element.257), channel_id=1, source_target_pairs={{0,8},{4,12},{8,0},{12,4},{16,24},{20,28},{24,16},{28,20},{1,9},{5... | collective-permute-start | bytes 663560 | tf_op jit(solution)/shard_map/ppermute | solution.py:390
  180.6 20.3 %collective-permute-start.33 = (bf16[144,768]{1,0:T(8,128)(2,1)S(1)}, bf16[144,768]{1,0:T(8,128)(2,1)S(1)}, u32[]{:S(2)}, u32[]{:S(2)}) collective-permute-start(bf16[144,768]{1,0:T(8,128)(2,1)S(1)} %get-tuple-element.258), channel_id=1, source_target_pairs={{0,16},{4,20},{8,24},{12,28},{16,0},{20,4},{24,8},{28,12},{1,17},{... | collective-permute-start | bytes 663560 | tf_op jit(solution)/shard_map/ppermute | solution.py:390
  186.1 24.4 %all-to-all-start.5 = ((bf16[4,192,768]{2,1,0:T(8,128)(2,1)}), bf16[4,192,768]{2,1,0:T(8,128)(2,1)S(1)}, u32[]{:S(2)}, u32[]{:S(2)}) async-start(bf16[4,192,768]{2,1,0:T(8,128)(2,1)} %bitcast.17), calls=%async_computation.5 | async-start | bytes 2359296 | tf_op jit(solution)/shard_map/all_to_all | solution.py:401
  189.7 22.2 %collective-permute-start.34 = (bf16[144,768]{1,0:T(8,128)(2,1)S(1)}, bf16[144,768]{1,0:T(8,128)(2,1)}, u32[]{:S(2)}, u32[]{:S(2)}) collective-permute-start(bf16[144,768]{1,0:T(8,128)(2,1)S(1)} %get-tuple-element.259), channel_id=1, source_target_pairs={{0,24},{4,28},{8,16},{12,20},{16,8},{20,12},{24,0},{28,4},{1,25},{... | collective-permute-start | bytes 663560 | tf_op jit(solution)/shard_map/ppermute | solution.py:390
  197.4 21.8 %collective-permute-start.40 = (bf16[48,1920]{1,0:T(8,128)(2,1)S(1)}, bf16[48,1920]{1,0:T(8,128)(2,1)S(1)}, u32[]{:S(2)}, u32[]{:S(2)}) collective-permute-start(bf16[48,1920]{1,0:T(8,128)(2,1)S(1)} %get-tuple-element.277.refs_0_), channel_id=1, source_target_pairs={{0,24},{4,28},{8,16},{12,20},{16,8},{20,12},{24,0},{28,4},{1,25},{... | collective-permute-start | bytes 552968 | tf_op jit(solution)/shard_map/ppermute | solution.py:390
  198.9 20.3 %collective-permute-start.39 = (bf16[48,1920]{1,0:T(8,128)(2,1)S(1)}, bf16[48,1920]{1,0:T(8,128)(2,1)S(1)}, u32[]{:S(2)}, u32[]{:S(2)}) collective-permute-start(bf16[48,1920]{1,0:T(8,128)(2,1)S(1)} %get-tuple-element.277.refs_0_), channel_id=1, source_target_pairs={{0,16},{4,20},{8,24},{12,28},{16,0},{20,4},{24,8},{28,12},{1,17},{... | collective-permute-start | bytes 552968 | tf_op jit(solution)/shard_map/ppermute | solution.py:390
  200.7 18.6 %collective-permute-start.38 = (bf16[48,1920]{1,0:T(8,128)(2,1)S(1)}, bf16[48,1920]{1,0:T(8,128)(2,1)S(1)}, u32[]{:S(2)}, u32[]{:S(2)}) collective-permute-start(bf16[48,1920]{1,0:T(8,128)(2,1)S(1)} %get-tuple-element.277.refs_0_), channel_id=1, source_target_pairs={{0,8},{4,12},{8,0},{12,4},{16,24},{20,28},{24,16},{28,20},{1,9},{5... | collective-permute-start | bytes 552968 | tf_op jit(solution)/shard_map/ppermute | solution.py:390
  (55 other events, 319.4 us)

commit v4 on v3

--- a/solution.py
+++ b/solution.py
@@ -534,6 +534,21 @@
     )
 
 
+def put_small(out, start, small):
+    third = small.shape[1] // 3
+    lanes = slice(9 * third, 10 * third)
+    for q in range(3):
+        block = slice(start + 16 * q, start + 16 * (q + 1))
+        out[block, lanes] = small[:, third * q : third * (q + 1)].astype(out.dtype)
+
+
+def get_small(piece, start, feat):
+    third = feat // 3
+    lanes = slice(9 * third, 10 * third)
+    parts = [piece[start + 16 * q : start + 16 * (q + 1), lanes].astype(F32) for q in range(3)]
+    return jnp.concatenate(parts, axis=1)
+
+
 def pack_tokens(where, tokens, segment, valid, out):
     rows, width = tokens.shape
     ids = segment[...]
@@ -564,6 +579,7 @@
     weights, vectors, long, valid, out = refs[:3], refs[3:11], refs[11], refs[12], refs[13]
     held, small, held_long, sems = refs[14], refs[15:23], refs[23], refs[24]
     half, feat = held.shape[1], small[0].shape[0]
+    out[48:, 3 * feat :] = jnp.zeros((half - 48, feat // 3), out.dtype)
     own_rows = rows_at(half * where[1], half, 32)
     run_copies(
         [(w.at[own_rows], held.at[i]) for i, w in enumerate(weights)]
@@ -582,8 +598,8 @@
     count = jnp.sum(valid[...].astype(F32), axis=1, keepdims=True)
     lines = [v[...].astype(F32).reshape(1, feat) for v in small]
     lines += [spread[:, feat * i : feat * (i + 1)] for i in range(4)]
-    lines += [jnp.broadcast_to(count, (1, feat)), jnp.zeros((half - 13, feat), F32)]
-    out[:, 3 * feat :] = jnp.concatenate(lines, axis=0).astype(out.dtype)
+    lines += [jnp.broadcast_to(count, (1, feat)), jnp.zeros((3, feat), F32)]
+    put_small(out, 0, jnp.concatenate(lines, axis=0))
 
 
 def pack_down(where, down, out, sem):
@@ -716,8 +732,7 @@
         for j, (i, source) in enumerate(zip((0, 1, 2, 4), kept))
     ]
     core, plane = where[1], where[2]
-    half, width = weights[0].shape
-    feat = width // 4
+    half, feat = weights[0].shape[0], small.shape[2]
     group = query_column.shape[0]
     rows = group // 4
 
@@ -727,7 +742,7 @@
         w_three[rows_at(base + half * core, half, 32), :] = piece[:, : 3 * feat]
         other = far_weights[half * s : half * (s + 1), :]
         w_three[rows_at(base + half * (1 - core), half, 32), :] = other[:, : 3 * feat]
-        near = piece[:16, 3 * feat :].astype(F32)
+        near = get_small(piece, 0, feat)
         small[plane ^ s] = near
         count += near[12:13, :1] + other[12:13, 3 * feat : 3 * feat + 1].astype(F32)
     vectors[...] = jnp.zeros(vectors.shape, F32)
@@ -1003,21 +1018,23 @@
 
 
 def up_grads(where, h_pair, d_up, kept, given, *refs):
-    outs, total = refs[:5], refs[5]
+    outs, total = refs[:4], refs[4]
     count, units = outs[0].shape[0] // 4, d_up.shape[1]
     total[:, :units] = dot(h_pair[...], d_up[...], TN).astype(BF16)
     total[:, units:] = (kept[...].astype(F32) + given[...].astype(F32)).astype(BF16)
-
-    def block(j, p):
-        return total[rows_at(4 * count * p + count * j, count, 16), :]
-
-    split_chips(where[0], block, outs, count)
-
-
-def send_planes(where, own, from_x, from_y, last_x, last_y, *refs):
+    for k, out in enumerate(outs):
+        for p in range(4):
+            at = rows_at(4 * count * p + count * (where[0] ^ k), count, 16)
+            out[count * p : count * (p + 1), :] = total[at, :]
+
+
+def send_planes(where, own, p1, p2, p3, *refs):
     outs, total = refs[:4], refs[4]
-    part, half = outs[0].shape[0], last_x.shape[0]
-    total[:half, :], total[half:, :] = add_chips(own, from_x, from_y, last_x, last_y)
+    part = outs[0].shape[0]
+    added = own[...].astype(F32)
+    for piece in (p1, p2, p3):
+        added = added + piece[...].astype(F32)
+    total[...] = added
     for s, out in enumerate(outs):
         out[...] = total[rows_at(part * (where[2] ^ s), part, 16), :].astype(out.dtype)
 
@@ -1081,8 +1098,7 @@
     for p in (1, 2, 3):
         arrived_down = arrived_down + down[part * p : part * (p + 1), :].astype(F32)
     down_sum[...] = arrived_down.astype(BF16)
-    half, width = out.shape[0] // 4, out.shape[1]
-    feat = width // 4
+    half, feat = out.shape[0] // 4, kept.shape[1] // 3
     for p in range(4):
         cut = slice(feat * p, feat * (p + 1))
         owner = jnp.where(chip == p, 1.0, 0.0)
@@ -1098,13 +1114,14 @@
             from_attention[2:3, :feat] * owner,
             from_attention[3:4, :feat] * owner,
             from_result[1:2, :feat],
-            jnp.zeros((half - 11, feat), F32),
+            jnp.zeros((5, feat), F32),
         ]
-        small = jnp.concatenate(lines, axis=0).astype(BF16)
+        small = jnp.concatenate(lines, axis=0)
         block = slice(half * p, half * (p + 1))
         total = (kept[block, :].astype(F32) + given[block, :].astype(F32)).astype(BF16)
         out[block, : 3 * feat] = total
-        out[block, 3 * feat :] = small
+        out[half * p + 48 : half * (p + 1), 3 * feat :] = jnp.zeros((half - 48, feat // 3), BF16)
+        put_small(out, half * p, small)
 
 
 def sum_planes(where, arrived, down, out):
@@ -1113,7 +1130,7 @@
     total = arrived[:half, :].astype(F32)
     for p in (1, 2, 3):
         total = total + arrived[half * p : half * (p + 1), :].astype(F32)
-    small = total[:16, 3 * feat :]
+    small = get_small(total, 0, feat)
     error = jnp.sum(small[10:11, :3], axis=1, keepdims=True)
     high = error.astype(BF16).astype(F32)
     middle = (error - high).astype(BF16).astype(F32)
@@ -1232,9 +1249,10 @@
     up_far = trade_planes(up_piece)
     bundle = step(pack_tokens, shaped(rows + 16, width), (own, segment_ids, valid_rows), cost=50)
     near_tokens = [bundle] + [swap_chips(bundle, k) for k in steps]
+    lanes = 3 * feat + feat // 3
     projections = step(
         pack_projections,
-        shaped(half, width),
+        shaped(half, lanes),
         (query_weight, key_weight, value_weight, *smalls, up_bias, valid_rows),
         far=range(12),
         scratch=[
@@ -1314,13 +1332,13 @@
     )
     w_output = step(build_output, shaped(width, width), (out_near, out_far))
 
+    down_all = all_chips(down_far, down_far[0].shape[0] // 2)
     second, h_two, count = step(
         project_output,
         (wide(rows, width), shaped(rows, width), wide(8, 128)),
         (mixed_low, w_output, own, vectors),
     )
     h_pair = both_cores(h_two)
-    down_all = all_chips(down_far, down_far[0].shape[0] // 2)
     act, slope = step(
         activate,
         (shaped(2 * rows, units), wide(2 * rows, units)),
@@ -1351,10 +1369,11 @@
     def five(count, lanes):
         return (shaped(4 * count, lanes),) * 3 + (shaped(2 * count, lanes),) * 2
 
-    def onward(parts, arrived, fetch):
+    def onward(parts, arrived):
         count, lanes = parts[3].shape
         to_x, to_y = step(
-            pass_on, (shaped(count, lanes),) * 2, (*arrived, *parts[3:]), fetch=fetch, cost=50
+            pass_on, (shaped(count, lanes),) * 2, (*arrived, *parts[3:]),
+            cost=50,
         )
         return (parts[0], *arrived, swap_chips(to_x, 1), swap_chips(to_y, 2))
 
@@ -1386,17 +1405,17 @@
         cost=1,
     )
     given_out = swap_cores(given_out)
-    down_sums = onward(down_parts, down_arrived, ())
+    down_sums = onward(down_parts, down_arrived)
     up_parts = step(
         up_grads,
-        five(quarter, 5 * core_units),
+        (shaped(4 * quarter, 5 * core_units),) * 4,
         (h_pair, d_up, kept_out, given_out),
-        store=(0, 3, 4),
+        store=(0,),
         scratch=[pltpu.VMEM((width, 5 * core_units), BF16)],
         vmem=24,
         cost=5,
     )
-    up_arrived = swap_chips(up_parts[1], 1), swap_chips(up_parts[2], 2)
+    up_sums = [up_parts[0]] + [swap_chips(up_parts[k], k) for k in steps]
     down_planes = trade_planes(step(sum_chips, shaped(4 * part_units, width), down_sums))
 
     d_near, d_far, kept, given, from_attention = step(
@@ -1426,10 +1445,9 @@
         cost=50,
     )
     given, d_far = swap_cores(given), swap_cores(d_far)
-    up_sums = onward(up_parts, up_arrived, (2, 3))
     arrived, down_planes = step(
         pack_gradients,
-        (shaped(4 * half, width), shaped(part_units, width)),
+        (shaped(4 * half, lanes), shaped(part_units, width)),
         (kept, given, from_attention, from_second, from_result, up_line, down_planes),
         fetch=(0, 1),
         cost=1,
@@ -1459,6 +1477,7 @@
         finish_inputs, shaped(rows, width), (*shares, own, d_second, vectors), fetch=(0, 4), cost=50
     )
     both = (both, swap_cores(both))
+    up_whole = whole(up_near)
     finished = step(
         finish_projections,
         (wide(shard, width),) * 3
@@ -1479,7 +1498,7 @@
     grad_up_weight, grad_output_weight = step(
         finish_up,
         (wide(shard, hidden), wide(shard, width)),
-        whole(up_near),
+        up_whole,
         far_outs=(0, 1),
         scratch=[pltpu.VMEM((shard, hidden), F32), pltpu.VMEM((shard, width), F32), dma((8,))],
     )

time: 226 us -> 220 us (0.973)
  Pallas kernels: 93.4 us -> 90.2 us
  waiting for transfers between devices: 44.1 us -> 41.6 us
    all_to_all x3, waiting for transfers between devices: 12.6 us -> 8.25 us  [trade_chips(): lax.all_to_all(value, 'ctx', 0, 0, axis_index_groups=groups, tiled=True)]
    ppermute x25 -> x24, waiting for transfers between devices: 14 us -> 17.4 us  [swap_chips(): return lax.ppermute(value, 'ctx', [(i, i ^ 2 * step) for i in range(size)])]
    pallas_call x39 -> x38, Pallas kernels: 93.4 us -> 90.2 us  [local_call(): pl.pallas_call(kernel, out_shape=(*(pltpu.HBM(o.shape, o.dtype) if i in f...]
    ppermute x25 -> x24, starting transfers between devices: 31.7 us -> 31 us  [swap_chips(): return lax.ppermute(value, 'ctx', [(i, i ^ 2 * step) for i in range(size)])]
    unnamed x78 -> x86, local copies, waits for them, and re-layouts: 5.49 us -> 5.27 us
  transfers between devices with their start and end apart: 48 -> 47, of which waited for: 18 -> 17; matrix products, arithmetic and copies ran while one was open for 0% -> 0% of each run, Pallas kernels for 35% -> 35%
where the time goes in v4:
time: 220 us; the launch traced here: 219 us
  Pallas kernels  90.2 us (41%)
  starting transfers between devices  71.6 us (33%)
  waiting for transfers between devices  41.6 us (19%)
  blocking collectives  8.61 us (4%)
  local copies, waits for them, and re-layouts  5.27 us (2%)
    pallas_call x38, Pallas kernels, local_call(): pl.pallas_call(kernel, out_shape=(*(pltpu.HBM(o.shape, o.dtype) if i in f...  90.2 us
    ppermute x24, starting transfers between devices, swap_chips(): return lax.ppermute(value, 'ctx', [(i, i ^ 2 * step) for i in range(size)])  31 us
    ppermute x24, waiting for transfers between devices, swap_chips(): return lax.ppermute(value, 'ctx', [(i, i ^ 2 * step) for i in range(size)])  17.4 us
    all_to_all x3, starting transfers between devices, trade_planes(): return lax.all_to_all(value, 'fsdp', 0, 0, tiled=True)  14.9 us
    ppermute x9, starting transfers between devices, swap_planes(): return lax.ppermute(value, 'fsdp', [(i, i ^ step) for i in range(size)])  13.3 us
    all_to_all x3, starting transfers between devices, trade_chips(): lax.all_to_all(value, 'ctx', 0, 0, axis_index_groups=groups, tiled=True)  11.4 us
    all_gather x4, blocking collectives, both_cores(): lax.all_gather(value, 'ctx', axis=0, tiled=True, axis_index_groups=pairs)  8.61 us
    all_to_all x3, waiting for transfers between devices, trade_chips(): lax.all_to_all(value, 'ctx', 0, 0, axis_index_groups=groups, tiled=True)  8.25 us
  transfers between devices with their start and end apart: 47, of which 17 were waited for; matrix products, arithmetic and copies ran while one was open for 0% of the time, Pallas kernels for 35%

profile of v4, /device:TPU:0, one launch (start us, length us, event | category | flops | bytes accessed | tf_op | source)
XLA Modules:
  0.0 219.0 jit_solution(13071376615884274583)
XLA Ops:
  0.8 2.3 %shard_map.331 = (bf16[192,1920]{1,0:T(8,128)(2,1)}, f32[8,128]{1,0:T(8,128)S(1)}) custom-call(s32[3]{0:T(128)S(1)} %pad_add_fusion.where_ref, bf16[192,3072]{1,0:T(8,128)(2,1)} %refs_0_.10, bf16[192,768]{1,0:T(8,128)(2,1)} %refs_0_.9), custom_call_target="tpu_custom_call" | custom-call | tf_op jit(solution)/shard_map/pallas_call | solution.py:476
  3.1 6.3 %all-to-all-start = ((bf16[4,48,1920]{2,1,0:T(8,128)(2,1)}), bf16[4,48,1920]{2,1,0:T(8,128)(2,1)S(1)}, u32[]{:S(2)}, u32[]{:S(2)}) async-start(bf16[4,48,1920]{2,1,0:T(8,128)(2,1)} %bitcast.4), calls=%async_computation | async-start | bytes 1474560 | tf_op jit(solution)/shard_map/all_to_all | solution.py:405
  10.0 2.5 %collective-permute-start.2 = (bf16[160,768]{1,0:T(8,128)(2,1)S(1)}, bf16[160,768]{1,0:T(8,128)(2,1)S(1)}, u32[]{:S(2)}, u32[]{:S(2)}) collective-permute-start(bf16[160,768]{1,0:T(8,128)(2,1)S(1)} %get-tuple-element.151.refs_0_), channel_id=1, source_target_pairs={{0,24},{4,28},{8,16},{12,20},{16,8},{20,12},{24,0},{28,4},{1,25},{... | collective-permute-start | bytes 737288 | tf_op jit(solution)/shard_map/ppermute | solution.py:390
  15.6 4.4 %collective-permute-done.2.refs_3_ = bf16[160,768]{1,0:T(8,128)(2,1)S(1)} collective-permute-done((bf16[160,768]{1,0:T(8,128)(2,1)S(1)}, bf16[160,768]{1,0:T(8,128)(2,1)S(1)}, u32[]{:S(2)}, u32[]{:S(2)}) %collective-permute-start.2) | collective-permute-done | bytes 245792 | tf_op jit(solution)/shard_map/ppermute | solution.py:390
  19.9 3.8 %collective-permute-done.1.refs_2_ = bf16[160,768]{1,0:T(8,128)(2,1)S(1)} collective-permute-done((bf16[160,768]{1,0:T(8,128)(2,1)S(1)}, bf16[160,768]{1,0:T(8,128)(2,1)S(1)}, u32[]{:S(2)}, u32[]{:S(2)}) %collective-permute-start.1) | collective-permute-done | bytes 245792 | tf_op jit(solution)/shard_map/ppermute | solution.py:390
  24.5 4.0 %all-to-all-done = bf16[4,48,1920]{2,1,0:T(8,128)(2,1)S(1)} async-done(((bf16[4,48,1920]{2,1,0:T(8,128)(2,1)}), bf16[4,48,1920]{2,1,0:T(8,128)(2,1)S(1)}, u32[]{:S(2)}, u32[]{:S(2)}) %all-to-all-start) | async-done | bytes 737312 | tf_op jit(solution)/shard_map/all_to_all | solution.py:405
  33.7 2.9 %collective-permute-start.4 = (bf16[96,640]{1,0:T(8,128)(2,1)S(1)}, bf16[96,640]{1,0:T(8,128)(2,1)S(1)}, u32[]{:S(2)}, u32[]{:S(2)}) collective-permute-start(bf16[96,640]{1,0:T(8,128)(2,1)S(1)} %get-tuple-element.161.refs_0_.refs_3_), channel_id=1, source_target_pairs={{0,1},{1,0},{2,3},{3,2},{4,5},{5,4},{6,7},{7,6},{8,9},{9,8},{10,11... | collective-permute-start | bytes 368648 | tf_op jit(solution)/shard_map/ppermute | solution.py:395
  36.6 2.4 %shard_map.336 = (f32[1152,768]{1,0:T(8,128)S(1)}, f32[8,1152]{1,0:T(8,128)S(1)}, f32[576,128]{1,0:T(8,128)S(1)}, f32[8,128]{1,0:T(8,128)S(1)}) custom-call(s32[3]{0:T(128)S(1)} %pad_add_fusion.where_ref, bf16[640,768]{1,0:T(8,128)(2,1)S(1)} %get-tuple-element.154.refs_0_, bf16[640,768]{1,0:T(8,128)(2,1)} %collective-permute-done.3.refs_1_, ...), custom_call_target="tpu_custom_call" | custom-call | flops 1000000000 | bytes 1000000 | tf_op jit(solution)/shard_map/pallas_call | solution.py:476
  40.3 2.9 %collective-permute-done.5.refs_2_.refs_5_ = bf16[96,640]{1,0:T(8,128)(2,1)S(1)} collective-permute-done((bf16[96,640]{1,0:T(8,128)(2,1)S(1)}, bf16[96,640]{1,0:T(8,128)(2,1)S(1)}, u32[]{:S(2)}, u32[]{:S(2)}) %collective-permute-start.5) | collective-permute-done | bytes 122912 | tf_op jit(solution)/shard_map/ppermute | solution.py:395
  52.7 10.5 %shard_map.340 = (bf16[1152,768]{1,0:T(8,128)(2,1)}, bf16[768,576]{1,0:T(8,128)(2,1)}, bf16[1152,576]{1,0:T(8,128)(2,1)}, bf16[3,576,1152]{2,1,0:T(8,128)(2,1)},...) custom-call(s32[3]{0:T(128)S(1)} %pad_add_fusion.where_ref, ...), custom_call_target="tpu_custom_call" | custom-call | flops 49999998976 | bytes 50000000 | tf_op jit(solution)/shard_map/pallas_call | solution.py:476
  63.7 4.3 %all-to-all-start.1 = ((bf16[4,160,192]{2,1,0:T(8,128)(2,1)}), bf16[4,160,192]{2,1,0:T(8,128)(2,1)}, u32[]{:S(2)}, u32[]{:S(2)}) async-start(bf16[4,160,192]{2,1,0:T(8,128)(2,1)} %bitcast.6), calls=%async_computation.1 | async-start | bytes 655360 | tf_op jit(solution)/shard_map/all_to_all | solution.py:401
  74.6 2.4 %shard_map.343 = (bf16[768,1536]{1,0:T(8,128)(2,1)S(1)}, f32[8,128]{1,0:T(8,128)S(1)}) custom-call(s32[3]{0:T(128)S(1)} %pad_add_fusion.where_ref, bf16[192,3072]{1,0:T(8,128)(2,1)} %refs_0_.10, bf16[144,1920]{1,0:T(8,128)(2,1)} %copy-done.4, bf16[144,1920]{1,0:T(8,128)(2,1)} %copy-done.6, bf16[144,1920]{1,0:T(8,128)(2,1)} %copy-done.5, ...), custom_call_target="tpu_custom_call" | custom-call | flops 49999998976 | bytes 50000000 | tf_op jit(solution)/shard_map/pallas_call | solution.py:476
  77.8 4.1 %collective-permute-done.17.refs_1_.refs_3_ = bf16[288,768]{1,0:T(8,128)(2,1)S(1)} collective-permute-done((bf16[288,768]{1,0:T(8,128)(2,1)S(1)}, bf16[288,768]{1,0:T(8,128)(2,1)S(1)}, u32[]{:S(2)}, u32[]{:S(2)}) %collective-permute-start.17) | collective-permute-done | bytes 442400 | tf_op jit(solution)/shard_map/ppermute | solution.py:390
  102.4 3.1 %shard_map.351 = (bf16[384,768]{1,0:T(8,128)(2,1)S(1)}, bf16[384,768]{1,0:T(8,128)(2,1)}, bf16[384,768]{1,0:T(8,128)(2,1)}, bf16[192,768]{1,0:T(8,128)(2,1)S(1)}...) custom-call(s32[3]{0:T(128)S(1)} %pad_add_fusion.where_ref, bf16[288,1536]{1,0:T(8,128)(2,1)S(1)} %get-tuple-element.187.refs_0_, ...), custom_call_target="tpu_custom_call" | custom-call | tf_op jit(solution)/shard_map/pallas_call | solution.py:476
  107.5 3.9 %shard_map.352 = (bf16[288,1536]{1,0:T(8,128)(2,1)S(1)}, f32[144,768]{1,0:T(8,128)S(1)}, bf16[144,768]{1,0:T(8,128)(2,1)S(1)}, f32[1,1536]{1,0:T(1,128)S(1)}, f32[8,128]{1,0:T(8,128)S(1)}) custom-call(s32[3]{0:T(128)S(1)} %pad_add_fusion.where_ref, bf16[288,768]{1,0:T(8,128)(2,1)S(1)} %all_gather.14.refs_1_.refs_0_, ...), custom_call_target="tpu_custom_call" | custom-call | flops 49999998976 | bytes 50000000 | tf_op jit(solution)/shard_map/pallas_call | solution.py:476
  116.5 3.5 %all-to-all-start.2 = ((bf16[4,144,192]{2,1,0:T(8,128)(2,1)}), bf16[4,144,192]{2,1,0:T(8,128)(2,1)S(1)}, u32[]{:S(2)}, u32[]{:S(2)}) async-start(bf16[4,144,192]{2,1,0:T(8,128)(2,1)} %bitcast.11), calls=%async_computation.2 | async-start | bytes 589824 | tf_op jit(solution)/shard_map/all_to_all | solution.py:401
  126.8 4.5 %shard_map.356 = (bf16[192,1920]{1,0:T(8,128)(2,1)}, bf16[192,1920]{1,0:T(8,128)(2,1)}, bf16[192,1920]{1,0:T(8,128)(2,1)}, bf16[192,1920]{1,0:T(8,128)(2,1)}, f32[8,128]{1,0:T(8,128)S(1)}) custom-call(s32[3]{0:T(128)S(1)} %pad_add_fusion.where_ref, bf16[288,768]{1,0:T(8,128)(2,1)S(1)} %copy-done.1, bf16[288,1536]{1,0:T(8,128)(2,1)S(1)} %copy-done.36, ...), custom_call_target="tpu_custom_call" | custom-call | flops 5000000000 | bytes 5000000 | tf_op jit(solution)/shard_map/pallas_call | solution.py:476
  132.4 2.4 %collective-permute-start.29 = (bf16[192,1920]{1,0:T(8,128)(2,1)}, bf16[192,1920]{1,0:T(8,128)(2,1)}, u32[]{:S(2)}, u32[]{:S(2)}) collective-permute-start(bf16[192,1920]{1,0:T(8,128)(2,1)} %get-tuple-element.243), channel_id=1, source_target_pairs={{0,24},{4,28},{8,16},{12,20},{16,8},{20,12},{24,0},{28,4},{1,25},{... | collective-permute-start | bytes 2211848 | tf_op jit(solution)/shard_map/ppermute | solution.py:390
  137.1 3.7 %all-to-all-start.3 = ((bf16[4,96,768]{2,1,0:T(8,128)(2,1)}), bf16[4,96,768]{2,1,0:T(8,128)(2,1)S(1)}, u32[]{:S(2)}, u32[]{:S(2)}) async-start(bf16[4,96,768]{2,1,0:T(8,128)(2,1)} %bitcast.13), calls=%async_computation.3 | async-start | bytes 1179648 | tf_op jit(solution)/shard_map/all_to_all | solution.py:405
  140.8 12.4 %shard_map.358 = (bf16[576,768]{1,0:T(8,128)(2,1)S(1)}, bf16[576,768]{1,0:T(8,128)(2,1)S(1)}, bf16[384,576]{1,0:T(8,128)(2,1)}, bf16[384,576]{1,0:T(8,128)(2,1)}...) custom-call(s32[3]{0:T(128)S(1)} %pad_add_fusion.where_ref, bf16[576,192]{1,0:T(8,128)(2,1)S(1)} %bitcast.27, ...), custom_call_target="tpu_custom_call" | custom-call | flops 49999998976 | bytes 50000000 | tf_op jit(solution)/shard_map/pallas_call | solution.py:476
  154.6 2.4 %collective-permute-done.25.refs_1_ = bf16[384,576]{1,0:T(8,128)(2,1)} collective-permute-done((bf16[384,576]{1,0:T(8,128)(2,1)}, bf16[384,576]{1,0:T(8,128)(2,1)}, u32[]{:S(2)}, u32[]{:S(2)}) %collective-permute-start.25) | collective-permute-done | bytes 442400 | tf_op jit(solution)/shard_map/ppermute | solution.py:380
  157.0 2.9 %shard_map.359 = (bf16[384,640]{1,0:T(8,128)(2,1)}, bf16[96,768]{1,0:T(8,128)(2,1)S(1)}, f32[8,128]{1,0:T(8,128)S(1)}) custom-call(s32[3]{0:T(128)S(1)} %pad_add_fusion.where_ref, bf16[384,576]{1,0:T(8,128)(2,1)} %get-tuple-element.228.refs_0_, bf16[384,576]{1,0:T(8,128)(2,1)} %collective-permute-done.25.refs_1_, f32[8,768]{1,0:T(8,128)S(1)} %get-tuple-element.230.refs_2_, ...), custom_call_target="tpu_custom_call" | custom-call | flops 1000000000 | bytes 1000000 | tf_op jit(solution)/shard_map/pallas_call | solution.py:476
  159.9 4.8 %all-to-all-start.4 = ((bf16[4,96,640]{2,1,0:T(8,128)(2,1)}), bf16[4,96,640]{2,1,0:T(8,128)(2,1)S(1)}, u32[]{:S(2)}, u32[]{:S(2)}) async-start(bf16[4,96,640]{2,1,0:T(8,128)(2,1)} %bitcast.15), calls=%async_computation.4 | async-start | bytes 983040 | tf_op jit(solution)/shard_map/all_to_all | solution.py:405
  166.1 4.0 %shard_map.360 = (bf16[48,1920]{1,0:T(8,128)(2,1)S(1)}, bf16[48,1920]{1,0:T(8,128)(2,1)}, bf16[48,1920]{1,0:T(8,128)(2,1)}, bf16[48,1920]{1,0:T(8,128)(2,1)}, f32[8,128]{1,0:T(8,128)S(1)}) custom-call(s32[3]{0:T(128)S(1)} %pad_add_fusion.where_ref, bf16[192,1920]{1,0:T(8,128)(2,1)} %get-tuple-element.240.refs_0_, ...), custom_call_target="tpu_custom_call" | custom-call | flops 49999998976 | bytes 50000000 | tf_op jit(solution)/shard_map/pallas_call | solution.py:476
  170.8 2.4 %collective-permute-start.32 = (bf16[48,1920]{1,0:T(8,128)(2,1)}, bf16[48,1920]{1,0:T(8,128)(2,1)}, u32[]{:S(2)}, u32[]{:S(2)}) collective-permute-start(bf16[48,1920]{1,0:T(8,128)(2,1)} %get-tuple-element.250), channel_id=1, source_target_pairs={{0,2},{1,3},{2,0},{3,1},{4,6},{5,7},{6,4},{7,5},{8,10},{9,11},{10,... | collective-permute-start | bytes 552968 | tf_op jit(solution)/shard_map/ppermute | solution.py:395
  181.7 3.7 %all-to-all-start.5 = ((bf16[4,192,768]{2,1,0:T(8,128)(2,1)}), bf16[4,192,768]{2,1,0:T(8,128)(2,1)S(1)}, u32[]{:S(2)}, u32[]{:S(2)}) async-start(bf16[4,192,768]{2,1,0:T(8,128)(2,1)} %bitcast.17), calls=%async_computation.5 | async-start | bytes 2359296 | tf_op jit(solution)/shard_map/all_to_all | solution.py:401
  185.4 2.9 %collective-permute-start.39 = (bf16[144,768]{1,0:T(8,128)(2,1)S(1)}, bf16[144,768]{1,0:T(8,128)(2,1)}, u32[]{:S(2)}, u32[]{:S(2)}) collective-permute-start(bf16[144,768]{1,0:T(8,128)(2,1)S(1)} %get-tuple-element.257), channel_id=1, source_target_pairs={{0,24},{4,28},{8,16},{12,20},{16,8},{20,12},{24,0},{28,4},{1,25},{... | collective-permute-start | bytes 663560 | tf_op jit(solution)/shard_map/ppermute | solution.py:390
  188.3 3.5 %collective-permute-done.32.refs_2_ = bf16[48,1920]{1,0:T(8,128)(2,1)} collective-permute-done((bf16[48,1920]{1,0:T(8,128)(2,1)}, bf16[48,1920]{1,0:T(8,128)(2,1)}, u32[]{:S(2)}, u32[]{:S(2)}) %collective-permute-start.32) | collective-permute-done | bytes 184352 | tf_op jit(solution)/shard_map/ppermute | solution.py:395
  196.6 8.2 %all-to-all-done.5 = bf16[4,192,768]{2,1,0:T(8,128)(2,1)S(1)} async-done(((bf16[4,192,768]{2,1,0:T(8,128)(2,1)}), bf16[4,192,768]{2,1,0:T(8,128)(2,1)S(1)}, u32[]{:S(2)}, u32[]{:S(2)}) %all-to-all-start.5) | async-done | bytes 1179680 | tf_op jit(solution)/shard_map/all_to_all | solution.py:401
  204.9 2.7 %collective-permute-done.39.refs_3_ = bf16[144,768]{1,0:T(8,128)(2,1)} collective-permute-done((bf16[144,768]{1,0:T(8,128)(2,1)S(1)}, bf16[144,768]{1,0:T(8,128)(2,1)}, u32[]{:S(2)}, u32[]{:S(2)}) %collective-permute-start.39) | collective-permute-done | bytes 221216 | tf_op jit(solution)/shard_map/ppermute | solution.py:390
  207.6 3.1 %shard_map.364 = (bf16[144,768]{1,0:T(8,128)(2,1)}, f32[8,128]{1,0:T(8,128)S(1)}) custom-call(s32[3]{0:T(128)S(1)} %pad_add_fusion.where_ref, bf16[144,768]{1,0:T(8,128)(2,1)} %get-tuple-element.254.refs_0_, bf16[144,768]{1,0:T(8,128)(2,1)S(1)} %collective-permute-done.37.refs_1_, bf16[144,768]{1,0:T(8,128)(2,1)S(1)} %collective-permute-done.38.refs_2_, ...), custom_call_target="tpu_custom_call" | custom-call | flops 49999998976 | bytes 50000000 | tf_op jit(solution)/shard_map/pallas_call | solution.py:476
  215.9 2.9 %shard_map.368 = (f32[192,3072]{1,0:T(8,128)}, f32[192,768]{1,0:T(8,128)}, f32[8,128]{1,0:T(8,128)}) custom-call(s32[3]{0:T(128)S(1)} %pad_add_fusion.where_ref, bf16[48,1920]{1,0:T(8,128)(2,1)S(1)} %get-tuple-element.253.refs_0_, bf16[48,1920]{1,0:T(8,128)(2,1)S(1)} %collective-permute-done.34.refs_1_, ...), custom_call_target="tpu_custom_call" | custom-call | tf_op jit(solution)/shard_map/pallas_call | solution.py:476
  (191 shorter events, 87.8 us)
Async XLA Ops:
  3.1 25.4 %all-to-all-start = ((bf16[4,48,1920]{2,1,0:T(8,128)(2,1)}), bf16[4,48,1920]{2,1,0:T(8,128)(2,1)S(1)}, u32[]{:S(2)}, u32[]{:S(2)}) async-start(bf16[4,48,1920]{2,1,0:T(8,128)(2,1)} %bitcast.4), calls=%async_computation | async-start | bytes 1474560 | tf_op jit(solution)/shard_map/all_to_all | solution.py:405
  12.5 11.1 %collective-permute-start.1 = (bf16[160,768]{1,0:T(8,128)(2,1)S(1)}, bf16[160,768]{1,0:T(8,128)(2,1)S(1)}, u32[]{:S(2)}, u32[]{:S(2)}) collective-permute-start(bf16[160,768]{1,0:T(8,128)(2,1)S(1)} %get-tuple-element.151.refs_0_), channel_id=1, source_target_pairs={{0,16},{4,20},{8,24},{12,28},{16,0},{20,4},{24,8},{28,12},{1,17},{... | collective-permute-start | bytes 737288 | tf_op jit(solution)/shard_map/ppermute | solution.py:390
  29.1 14.7 %collective-permute-start.9 = (bf16[144,1920]{1,0:T(8,128)(2,1)S(1)}, bf16[144,1920]{1,0:T(8,128)(2,1)S(1)}, u32[]{:S(2)}, u32[]{:S(2)}) collective-permute-start(bf16[144,1920]{1,0:T(8,128)(2,1)S(1)} %get-tuple-element.164.refs_1_), channel_id=1, source_target_pairs={{0,16},{4,20},{8,24},{12,28},{16,0},{20,4},{24,8},{28,12},{1,17},{... | collective-permute-start | bytes 1658888 | tf_op jit(solution)/shard_map/ppermute | solution.py:390
  30.7 13.2 %collective-permute-start.8 = (bf16[144,1920]{1,0:T(8,128)(2,1)S(1)}, bf16[144,1920]{1,0:T(8,128)(2,1)S(1)}, u32[]{:S(2)}, u32[]{:S(2)}) collective-permute-start(bf16[144,1920]{1,0:T(8,128)(2,1)S(1)} %get-tuple-element.164.refs_1_), channel_id=1, source_target_pairs={{0,8},{4,12},{8,0},{12,4},{16,24},{20,28},{24,16},{28,20},{1,9},{5... | collective-permute-start | bytes 1658888 | tf_op jit(solution)/shard_map/ppermute | solution.py:390
  46.3 21.7 %collective-permute-start.14 = (bf16[96,768]{1,0:T(8,128)(2,1)S(1)}, bf16[96,768]{1,0:T(8,128)(2,1)S(1)}, u32[]{:S(2)}, u32[]{:S(2)}) collective-permute-start(bf16[96,768]{1,0:T(8,128)(2,1)S(1)} %get-tuple-element.171), channel_id=1, source_target_pairs={{0,3},{1,2},{2,1},{3,0},{4,7},{5,6},{6,5},{7,4},{8,11},{9,10},{10,... | collective-permute-start | bytes 442376 | tf_op jit(solution)/shard_map/ppermute | solution.py:395
  48.6 19.5 %collective-permute-start.13 = (bf16[96,768]{1,0:T(8,128)(2,1)S(1)}, bf16[96,768]{1,0:T(8,128)(2,1)S(1)}, u32[]{:S(2)}, u32[]{:S(2)}) collective-permute-start(bf16[96,768]{1,0:T(8,128)(2,1)S(1)} %get-tuple-element.171), channel_id=1, source_target_pairs={{0,2},{1,3},{2,0},{3,1},{4,6},{5,7},{6,4},{7,5},{8,10},{9,11},{10,... | collective-permute-start | bytes 442376 | tf_op jit(solution)/shard_map/ppermute | solution.py:395
  48.6 19.5 %collective-permute-start.12 = (bf16[96,768]{1,0:T(8,128)(2,1)S(1)}, bf16[96,768]{1,0:T(8,128)(2,1)S(1)}, u32[]{:S(2)}, u32[]{:S(2)}) collective-permute-start(bf16[96,768]{1,0:T(8,128)(2,1)S(1)} %get-tuple-element.171), channel_id=1, source_target_pairs={{0,1},{1,0},{2,3},{3,2},{4,5},{5,4},{6,7},{7,6},{8,9},{9,8},{10,11... | collective-permute-start | bytes 442376 | tf_op jit(solution)/shard_map/ppermute | solution.py:395
  50.8 21.2 %collective-permute-start.11 = (bf16[64,1920]{1,0:T(8,128)(2,1)S(1)}, bf16[64,1920]{1,0:T(8,128)(2,1)S(1)}, u32[]{:S(2)}, u32[]{:S(2)}) collective-permute-start(bf16[64,1920]{1,0:T(8,128)(2,1)S(1)} %get-tuple-element.170), channel_id=1, source_target_pairs={{0,16},{4,20},{8,24},{12,28},{16,0},{20,4},{24,8},{28,12},{1,17},{... | collective-permute-start | bytes 737288 | tf_op jit(solution)/shard_map/ppermute | solution.py:390
  51.3 20.7 %collective-permute-start.10 = (bf16[80,1920]{1,0:T(8,128)(2,1)S(1)}, bf16[80,1920]{1,0:T(8,128)(2,1)S(1)}, u32[]{:S(2)}, u32[]{:S(2)}) collective-permute-start(bf16[80,1920]{1,0:T(8,128)(2,1)S(1)} %get-tuple-element.169), channel_id=1, source_target_pairs={{0,8},{4,12},{8,0},{12,4},{16,24},{20,28},{24,16},{28,20},{1,9},{5... | collective-permute-start | bytes 921608 | tf_op jit(solution)/shard_map/ppermute | solution.py:390
  63.7 21.6 %all-to-all-start.1 = ((bf16[4,160,192]{2,1,0:T(8,128)(2,1)}), bf16[4,160,192]{2,1,0:T(8,128)(2,1)}, u32[]{:S(2)}, u32[]{:S(2)}) async-start(bf16[4,160,192]{2,1,0:T(8,128)(2,1)} %bitcast.6), calls=%async_computation.1 | async-start | bytes 655360 | tf_op jit(solution)/shard_map/all_to_all | solution.py:401
  68.6 13.2 %collective-permute-start.17 = (bf16[288,768]{1,0:T(8,128)(2,1)S(1)}, bf16[288,768]{1,0:T(8,128)(2,1)S(1)}, u32[]{:S(2)}, u32[]{:S(2)}) collective-permute-start(bf16[288,768]{1,0:T(8,128)(2,1)S(1)} %get-tuple-element.179.refs_1_), channel_id=1, source_target_pairs={{0,16},{4,20},{8,24},{12,28},{16,0},{20,4},{24,8},{28,12},{1,17},{... | collective-permute-start | bytes 1327112 | tf_op jit(solution)/shard_map/ppermute | solution.py:390
  70.5 11.5 %collective-permute-start.16 = (bf16[288,768]{1,0:T(8,128)(2,1)S(1)}, bf16[288,768]{1,0:T(8,128)(2,1)S(1)}, u32[]{:S(2)}, u32[]{:S(2)}) collective-permute-start(bf16[288,768]{1,0:T(8,128)(2,1)S(1)} %get-tuple-element.179.refs_1_), channel_id=1, source_target_pairs={{0,8},{4,12},{8,0},{12,4},{16,24},{20,28},{24,16},{28,20},{1,9},{5... | collective-permute-start | bytes 1327112 | tf_op jit(solution)/shard_map/ppermute | solution.py:390
  105.5 16.4 %collective-permute-start.20 = (bf16[384,768]{1,0:T(8,128)(2,1)}, bf16[384,768]{1,0:T(8,128)(2,1)}, u32[]{:S(2)}, u32[]{:S(2)}) collective-permute-start(bf16[384,768]{1,0:T(8,128)(2,1)} %get-tuple-element.213), channel_id=1, source_target_pairs={{0,8},{4,12},{8,0},{12,4},{16,24},{20,28},{24,16},{28,20},{1,9},{5... | collective-permute-start | bytes 1769480 | tf_op jit(solution)/shard_map/ppermute | solution.py:390
  106.8 15.4 %collective-permute-start.21 = (bf16[384,768]{1,0:T(8,128)(2,1)}, bf16[384,768]{1,0:T(8,128)(2,1)}, u32[]{:S(2)}, u32[]{:S(2)}) collective-permute-start(bf16[384,768]{1,0:T(8,128)(2,1)} %get-tuple-element.214), channel_id=1, source_target_pairs={{0,16},{4,20},{8,24},{12,28},{16,0},{20,4},{24,8},{28,12},{1,17},{... | collective-permute-start | bytes 1769480 | tf_op jit(solution)/shard_map/ppermute | solution.py:390
  116.5 20.6 %all-to-all-start.2 = ((bf16[4,144,192]{2,1,0:T(8,128)(2,1)}), bf16[4,144,192]{2,1,0:T(8,128)(2,1)S(1)}, u32[]{:S(2)}, u32[]{:S(2)}) async-start(bf16[4,144,192]{2,1,0:T(8,128)(2,1)} %bitcast.11), calls=%async_computation.2 | async-start | bytes 589824 | tf_op jit(solution)/shard_map/all_to_all | solution.py:401
  123.7 11.1 %collective-permute-start.22 = (bf16[192,768]{1,0:T(8,128)(2,1)S(1)}, bf16[192,768]{1,0:T(8,128)(2,1)S(1)}, u32[]{:S(2)}, u32[]{:S(2)}) collective-permute-start(bf16[192,768]{1,0:T(8,128)(2,1)S(1)} %get-tuple-element.220), channel_id=1, source_target_pairs={{0,8},{4,12},{8,0},{12,4},{16,24},{20,28},{24,16},{28,20},{1,9},{5... | collective-permute-start | bytes 884744 | tf_op jit(solution)/shard_map/ppermute | solution.py:390
  131.2 33.5 %collective-permute-start.27 = (bf16[192,1920]{1,0:T(8,128)(2,1)}, bf16[192,1920]{1,0:T(8,128)(2,1)S(1)}, u32[]{:S(2)}, u32[]{:S(2)}) collective-permute-start(bf16[192,1920]{1,0:T(8,128)(2,1)} %get-tuple-element.241), channel_id=1, source_target_pairs={{0,8},{4,12},{8,0},{12,4},{16,24},{20,28},{24,16},{28,20},{1,9},{5... | collective-permute-start | bytes 2211848 | tf_op jit(solution)/shard_map/ppermute | solution.py:390
  131.9 34.2 %collective-permute-start.28 = (bf16[192,1920]{1,0:T(8,128)(2,1)}, bf16[192,1920]{1,0:T(8,128)(2,1)}, u32[]{:S(2)}, u32[]{:S(2)}) collective-permute-start(bf16[192,1920]{1,0:T(8,128)(2,1)} %get-tuple-element.242), channel_id=1, source_target_pairs={{0,16},{4,20},{8,24},{12,28},{16,0},{20,4},{24,8},{28,12},{1,17},{... | collective-permute-start | bytes 2211848 | tf_op jit(solution)/shard_map/ppermute | solution.py:390
  132.4 33.7 %collective-permute-start.29 = (bf16[192,1920]{1,0:T(8,128)(2,1)}, bf16[192,1920]{1,0:T(8,128)(2,1)}, u32[]{:S(2)}, u32[]{:S(2)}) collective-permute-start(bf16[192,1920]{1,0:T(8,128)(2,1)} %get-tuple-element.243), channel_id=1, source_target_pairs={{0,24},{4,28},{8,16},{12,20},{16,8},{20,12},{24,0},{28,4},{1,25},{... | collective-permute-start | bytes 2211848 | tf_op jit(solution)/shard_map/ppermute | solution.py:390
  137.1 19.9 %all-to-all-start.3 = ((bf16[4,96,768]{2,1,0:T(8,128)(2,1)}), bf16[4,96,768]{2,1,0:T(8,128)(2,1)S(1)}, u32[]{:S(2)}, u32[]{:S(2)}) async-start(bf16[4,96,768]{2,1,0:T(8,128)(2,1)} %bitcast.13), calls=%async_computation.3 | async-start | bytes 1179648 | tf_op jit(solution)/shard_map/all_to_all | solution.py:405
  154.1 20.4 %collective-permute-start.26 = (bf16[576,768]{1,0:T(8,128)(2,1)S(1)}, bf16[576,768]{1,0:T(8,128)(2,1)S(1)}, u32[]{:S(2)}, u32[]{:S(2)}) collective-permute-start(bf16[576,768]{1,0:T(8,128)(2,1)S(1)} %get-tuple-element.239), channel_id=1, source_target_pairs={{0,4},{4,0},{8,12},{12,8},{16,20},{20,16},{24,28},{28,24},{1,5},{5... | collective-permute-start | bytes 2654216 | tf_op jit(solution)/shard_map/ppermute | solution.py:380
  159.9 20.0 %all-to-all-start.4 = ((bf16[4,96,640]{2,1,0:T(8,128)(2,1)}), bf16[4,96,640]{2,1,0:T(8,128)(2,1)S(1)}, u32[]{:S(2)}, u32[]{:S(2)}) async-start(bf16[4,96,640]{2,1,0:T(8,128)(2,1)} %bitcast.15), calls=%async_computation.4 | async-start | bytes 983040 | tf_op jit(solution)/shard_map/all_to_all | solution.py:405
  170.1 15.3 %collective-permute-start.31 = (bf16[48,1920]{1,0:T(8,128)(2,1)}, bf16[48,1920]{1,0:T(8,128)(2,1)}, u32[]{:S(2)}, u32[]{:S(2)}) collective-permute-start(bf16[48,1920]{1,0:T(8,128)(2,1)} %get-tuple-element.249), channel_id=1, source_target_pairs={{0,1},{1,0},{2,3},{3,2},{4,5},{5,4},{6,7},{7,6},{8,9},{9,8},{10,11... | collective-permute-start | bytes 552968 | tf_op jit(solution)/shard_map/ppermute | solution.py:395
  170.8 21.0 %collective-permute-start.32 = (bf16[48,1920]{1,0:T(8,128)(2,1)}, bf16[48,1920]{1,0:T(8,128)(2,1)}, u32[]{:S(2)}, u32[]{:S(2)}) collective-permute-start(bf16[48,1920]{1,0:T(8,128)(2,1)} %get-tuple-element.250), channel_id=1, source_target_pairs={{0,2},{1,3},{2,0},{3,1},{4,6},{5,7},{6,4},{7,5},{8,10},{9,11},{10,... | collective-permute-start | bytes 552968 | tf_op jit(solution)/shard_map/ppermute | solution.py:395
  173.2 18.6 %collective-permute-start.33 = (bf16[48,1920]{1,0:T(8,128)(2,1)}, bf16[48,1920]{1,0:T(8,128)(2,1)}, u32[]{:S(2)}, u32[]{:S(2)}) collective-permute-start(bf16[48,1920]{1,0:T(8,128)(2,1)} %get-tuple-element.251), channel_id=1, source_target_pairs={{0,3},{1,2},{2,1},{3,0},{4,7},{5,6},{6,5},{7,4},{8,11},{9,10},{10,... | collective-permute-start | bytes 552968 | tf_op jit(solution)/shard_map/ppermute | solution.py:395
  175.9 19.3 %collective-permute-start.37 = (bf16[144,768]{1,0:T(8,128)(2,1)S(1)}, bf16[144,768]{1,0:T(8,128)(2,1)S(1)}, u32[]{:S(2)}, u32[]{:S(2)}) collective-permute-start(bf16[144,768]{1,0:T(8,128)(2,1)S(1)} %get-tuple-element.255), channel_id=1, source_target_pairs={{0,8},{4,12},{8,0},{12,4},{16,24},{20,28},{24,16},{28,20},{1,9},{5... | collective-permute-start | bytes 663560 | tf_op jit(solution)/shard_map/ppermute | solution.py:390
  177.3 19.3 %collective-permute-start.38 = (bf16[144,768]{1,0:T(8,128)(2,1)S(1)}, bf16[144,768]{1,0:T(8,128)(2,1)S(1)}, u32[]{:S(2)}, u32[]{:S(2)}) collective-permute-start(bf16[144,768]{1,0:T(8,128)(2,1)S(1)} %get-tuple-element.256), channel_id=1, source_target_pairs={{0,16},{4,20},{8,24},{12,28},{16,0},{20,4},{24,8},{28,12},{1,17},{... | collective-permute-start | bytes 663560 | tf_op jit(solution)/shard_map/ppermute | solution.py:390
  181.7 23.1 %all-to-all-start.5 = ((bf16[4,192,768]{2,1,0:T(8,128)(2,1)}), bf16[4,192,768]{2,1,0:T(8,128)(2,1)S(1)}, u32[]{:S(2)}, u32[]{:S(2)}) async-start(bf16[4,192,768]{2,1,0:T(8,128)(2,1)} %bitcast.17), calls=%async_computation.5 | async-start | bytes 2359296 | tf_op jit(solution)/shard_map/all_to_all | solution.py:401
  185.4 22.2 %collective-permute-start.39 = (bf16[144,768]{1,0:T(8,128)(2,1)S(1)}, bf16[144,768]{1,0:T(8,128)(2,1)}, u32[]{:S(2)}, u32[]{:S(2)}) collective-permute-start(bf16[144,768]{1,0:T(8,128)(2,1)S(1)} %get-tuple-element.257), channel_id=1, source_target_pairs={{0,24},{4,28},{8,16},{12,20},{16,8},{20,12},{24,0},{28,4},{1,25},{... | collective-permute-start | bytes 663560 | tf_op jit(solution)/shard_map/ppermute | solution.py:390
  193.1 17.7 %collective-permute-start.36 = (bf16[48,1920]{1,0:T(8,128)(2,1)S(1)}, bf16[48,1920]{1,0:T(8,128)(2,1)S(1)}, u32[]{:S(2)}, u32[]{:S(2)}) collective-permute-start(bf16[48,1920]{1,0:T(8,128)(2,1)S(1)} %get-tuple-element.253.refs_0_), channel_id=1, source_target_pairs={{0,24},{4,28},{8,16},{12,20},{16,8},{20,12},{24,0},{28,4},{1,25},{... | collective-permute-start | bytes 552968 | tf_op jit(solution)/shard_map/ppermute | solution.py:390
  194.3 16.8 %collective-permute-start.35 = (bf16[48,1920]{1,0:T(8,128)(2,1)S(1)}, bf16[48,1920]{1,0:T(8,128)(2,1)S(1)}, u32[]{:S(2)}, u32[]{:S(2)}) collective-permute-start(bf16[48,1920]{1,0:T(8,128)(2,1)S(1)} %get-tuple-element.253.refs_0_), channel_id=1, source_target_pairs={{0,16},{4,20},{8,24},{12,28},{16,0},{20,4},{24,8},{28,12},{1,17},{... | collective-permute-start | bytes 552968 | tf_op jit(solution)/shard_map/ppermute | solution.py:390
  195.2 16.0 %collective-permute-start.34 = (bf16[48,1920]{1,0:T(8,128)(2,1)S(1)}, bf16[48,1920]{1,0:T(8,128)(2,1)S(1)}, u32[]{:S(2)}, u32[]{:S(2)}) collective-permute-start(bf16[48,1920]{1,0:T(8,128)(2,1)S(1)} %get-tuple-element.253.refs_0_), channel_id=1, source_target_pairs={{0,8},{4,12},{8,0},{12,4},{16,24},{20,28},{24,16},{28,20},{1,9},{5... | collective-permute-start | bytes 552968 | tf_op jit(solution)/shard_map/ppermute | solution.py:390
  (58 other events, 335.0 us)

commit v5 on v4

--- a/solution.py
+++ b/solution.py
@@ -890,23 +890,21 @@
 
 
 def activate(where, h_pair, w_up, b_up, act, slope):
-    rows = h_pair.shape[0] // 2
     root = 0.7978845608028654
-    for i in range(2):
-        block = slice(rows * i, rows * (i + 1))
-        value = dot(h_pair[block, :], w_up[...], NN) + b_up[...]
-        square = value * value
-        bent = jnp.tanh(root * value * (1.0 + 0.044715 * square))
-        act[block, :] = (0.5 * value * (1.0 + bent)).astype(BF16)
-        slope[block, :] = 0.5 * (1.0 + bent) + 0.5 * value * (1.0 - bent * bent) * root * (
-            1.0 + 3.0 * 0.044715 * square
-        )
-
-
-def project_down(where, act, w_down, near, far):
+    value = dot(h_pair[...], w_up[...], NN) + b_up[...]
+    square = value * value
+    bent = jnp.tanh(root * value * (1.0 + 0.044715 * square))
+    act[...] = (0.5 * value * (1.0 + bent)).astype(BF16)
+    slope[...] = 0.5 * (1.0 + bent) + 0.5 * value * (1.0 - bent * bent) * root * (
+        1.0 + 3.0 * 0.044715 * square
+    )
+
+
+def project_down(where, act, w_down, near, far, both):
     rows, core = near.shape[0], where[1]
-    near[...] = dot(act[core_rows(core, rows), :], w_down[...], NN)
-    far[...] = dot(act[core_rows(1 - core, rows), :], w_down[...], NN).astype(BF16)
+    both[...] = dot(act[...], w_down[...], NN)
+    near[...] = both[core_rows(core, rows), :]
+    far[...] = both[core_rows(1 - core, rows), :].astype(BF16)
 
 
 def compare(where, second, near, far, vectors, teacher, cotangent, valid, count, *outs):
@@ -934,17 +932,14 @@
     lines[2:, :] = jnp.zeros((6, width), F32)
 
 
-def activate_back(where, d_down, w_down, slope, w_up, d_up, near, far, line):
+def activate_back(where, d_down, w_down, slope, w_up, d_up, near, far, line, both):
     rows, core = near.shape[0], where[1]
-    total = jnp.zeros(line.shape, F32)
-    for i in range(2):
-        block = slice(rows * i, rows * (i + 1))
-        low = (dot(d_down[block, :], w_down[...], NT) * slope[block, :]).astype(BF16)
-        d_up[block, :] = low
-        total += jnp.sum(low.astype(F32), axis=0, keepdims=True)
-    line[...] = total
-    near[...] = dot(d_up[core_rows(core, rows), :], w_up[...], NT)
-    far[...] = dot(d_up[core_rows(1 - core, rows), :], w_up[...], NT).astype(BF16)
+    low = (dot(d_down[...], w_down[...], NT) * slope[...]).astype(BF16)
+    d_up[...] = low
+    line[...] = jnp.sum(low.astype(F32), axis=0, keepdims=True)
+    both[...] = dot(low, w_up[...], NT)
+    near[...] = both[core_rows(core, rows), :]
+    far[...] = both[core_rows(1 - core, rows), :].astype(BF16)
 
 
 def second_back(where, near, far, d_result, second, vectors, w_output, *outs):
@@ -1046,7 +1041,7 @@
     out[...] = total.astype(out.dtype)
 
 
-def finish_down(where, near, far, out, held, sems):
+def start_down(where, near, far, out, held, sems):
     core = where[1]
     both = near.shape[0] // 4
     part = both // 2
@@ -1058,8 +1053,7 @@
             held[at, :] = piece[block, :].astype(F32)
             copies.append(pltpu.make_async_copy(held.at[at], out.at[at], sems.at[len(copies)]))
             copies[-1].start()
-    for copy in copies:
-        copy.wait()
+    return copies
 
 
 def finish_up(where, n0, n1, n2, n3, far, out, out_half, held, held_half, sems):
@@ -1175,6 +1169,14 @@
     up_line[...] = whole_line[0]
     error = jnp.sum(total[10:11, :3], axis=1, keepdims=True)
     loss[0, 0] = jnp.sum(error / (width * count[0:1, 0:1]))
+
+
+def finish_gathered(where, near, far, count, *refs):
+    outs, down, scratch = refs[:13], refs[13], refs[14:]
+    copies = start_down(where, near, far, down, scratch[2], scratch[3])
+    finish_projections(where, near, far, count, *outs, *scratch[:2])
+    for copy in copies:
+        copy.wait()
 
 
 def layer(
@@ -1348,7 +1350,10 @@
         build_down, shaped(units, width), (down_weight, *down_all), far=(0,), scratch=[dma]
     )
     down_near, down_other = step(
-        project_down, (wide(rows, width), shaped(rows, width)), (act, w_down)
+        project_down,
+        (wide(rows, width), shaped(rows, width)),
+        (act, w_down),
+        scratch=[pltpu.VMEM((2 * rows, width), F32)],
     )
     layer_output, d_result, d_down, from_result = step(
         compare,
@@ -1389,6 +1394,7 @@
         activate_back,
         (shaped(2 * rows, units), wide(rows, width), shaped(rows, width), wide(1, units)),
         (d_down, w_down, slope, w_up),
+        scratch=[pltpu.VMEM((2 * rows, width), F32)],
         cost=50,
     )
     d_second, d_attn, from_second, d_sent = step(
@@ -1479,22 +1485,22 @@
     both = (both, swap_cores(both))
     up_whole = whole(up_near)
     finished = step(
-        finish_projections,
+        finish_gathered,
         (wide(shard, width),) * 3
         + (wide(1, 1),)
         + (wide(shard),) * 8
-        + (wide(own_units),),
+        + (wide(own_units), wide(own_units, width)),
         (*both, count),
-        scratch=[pltpu.VMEM((8, 16, feat), F32), pltpu.VMEM((8, own_units), F32)],
+        far_outs=(13,),
+        scratch=[
+            pltpu.VMEM((8, 16, feat), F32),
+            pltpu.VMEM((8, own_units), F32),
+            pltpu.VMEM((own_units, width), F32),
+            dma((8,)),
+        ],
         scalar=3,
     )
-    grad_down_weight = step(
-        finish_down,
-        wide(own_units, width),
-        both,
-        far_outs=(0,),
-        scratch=[pltpu.VMEM((own_units, width), F32), dma((8,))],
-    )
+    grad_down_weight = finished[13]
     grad_up_weight, grad_output_weight = step(
         finish_up,
         (wide(shard, hidden), wide(shard, width)),

time: 220 us -> 220 us (level)
  waiting for transfers between devices: 41.6 us -> 43.9 us
    ppermute x24, waiting for transfers between devices: 17.4 us -> 20.1 us  [swap_chips(): return lax.ppermute(value, 'ctx', [(i, i ^ 2 * step) for i in range(size)])]
    pallas_call x38 -> x37, Pallas kernels: 90.2 us -> 88.3 us  [local_call(): pl.pallas_call(kernel, out_shape=(*(pltpu.HBM(o.shape, o.dtype) if i in f...]
  transfers between devices with their start and end apart: 47 -> 47, of which waited for: 17 -> 17; matrix products, arithmetic and copies ran while one was open for 0% -> 0% of each run, Pallas kernels for 35% -> 34%
where the time goes in v5:
time: 220 us; the launch traced here: 219 us
  Pallas kernels  88.3 us (40%)
  starting transfers between devices  71.2 us (32%)
  waiting for transfers between devices  43.9 us (20%)
  blocking collectives  8.61 us (4%)
  local copies, waits for them, and re-layouts  5.27 us (2%)
    pallas_call x37, Pallas kernels, local_call(): pl.pallas_call(kernel, out_shape=(*(pltpu.HBM(o.shape, o.dtype) if i in f...  88.3 us
    ppermute x24, starting transfers between devices, swap_chips(): return lax.ppermute(value, 'ctx', [(i, i ^ 2 * step) for i in range(size)])  30.3 us
    ppermute x24, waiting for transfers between devices, swap_chips(): return lax.ppermute(value, 'ctx', [(i, i ^ 2 * step) for i in range(size)])  20.1 us
    all_to_all x3, starting transfers between devices, trade_planes(): return lax.all_to_all(value, 'fsdp', 0, 0, tiled=True)  14.9 us
    ppermute x9, starting transfers between devices, swap_planes(): return lax.ppermute(value, 'fsdp', [(i, i ^ step) for i in range(size)])  13.4 us
    all_to_all x3, starting transfers between devices, trade_chips(): lax.all_to_all(value, 'ctx', 0, 0, axis_index_groups=groups, tiled=True)  11.7 us
    all_gather x4, blocking collectives, both_cores(): lax.all_gather(value, 'ctx', axis=0, tiled=True, axis_index_groups=pairs)  8.61 us
    all_to_all x3, waiting for transfers between devices, trade_chips(): lax.all_to_all(value, 'ctx', 0, 0, axis_index_groups=groups, tiled=True)  7.95 us
  transfers between devices with their start and end apart: 47, of which 17 were waited for; matrix products, arithmetic and copies ran while one was open for 0% of the time, Pallas kernels for 34%

profile of v5, /device:TPU:0, one launch (start us, length us, event | category | flops | bytes accessed | tf_op | source)
XLA Modules:
  0.0 219.0 jit_solution(5189768748704089414)
XLA Ops:
  3.1 6.3 %all-to-all-start = ((bf16[4,48,1920]{2,1,0:T(8,128)(2,1)}), bf16[4,48,1920]{2,1,0:T(8,128)(2,1)S(1)}, u32[]{:S(2)}, u32[]{:S(2)}) async-start(bf16[4,48,1920]{2,1,0:T(8,128)(2,1)} %bitcast.4), calls=%async_computation | async-start | bytes 1474560 | tf_op jit(solution)/shard_map/all_to_all | solution.py:405
  10.0 2.5 %collective-permute-start.2 = (bf16[160,768]{1,0:T(8,128)(2,1)S(1)}, bf16[160,768]{1,0:T(8,128)(2,1)S(1)}, u32[]{:S(2)}, u32[]{:S(2)}) collective-permute-start(bf16[160,768]{1,0:T(8,128)(2,1)S(1)} %get-tuple-element.150.refs_0_), channel_id=1, source_target_pairs={{0,24},{4,28},{8,16},{12,20},{16,8},{20,12},{24,0},{28,4},{1,25},{... | collective-permute-start | bytes 737288 | tf_op jit(solution)/shard_map/ppermute | solution.py:390
  15.6 4.4 %collective-permute-done.2.refs_3_ = bf16[160,768]{1,0:T(8,128)(2,1)S(1)} collective-permute-done((bf16[160,768]{1,0:T(8,128)(2,1)S(1)}, bf16[160,768]{1,0:T(8,128)(2,1)S(1)}, u32[]{:S(2)}, u32[]{:S(2)}) %collective-permute-start.2) | collective-permute-done | bytes 245792 | tf_op jit(solution)/shard_map/ppermute | solution.py:390
  19.9 3.8 %collective-permute-done.1.refs_2_ = bf16[160,768]{1,0:T(8,128)(2,1)S(1)} collective-permute-done((bf16[160,768]{1,0:T(8,128)(2,1)S(1)}, bf16[160,768]{1,0:T(8,128)(2,1)S(1)}, u32[]{:S(2)}, u32[]{:S(2)}) %collective-permute-start.1) | collective-permute-done | bytes 245792 | tf_op jit(solution)/shard_map/ppermute | solution.py:390
  24.5 4.0 %all-to-all-done = bf16[4,48,1920]{2,1,0:T(8,128)(2,1)S(1)} async-done(((bf16[4,48,1920]{2,1,0:T(8,128)(2,1)}), bf16[4,48,1920]{2,1,0:T(8,128)(2,1)S(1)}, u32[]{:S(2)}, u32[]{:S(2)}) %all-to-all-start) | async-done | bytes 737312 | tf_op jit(solution)/shard_map/all_to_all | solution.py:405
  33.7 2.9 %collective-permute-start.4 = (bf16[96,640]{1,0:T(8,128)(2,1)S(1)}, bf16[96,640]{1,0:T(8,128)(2,1)S(1)}, u32[]{:S(2)}, u32[]{:S(2)}) collective-permute-start(bf16[96,640]{1,0:T(8,128)(2,1)S(1)} %get-tuple-element.160.refs_0_.refs_3_), channel_id=1, source_target_pairs={{0,1},{1,0},{2,3},{3,2},{4,5},{5,4},{6,7},{7,6},{8,9},{9,8},{10,11... | collective-permute-start | bytes 368648 | tf_op jit(solution)/shard_map/ppermute | solution.py:395
  36.6 2.4 %shard_map.336 = (f32[1152,768]{1,0:T(8,128)S(1)}, f32[8,1152]{1,0:T(8,128)S(1)}, f32[576,128]{1,0:T(8,128)S(1)}, f32[8,128]{1,0:T(8,128)S(1)}) custom-call(s32[3]{0:T(128)S(1)} %pad_add_fusion.where_ref, bf16[640,768]{1,0:T(8,128)(2,1)S(1)} %get-tuple-element.153.refs_0_, bf16[640,768]{1,0:T(8,128)(2,1)} %collective-permute-done.3.refs_1_, ...), custom_call_target="tpu_custom_call" | custom-call | flops 1000000000 | bytes 1000000 | tf_op jit(solution)/shard_map/pallas_call | solution.py:476
  40.3 2.9 %collective-permute-done.5.refs_2_.refs_5_ = bf16[96,640]{1,0:T(8,128)(2,1)S(1)} collective-permute-done((bf16[96,640]{1,0:T(8,128)(2,1)S(1)}, bf16[96,640]{1,0:T(8,128)(2,1)S(1)}, u32[]{:S(2)}, u32[]{:S(2)}) %collective-permute-start.5) | collective-permute-done | bytes 122912 | tf_op jit(solution)/shard_map/ppermute | solution.py:395
  52.7 10.5 %shard_map.340 = (bf16[1152,768]{1,0:T(8,128)(2,1)}, bf16[768,576]{1,0:T(8,128)(2,1)}, bf16[1152,576]{1,0:T(8,128)(2,1)}, bf16[3,576,1152]{2,1,0:T(8,128)(2,1)},...) custom-call(s32[3]{0:T(128)S(1)} %pad_add_fusion.where_ref, ...), custom_call_target="tpu_custom_call" | custom-call | flops 49999998976 | bytes 50000000 | tf_op jit(solution)/shard_map/pallas_call | solution.py:476
  63.7 4.3 %all-to-all-start.1 = ((bf16[4,160,192]{2,1,0:T(8,128)(2,1)}), bf16[4,160,192]{2,1,0:T(8,128)(2,1)}, u32[]{:S(2)}, u32[]{:S(2)}) async-start(bf16[4,160,192]{2,1,0:T(8,128)(2,1)} %bitcast.6), calls=%async_computation.1 | async-start | bytes 655360 | tf_op jit(solution)/shard_map/all_to_all | solution.py:401
  74.6 2.4 %shard_map.343 = (bf16[768,1536]{1,0:T(8,128)(2,1)S(1)}, f32[8,128]{1,0:T(8,128)S(1)}) custom-call(s32[3]{0:T(128)S(1)} %pad_add_fusion.where_ref, bf16[192,3072]{1,0:T(8,128)(2,1)} %refs_0_.10, bf16[144,1920]{1,0:T(8,128)(2,1)} %copy-done.4, bf16[144,1920]{1,0:T(8,128)(2,1)} %copy-done.6, bf16[144,1920]{1,0:T(8,128)(2,1)} %copy-done.5, ...), custom_call_target="tpu_custom_call" | custom-call | flops 49999998976 | bytes 50000000 | tf_op jit(solution)/shard_map/pallas_call | solution.py:476
  77.8 4.1 %collective-permute-done.17.refs_1_.refs_3_ = bf16[288,768]{1,0:T(8,128)(2,1)S(1)} collective-permute-done((bf16[288,768]{1,0:T(8,128)(2,1)S(1)}, bf16[288,768]{1,0:T(8,128)(2,1)S(1)}, u32[]{:S(2)}, u32[]{:S(2)}) %collective-permute-start.17) | collective-permute-done | bytes 442400 | tf_op jit(solution)/shard_map/ppermute | solution.py:390
  102.6 3.1 %shard_map.351 = (bf16[384,768]{1,0:T(8,128)(2,1)S(1)}, bf16[384,768]{1,0:T(8,128)(2,1)}, bf16[384,768]{1,0:T(8,128)(2,1)}, bf16[192,768]{1,0:T(8,128)(2,1)S(1)}...) custom-call(s32[3]{0:T(128)S(1)} %pad_add_fusion.where_ref, bf16[288,1536]{1,0:T(8,128)(2,1)S(1)} %get-tuple-element.186.refs_0_, ...), custom_call_target="tpu_custom_call" | custom-call | tf_op jit(solution)/shard_map/pallas_call | solution.py:476
  115.2 3.5 %all-to-all-start.2 = ((bf16[4,144,192]{2,1,0:T(8,128)(2,1)}), bf16[4,144,192]{2,1,0:T(8,128)(2,1)S(1)}, u32[]{:S(2)}, u32[]{:S(2)}) async-start(bf16[4,144,192]{2,1,0:T(8,128)(2,1)} %bitcast.11), calls=%async_computation.2 | async-start | bytes 589824 | tf_op jit(solution)/shard_map/all_to_all | solution.py:401
  121.4 3.1 %collective-permute-done.21.refs_1_.refs_2_ = bf16[384,768]{1,0:T(8,128)(2,1)} collective-permute-done((bf16[384,768]{1,0:T(8,128)(2,1)}, bf16[384,768]{1,0:T(8,128)(2,1)}, u32[]{:S(2)}, u32[]{:S(2)}) %collective-permute-start.21) | collective-permute-done | bytes 589856 | tf_op jit(solution)/shard_map/ppermute | solution.py:390
  127.2 4.5 %shard_map.356 = (bf16[192,1920]{1,0:T(8,128)(2,1)}, bf16[192,1920]{1,0:T(8,128)(2,1)}, bf16[192,1920]{1,0:T(8,128)(2,1)}, bf16[192,1920]{1,0:T(8,128)(2,1)}, f32[8,128]{1,0:T(8,128)S(1)}) custom-call(s32[3]{0:T(128)S(1)} %pad_add_fusion.where_ref, bf16[288,768]{1,0:T(8,128)(2,1)S(1)} %copy-done.1, bf16[288,1536]{1,0:T(8,128)(2,1)S(1)} %copy-done.36, ...), custom_call_target="tpu_custom_call" | custom-call | flops 5000000000 | bytes 5000000 | tf_op jit(solution)/shard_map/pallas_call | solution.py:476
  137.5 3.7 %all-to-all-start.3 = ((bf16[4,96,768]{2,1,0:T(8,128)(2,1)}), bf16[4,96,768]{2,1,0:T(8,128)(2,1)S(1)}, u32[]{:S(2)}, u32[]{:S(2)}) async-start(bf16[4,96,768]{2,1,0:T(8,128)(2,1)} %bitcast.13), calls=%async_computation.3 | async-start | bytes 1179648 | tf_op jit(solution)/shard_map/all_to_all | solution.py:405
  141.3 12.4 %shard_map.358 = (bf16[576,768]{1,0:T(8,128)(2,1)S(1)}, bf16[576,768]{1,0:T(8,128)(2,1)S(1)}, bf16[384,576]{1,0:T(8,128)(2,1)}, bf16[384,576]{1,0:T(8,128)(2,1)}...) custom-call(s32[3]{0:T(128)S(1)} %pad_add_fusion.where_ref, bf16[576,192]{1,0:T(8,128)(2,1)S(1)} %bitcast.26, ...), custom_call_target="tpu_custom_call" | custom-call | flops 49999998976 | bytes 50000000 | tf_op jit(solution)/shard_map/pallas_call | solution.py:476
  155.1 2.4 %collective-permute-done.25.refs_1_ = bf16[384,576]{1,0:T(8,128)(2,1)} collective-permute-done((bf16[384,576]{1,0:T(8,128)(2,1)}, bf16[384,576]{1,0:T(8,128)(2,1)}, u32[]{:S(2)}, u32[]{:S(2)}) %collective-permute-start.25) | collective-permute-done | bytes 442400 | tf_op jit(solution)/shard_map/ppermute | solution.py:380
  157.4 2.9 %shard_map.359 = (bf16[384,640]{1,0:T(8,128)(2,1)}, bf16[96,768]{1,0:T(8,128)(2,1)S(1)}, f32[8,128]{1,0:T(8,128)S(1)}) custom-call(s32[3]{0:T(128)S(1)} %pad_add_fusion.where_ref, bf16[384,576]{1,0:T(8,128)(2,1)} %get-tuple-element.227.refs_0_, bf16[384,576]{1,0:T(8,128)(2,1)} %collective-permute-done.25.refs_1_, f32[8,768]{1,0:T(8,128)S(1)} %get-tuple-element.229.refs_2_, ...), custom_call_target="tpu_custom_call" | custom-call | flops 1000000000 | bytes 1000000 | tf_op jit(solution)/shard_map/pallas_call | solution.py:476
  160.3 4.8 %all-to-all-start.4 = ((bf16[4,96,640]{2,1,0:T(8,128)(2,1)}), bf16[4,96,640]{2,1,0:T(8,128)(2,1)S(1)}, u32[]{:S(2)}, u32[]{:S(2)}) async-start(bf16[4,96,640]{2,1,0:T(8,128)(2,1)} %bitcast.15), calls=%async_computation.4 | async-start | bytes 983040 | tf_op jit(solution)/shard_map/all_to_all | solution.py:405
  165.1 4.0 %shard_map.360 = (bf16[48,1920]{1,0:T(8,128)(2,1)S(1)}, bf16[48,1920]{1,0:T(8,128)(2,1)}, bf16[48,1920]{1,0:T(8,128)(2,1)}, bf16[48,1920]{1,0:T(8,128)(2,1)}, f32[8,128]{1,0:T(8,128)S(1)}) custom-call(s32[3]{0:T(128)S(1)} %pad_add_fusion.where_ref, bf16[192,1920]{1,0:T(8,128)(2,1)} %get-tuple-element.239.refs_0_, ...), custom_call_target="tpu_custom_call" | custom-call | flops 49999998976 | bytes 50000000 | tf_op jit(solution)/shard_map/pallas_call | solution.py:476
  171.2 2.4 %collective-permute-start.32 = (bf16[48,1920]{1,0:T(8,128)(2,1)}, bf16[48,1920]{1,0:T(8,128)(2,1)}, u32[]{:S(2)}, u32[]{:S(2)}) collective-permute-start(bf16[48,1920]{1,0:T(8,128)(2,1)} %get-tuple-element.249), channel_id=1, source_target_pairs={{0,2},{1,3},{2,0},{3,1},{4,6},{5,7},{6,4},{7,5},{8,10},{9,11},{10,... | collective-permute-start | bytes 552968 | tf_op jit(solution)/shard_map/ppermute | solution.py:395
  182.2 3.9 %all-to-all-start.5 = ((bf16[4,192,768]{2,1,0:T(8,128)(2,1)}), bf16[4,192,768]{2,1,0:T(8,128)(2,1)S(1)}, u32[]{:S(2)}, u32[]{:S(2)}) async-start(bf16[4,192,768]{2,1,0:T(8,128)(2,1)} %bitcast.17), calls=%async_computation.5 | async-start | bytes 2359296 | tf_op jit(solution)/shard_map/all_to_all | solution.py:401
  186.1 2.9 %collective-permute-start.39 = (bf16[144,768]{1,0:T(8,128)(2,1)S(1)}, bf16[144,768]{1,0:T(8,128)(2,1)}, u32[]{:S(2)}, u32[]{:S(2)}) collective-permute-start(bf16[144,768]{1,0:T(8,128)(2,1)S(1)} %get-tuple-element.256), channel_id=1, source_target_pairs={{0,24},{4,28},{8,16},{12,20},{16,8},{20,12},{24,0},{28,4},{1,25},{... | collective-permute-start | bytes 663560 | tf_op jit(solution)/shard_map/ppermute | solution.py:390
  189.0 3.2 %collective-permute-done.32.refs_2_ = bf16[48,1920]{1,0:T(8,128)(2,1)} collective-permute-done((bf16[48,1920]{1,0:T(8,128)(2,1)}, bf16[48,1920]{1,0:T(8,128)(2,1)}, u32[]{:S(2)}, u32[]{:S(2)}) %collective-permute-start.32) | collective-permute-done | bytes 184352 | tf_op jit(solution)/shard_map/ppermute | solution.py:395
  193.5 2.6 %collective-permute-start.36 = (bf16[48,1920]{1,0:T(8,128)(2,1)S(1)}, bf16[48,1920]{1,0:T(8,128)(2,1)S(1)}, u32[]{:S(2)}, u32[]{:S(2)}) collective-permute-start(bf16[48,1920]{1,0:T(8,128)(2,1)S(1)} %get-tuple-element.252.refs_0_), channel_id=1, source_target_pairs={{0,24},{4,28},{8,16},{12,20},{16,8},{20,12},{24,0},{28,4},{1,25},{... | collective-permute-start | bytes 552968 | tf_op jit(solution)/shard_map/ppermute | solution.py:390
  197.1 7.9 %all-to-all-done.5 = bf16[4,192,768]{2,1,0:T(8,128)(2,1)S(1)} async-done(((bf16[4,192,768]{2,1,0:T(8,128)(2,1)}), bf16[4,192,768]{2,1,0:T(8,128)(2,1)S(1)}, u32[]{:S(2)}, u32[]{:S(2)}) %all-to-all-start.5) | async-done | bytes 1179680 | tf_op jit(solution)/shard_map/all_to_all | solution.py:401
  205.0 3.4 %collective-permute-done.39.refs_3_ = bf16[144,768]{1,0:T(8,128)(2,1)} collective-permute-done((bf16[144,768]{1,0:T(8,128)(2,1)S(1)}, bf16[144,768]{1,0:T(8,128)(2,1)}, u32[]{:S(2)}, u32[]{:S(2)}) %collective-permute-start.39) | collective-permute-done | bytes 221216 | tf_op jit(solution)/shard_map/ppermute | solution.py:390
  208.4 3.1 %shard_map.364 = (bf16[144,768]{1,0:T(8,128)(2,1)}, f32[8,128]{1,0:T(8,128)S(1)}) custom-call(s32[3]{0:T(128)S(1)} %pad_add_fusion.where_ref, bf16[144,768]{1,0:T(8,128)(2,1)} %get-tuple-element.253.refs_0_, bf16[144,768]{1,0:T(8,128)(2,1)S(1)} %collective-permute-done.37.refs_1_, bf16[144,768]{1,0:T(8,128)(2,1)S(1)} %collective-permute-done.38.refs_2_, ...), custom_call_target="tpu_custom_call" | custom-call | flops 49999998976 | bytes 50000000 | tf_op jit(solution)/shard_map/pallas_call | solution.py:476
  212.4 3.5 %shard_map.366 = (f32[192,768]{1,0:T(8,128)}, f32[192,768]{1,0:T(8,128)}, f32[192,768]{1,0:T(8,128)}, f32[1,1]{1,0:T(1,128)}, f32[192]{0:T(256)}, /*index=5*/f32...) custom-call(s32[3]{0:T(128)S(1)} %pad_add_fusion.where_ref, ...), custom_call_target="tpu_custom_call" | custom-call | tf_op jit(solution)/shard_map/pallas_call | solution.py:476
  216.0 2.9 %shard_map.367 = (f32[192,3072]{1,0:T(8,128)}, f32[192,768]{1,0:T(8,128)}, f32[8,128]{1,0:T(8,128)}) custom-call(s32[3]{0:T(128)S(1)} %pad_add_fusion.where_ref, bf16[48,1920]{1,0:T(8,128)(2,1)S(1)} %get-tuple-element.252.refs_0_, bf16[48,1920]{1,0:T(8,128)(2,1)S(1)} %collective-permute-done.34.refs_1_, ...), custom_call_target="tpu_custom_call" | custom-call | tf_op jit(solution)/shard_map/pallas_call | solution.py:476
  (190 shorter events, 87.0 us)
Async XLA Ops:
  3.1 25.4 %all-to-all-start = ((bf16[4,48,1920]{2,1,0:T(8,128)(2,1)}), bf16[4,48,1920]{2,1,0:T(8,128)(2,1)S(1)}, u32[]{:S(2)}, u32[]{:S(2)}) async-start(bf16[4,48,1920]{2,1,0:T(8,128)(2,1)} %bitcast.4), calls=%async_computation | async-start | bytes 1474560 | tf_op jit(solution)/shard_map/all_to_all | solution.py:405
  12.5 11.1 %collective-permute-start.1 = (bf16[160,768]{1,0:T(8,128)(2,1)S(1)}, bf16[160,768]{1,0:T(8,128)(2,1)S(1)}, u32[]{:S(2)}, u32[]{:S(2)}) collective-permute-start(bf16[160,768]{1,0:T(8,128)(2,1)S(1)} %get-tuple-element.150.refs_0_), channel_id=1, source_target_pairs={{0,16},{4,20},{8,24},{12,28},{16,0},{20,4},{24,8},{28,12},{1,17},{... | collective-permute-start | bytes 737288 | tf_op jit(solution)/shard_map/ppermute | solution.py:390
  13.1 10.7 %collective-permute-start = (bf16[160,768]{1,0:T(8,128)(2,1)S(1)}, bf16[160,768]{1,0:T(8,128)(2,1)S(1)}, u32[]{:S(2)}, u32[]{:S(2)}) collective-permute-start(bf16[160,768]{1,0:T(8,128)(2,1)S(1)} %get-tuple-element.150.refs_0_), channel_id=1, source_target_pairs={{0,8},{4,12},{8,0},{12,4},{16,24},{20,28},{24,16},{28,20},{1,9},{5... | collective-permute-start | bytes 737288 | tf_op jit(solution)/shard_map/ppermute | solution.py:390
  29.1 14.7 %collective-permute-start.9 = (bf16[144,1920]{1,0:T(8,128)(2,1)S(1)}, bf16[144,1920]{1,0:T(8,128)(2,1)S(1)}, u32[]{:S(2)}, u32[]{:S(2)}) collective-permute-start(bf16[144,1920]{1,0:T(8,128)(2,1)S(1)} %get-tuple-element.163.refs_1_), channel_id=1, source_target_pairs={{0,16},{4,20},{8,24},{12,28},{16,0},{20,4},{24,8},{28,12},{1,17},{... | collective-permute-start | bytes 1658888 | tf_op jit(solution)/shard_map/ppermute | solution.py:390
  30.7 13.2 %collective-permute-start.8 = (bf16[144,1920]{1,0:T(8,128)(2,1)S(1)}, bf16[144,1920]{1,0:T(8,128)(2,1)S(1)}, u32[]{:S(2)}, u32[]{:S(2)}) collective-permute-start(bf16[144,1920]{1,0:T(8,128)(2,1)S(1)} %get-tuple-element.163.refs_1_), channel_id=1, source_target_pairs={{0,8},{4,12},{8,0},{12,4},{16,24},{20,28},{24,16},{28,20},{1,9},{5... | collective-permute-start | bytes 1658888 | tf_op jit(solution)/shard_map/ppermute | solution.py:390
  46.3 21.7 %collective-permute-start.14 = (bf16[96,768]{1,0:T(8,128)(2,1)S(1)}, bf16[96,768]{1,0:T(8,128)(2,1)S(1)}, u32[]{:S(2)}, u32[]{:S(2)}) collective-permute-start(bf16[96,768]{1,0:T(8,128)(2,1)S(1)} %get-tuple-element.170), channel_id=1, source_target_pairs={{0,3},{1,2},{2,1},{3,0},{4,7},{5,6},{6,5},{7,4},{8,11},{9,10},{10,... | collective-permute-start | bytes 442376 | tf_op jit(solution)/shard_map/ppermute | solution.py:395
  48.6 19.5 %collective-permute-start.13 = (bf16[96,768]{1,0:T(8,128)(2,1)S(1)}, bf16[96,768]{1,0:T(8,128)(2,1)S(1)}, u32[]{:S(2)}, u32[]{:S(2)}) collective-permute-start(bf16[96,768]{1,0:T(8,128)(2,1)S(1)} %get-tuple-element.170), channel_id=1, source_target_pairs={{0,2},{1,3},{2,0},{3,1},{4,6},{5,7},{6,4},{7,5},{8,10},{9,11},{10,... | collective-permute-start | bytes 442376 | tf_op jit(solution)/shard_map/ppermute | solution.py:395
  48.6 19.5 %collective-permute-start.12 = (bf16[96,768]{1,0:T(8,128)(2,1)S(1)}, bf16[96,768]{1,0:T(8,128)(2,1)S(1)}, u32[]{:S(2)}, u32[]{:S(2)}) collective-permute-start(bf16[96,768]{1,0:T(8,128)(2,1)S(1)} %get-tuple-element.170), channel_id=1, source_target_pairs={{0,1},{1,0},{2,3},{3,2},{4,5},{5,4},{6,7},{7,6},{8,9},{9,8},{10,11... | collective-permute-start | bytes 442376 | tf_op jit(solution)/shard_map/ppermute | solution.py:395
  50.8 21.2 %collective-permute-start.11 = (bf16[64,1920]{1,0:T(8,128)(2,1)S(1)}, bf16[64,1920]{1,0:T(8,128)(2,1)S(1)}, u32[]{:S(2)}, u32[]{:S(2)}) collective-permute-start(bf16[64,1920]{1,0:T(8,128)(2,1)S(1)} %get-tuple-element.169), channel_id=1, source_target_pairs={{0,16},{4,20},{8,24},{12,28},{16,0},{20,4},{24,8},{28,12},{1,17},{... | collective-permute-start | bytes 737288 | tf_op jit(solution)/shard_map/ppermute | solution.py:390
  51.3 20.7 %collective-permute-start.10 = (bf16[80,1920]{1,0:T(8,128)(2,1)S(1)}, bf16[80,1920]{1,0:T(8,128)(2,1)S(1)}, u32[]{:S(2)}, u32[]{:S(2)}) collective-permute-start(bf16[80,1920]{1,0:T(8,128)(2,1)S(1)} %get-tuple-element.168), channel_id=1, source_target_pairs={{0,8},{4,12},{8,0},{12,4},{16,24},{20,28},{24,16},{28,20},{1,9},{5... | collective-permute-start | bytes 921608 | tf_op jit(solution)/shard_map/ppermute | solution.py:390
  63.7 21.6 %all-to-all-start.1 = ((bf16[4,160,192]{2,1,0:T(8,128)(2,1)}), bf16[4,160,192]{2,1,0:T(8,128)(2,1)}, u32[]{:S(2)}, u32[]{:S(2)}) async-start(bf16[4,160,192]{2,1,0:T(8,128)(2,1)} %bitcast.6), calls=%async_computation.1 | async-start | bytes 655360 | tf_op jit(solution)/shard_map/all_to_all | solution.py:401
  68.6 13.2 %collective-permute-start.17 = (bf16[288,768]{1,0:T(8,128)(2,1)S(1)}, bf16[288,768]{1,0:T(8,128)(2,1)S(1)}, u32[]{:S(2)}, u32[]{:S(2)}) collective-permute-start(bf16[288,768]{1,0:T(8,128)(2,1)S(1)} %get-tuple-element.178.refs_1_), channel_id=1, source_target_pairs={{0,16},{4,20},{8,24},{12,28},{16,0},{20,4},{24,8},{28,12},{1,17},{... | collective-permute-start | bytes 1327112 | tf_op jit(solution)/shard_map/ppermute | solution.py:390
  70.5 11.5 %collective-permute-start.16 = (bf16[288,768]{1,0:T(8,128)(2,1)S(1)}, bf16[288,768]{1,0:T(8,128)(2,1)S(1)}, u32[]{:S(2)}, u32[]{:S(2)}) collective-permute-start(bf16[288,768]{1,0:T(8,128)(2,1)S(1)} %get-tuple-element.178.refs_1_), channel_id=1, source_target_pairs={{0,8},{4,12},{8,0},{12,4},{16,24},{20,28},{24,16},{28,20},{1,9},{5... | collective-permute-start | bytes 1327112 | tf_op jit(solution)/shard_map/ppermute | solution.py:390
  105.7 15.7 %collective-permute-start.20 = (bf16[384,768]{1,0:T(8,128)(2,1)}, bf16[384,768]{1,0:T(8,128)(2,1)}, u32[]{:S(2)}, u32[]{:S(2)}) collective-permute-start(bf16[384,768]{1,0:T(8,128)(2,1)} %get-tuple-element.212), channel_id=1, source_target_pairs={{0,8},{4,12},{8,0},{12,4},{16,24},{20,28},{24,16},{28,20},{1,9},{5... | collective-permute-start | bytes 1769480 | tf_op jit(solution)/shard_map/ppermute | solution.py:390
  107.0 17.4 %collective-permute-start.21 = (bf16[384,768]{1,0:T(8,128)(2,1)}, bf16[384,768]{1,0:T(8,128)(2,1)}, u32[]{:S(2)}, u32[]{:S(2)}) collective-permute-start(bf16[384,768]{1,0:T(8,128)(2,1)} %get-tuple-element.213), channel_id=1, source_target_pairs={{0,16},{4,20},{8,24},{12,28},{16,0},{20,4},{24,8},{28,12},{1,17},{... | collective-permute-start | bytes 1769480 | tf_op jit(solution)/shard_map/ppermute | solution.py:390
  115.2 22.4 %all-to-all-start.2 = ((bf16[4,144,192]{2,1,0:T(8,128)(2,1)}), bf16[4,144,192]{2,1,0:T(8,128)(2,1)S(1)}, u32[]{:S(2)}, u32[]{:S(2)}) async-start(bf16[4,144,192]{2,1,0:T(8,128)(2,1)} %bitcast.11), calls=%async_computation.2 | async-start | bytes 589824 | tf_op jit(solution)/shard_map/all_to_all | solution.py:401
  131.7 33.5 %collective-permute-start.27 = (bf16[192,1920]{1,0:T(8,128)(2,1)}, bf16[192,1920]{1,0:T(8,128)(2,1)S(1)}, u32[]{:S(2)}, u32[]{:S(2)}) collective-permute-start(bf16[192,1920]{1,0:T(8,128)(2,1)} %get-tuple-element.240), channel_id=1, source_target_pairs={{0,8},{4,12},{8,0},{12,4},{16,24},{20,28},{24,16},{28,20},{1,9},{5... | collective-permute-start | bytes 2211848 | tf_op jit(solution)/shard_map/ppermute | solution.py:390
  133.7 31.4 %collective-permute-start.28 = (bf16[192,1920]{1,0:T(8,128)(2,1)}, bf16[192,1920]{1,0:T(8,128)(2,1)}, u32[]{:S(2)}, u32[]{:S(2)}) collective-permute-start(bf16[192,1920]{1,0:T(8,128)(2,1)} %get-tuple-element.241), channel_id=1, source_target_pairs={{0,16},{4,20},{8,24},{12,28},{16,0},{20,4},{24,8},{28,12},{1,17},{... | collective-permute-start | bytes 2211848 | tf_op jit(solution)/shard_map/ppermute | solution.py:390
  134.6 30.5 %collective-permute-start.29 = (bf16[192,1920]{1,0:T(8,128)(2,1)}, bf16[192,1920]{1,0:T(8,128)(2,1)}, u32[]{:S(2)}, u32[]{:S(2)}) collective-permute-start(bf16[192,1920]{1,0:T(8,128)(2,1)} %get-tuple-element.242), channel_id=1, source_target_pairs={{0,24},{4,28},{8,16},{12,20},{16,8},{20,12},{24,0},{28,4},{1,25},{... | collective-permute-start | bytes 2211848 | tf_op jit(solution)/shard_map/ppermute | solution.py:390
  137.5 19.9 %all-to-all-start.3 = ((bf16[4,96,768]{2,1,0:T(8,128)(2,1)}), bf16[4,96,768]{2,1,0:T(8,128)(2,1)S(1)}, u32[]{:S(2)}, u32[]{:S(2)}) async-start(bf16[4,96,768]{2,1,0:T(8,128)(2,1)} %bitcast.13), calls=%async_computation.3 | async-start | bytes 1179648 | tf_op jit(solution)/shard_map/all_to_all | solution.py:405
  154.5 19.1 %collective-permute-start.26 = (bf16[576,768]{1,0:T(8,128)(2,1)S(1)}, bf16[576,768]{1,0:T(8,128)(2,1)S(1)}, u32[]{:S(2)}, u32[]{:S(2)}) collective-permute-start(bf16[576,768]{1,0:T(8,128)(2,1)S(1)} %get-tuple-element.238), channel_id=1, source_target_pairs={{0,4},{4,0},{8,12},{12,8},{16,20},{20,16},{24,28},{28,24},{1,5},{5... | collective-permute-start | bytes 2654216 | tf_op jit(solution)/shard_map/ppermute | solution.py:380
  160.3 20.0 %all-to-all-start.4 = ((bf16[4,96,640]{2,1,0:T(8,128)(2,1)}), bf16[4,96,640]{2,1,0:T(8,128)(2,1)S(1)}, u32[]{:S(2)}, u32[]{:S(2)}) async-start(bf16[4,96,640]{2,1,0:T(8,128)(2,1)} %bitcast.15), calls=%async_computation.4 | async-start | bytes 983040 | tf_op jit(solution)/shard_map/all_to_all | solution.py:405
  169.2 17.0 %collective-permute-start.31 = (bf16[48,1920]{1,0:T(8,128)(2,1)}, bf16[48,1920]{1,0:T(8,128)(2,1)}, u32[]{:S(2)}, u32[]{:S(2)}) collective-permute-start(bf16[48,1920]{1,0:T(8,128)(2,1)} %get-tuple-element.248), channel_id=1, source_target_pairs={{0,1},{1,0},{2,3},{3,2},{4,5},{5,4},{6,7},{7,6},{8,9},{9,8},{10,11... | collective-permute-start | bytes 552968 | tf_op jit(solution)/shard_map/ppermute | solution.py:395
  171.2 21.0 %collective-permute-start.32 = (bf16[48,1920]{1,0:T(8,128)(2,1)}, bf16[48,1920]{1,0:T(8,128)(2,1)}, u32[]{:S(2)}, u32[]{:S(2)}) collective-permute-start(bf16[48,1920]{1,0:T(8,128)(2,1)} %get-tuple-element.249), channel_id=1, source_target_pairs={{0,2},{1,3},{2,0},{3,1},{4,6},{5,7},{6,4},{7,5},{8,10},{9,11},{10,... | collective-permute-start | bytes 552968 | tf_op jit(solution)/shard_map/ppermute | solution.py:395
  173.6 18.6 %collective-permute-start.33 = (bf16[48,1920]{1,0:T(8,128)(2,1)}, bf16[48,1920]{1,0:T(8,128)(2,1)}, u32[]{:S(2)}, u32[]{:S(2)}) collective-permute-start(bf16[48,1920]{1,0:T(8,128)(2,1)} %get-tuple-element.250), channel_id=1, source_target_pairs={{0,3},{1,2},{2,1},{3,0},{4,7},{5,6},{6,5},{7,4},{8,11},{9,10},{10,... | collective-permute-start | bytes 552968 | tf_op jit(solution)/shard_map/ppermute | solution.py:395
  175.0 22.0 %collective-permute-start.37 = (bf16[144,768]{1,0:T(8,128)(2,1)S(1)}, bf16[144,768]{1,0:T(8,128)(2,1)S(1)}, u32[]{:S(2)}, u32[]{:S(2)}) collective-permute-start(bf16[144,768]{1,0:T(8,128)(2,1)S(1)} %get-tuple-element.254), channel_id=1, source_target_pairs={{0,8},{4,12},{8,0},{12,4},{16,24},{20,28},{24,16},{28,20},{1,9},{5... | collective-permute-start | bytes 663560 | tf_op jit(solution)/shard_map/ppermute | solution.py:390
  177.0 20.1 %collective-permute-start.38 = (bf16[144,768]{1,0:T(8,128)(2,1)S(1)}, bf16[144,768]{1,0:T(8,128)(2,1)S(1)}, u32[]{:S(2)}, u32[]{:S(2)}) collective-permute-start(bf16[144,768]{1,0:T(8,128)(2,1)S(1)} %get-tuple-element.255), channel_id=1, source_target_pairs={{0,16},{4,20},{8,24},{12,28},{16,0},{20,4},{24,8},{28,12},{1,17},{... | collective-permute-start | bytes 663560 | tf_op jit(solution)/shard_map/ppermute | solution.py:390
  182.2 22.8 %all-to-all-start.5 = ((bf16[4,192,768]{2,1,0:T(8,128)(2,1)}), bf16[4,192,768]{2,1,0:T(8,128)(2,1)S(1)}, u32[]{:S(2)}, u32[]{:S(2)}) async-start(bf16[4,192,768]{2,1,0:T(8,128)(2,1)} %bitcast.17), calls=%async_computation.5 | async-start | bytes 2359296 | tf_op jit(solution)/shard_map/all_to_all | solution.py:401
  186.1 22.3 %collective-permute-start.39 = (bf16[144,768]{1,0:T(8,128)(2,1)S(1)}, bf16[144,768]{1,0:T(8,128)(2,1)}, u32[]{:S(2)}, u32[]{:S(2)}) collective-permute-start(bf16[144,768]{1,0:T(8,128)(2,1)S(1)} %get-tuple-element.256), channel_id=1, source_target_pairs={{0,24},{4,28},{8,16},{12,20},{16,8},{20,12},{24,0},{28,4},{1,25},{... | collective-permute-start | bytes 663560 | tf_op jit(solution)/shard_map/ppermute | solution.py:390
  193.5 18.0 %collective-permute-start.36 = (bf16[48,1920]{1,0:T(8,128)(2,1)S(1)}, bf16[48,1920]{1,0:T(8,128)(2,1)S(1)}, u32[]{:S(2)}, u32[]{:S(2)}) collective-permute-start(bf16[48,1920]{1,0:T(8,128)(2,1)S(1)} %get-tuple-element.252.refs_0_), channel_id=1, source_target_pairs={{0,24},{4,28},{8,16},{12,20},{16,8},{20,12},{24,0},{28,4},{1,25},{... | collective-permute-start | bytes 552968 | tf_op jit(solution)/shard_map/ppermute | solution.py:390
  196.1 15.4 %collective-permute-start.35 = (bf16[48,1920]{1,0:T(8,128)(2,1)S(1)}, bf16[48,1920]{1,0:T(8,128)(2,1)S(1)}, u32[]{:S(2)}, u32[]{:S(2)}) collective-permute-start(bf16[48,1920]{1,0:T(8,128)(2,1)S(1)} %get-tuple-element.252.refs_0_), channel_id=1, source_target_pairs={{0,16},{4,20},{8,24},{12,28},{16,0},{20,4},{24,8},{28,12},{1,17},{... | collective-permute-start | bytes 552968 | tf_op jit(solution)/shard_map/ppermute | solution.py:390
  197.0 14.8 %collective-permute-start.34 = (bf16[48,1920]{1,0:T(8,128)(2,1)S(1)}, bf16[48,1920]{1,0:T(8,128)(2,1)S(1)}, u32[]{:S(2)}, u32[]{:S(2)}) collective-permute-start(bf16[48,1920]{1,0:T(8,128)(2,1)S(1)} %get-tuple-element.252.refs_0_), channel_id=1, source_target_pairs={{0,8},{4,12},{8,0},{12,4},{16,24},{20,28},{24,16},{28,20},{1,9},{5... | collective-permute-start | bytes 552968 | tf_op jit(solution)/shard_map/ppermute | solution.py:390
  (58 other events, 336.1 us)

commit v6 on v4

--- a/solution.py
+++ b/solution.py
@@ -1470,7 +1470,7 @@
     )
     up_planes = [up_planes[0]] + [swap_planes(up_planes[s], s) for s in steps]
     shares = step(share_inputs, (shaped(rows, width),) * 4, (d_near, d_far), store=(0,), cost=50)
-    shares = [shares[0]] + [swap_chips(shares[k], k) for k in steps]
+    shares = [shares[0]] + [swap_chips(shares[k], k) for k in steps[::-1]]
     both = trade_chips(step(sum_planes, shaped(8 * half, width), (arrived, down_planes), cost=50))
     up_near = spread(step(sum_pieces, shaped(quarter, 5 * core_units), up_planes, cost=50))
     grad_tokens = step(

time: 220 us -> 220 us (level)
    all_to_all x3, waiting for transfers between devices: 8.25 us -> 5.22 us  [trade_chips(): lax.all_to_all(value, 'ctx', 0, 0, axis_index_groups=groups, tiled=True)]
    ppermute x24, waiting for transfers between devices: 17.4 us -> 20.4 us  [swap_chips(): return lax.ppermute(value, 'ctx', [(i, i ^ 2 * step) for i in range(size)])]
  transfers between devices with their start and end apart: 47 -> 47, of which waited for: 17 -> 18; matrix products, arithmetic and copies ran while one was open for 0% -> 0% of each run, Pallas kernels for 35% -> 35%
where the time goes in v6:
time: 220 us; the launch traced here: 219 us
  Pallas kernels  90.2 us (41%)
  starting transfers between devices  71.5 us (32%)
  waiting for transfers between devices  41.7 us (19%)
  blocking collectives  8.61 us (4%)
  local copies, waits for them, and re-layouts  5.27 us (2%)
    pallas_call x38, Pallas kernels, local_call(): pl.pallas_call(kernel, out_shape=(*(pltpu.HBM(o.shape, o.dtype) if i in f...  90.2 us
    ppermute x24, starting transfers between devices, swap_chips(): return lax.ppermute(value, 'ctx', [(i, i ^ 2 * step) for i in range(size)])  31 us
    ppermute x24, waiting for transfers between devices, swap_chips(): return lax.ppermute(value, 'ctx', [(i, i ^ 2 * step) for i in range(size)])  20.4 us
    all_to_all x3, starting transfers between devices, trade_planes(): return lax.all_to_all(value, 'fsdp', 0, 0, tiled=True)  14.9 us
    ppermute x9, starting transfers between devices, swap_planes(): return lax.ppermute(value, 'fsdp', [(i, i ^ step) for i in range(size)])  13.3 us
    all_to_all x3, starting transfers between devices, trade_chips(): lax.all_to_all(value, 'ctx', 0, 0, axis_index_groups=groups, tiled=True)  11.4 us
    all_gather x4, blocking collectives, both_cores(): lax.all_gather(value, 'ctx', axis=0, tiled=True, axis_index_groups=pairs)  8.61 us
    ppermute x9, waiting for transfers between devices, swap_planes(): return lax.ppermute(value, 'fsdp', [(i, i ^ step) for i in range(size)])  8.51 us
  transfers between devices with their start and end apart: 47, of which 18 were waited for; matrix products, arithmetic and copies ran while one was open for 0% of the time, Pallas kernels for 35%

profile of v6, /device:TPU:0, one launch (start us, length us, event | category | flops | bytes accessed | tf_op | source)
XLA Modules:
  0.0 219.0 jit_solution(1173500900872681993)
XLA Ops:
  0.8 2.3 %shard_map.331 = (bf16[192,1920]{1,0:T(8,128)(2,1)}, f32[8,128]{1,0:T(8,128)S(1)}) custom-call(s32[3]{0:T(128)S(1)} %pad_add_fusion.where_ref, bf16[192,3072]{1,0:T(8,128)(2,1)} %refs_0_.10, bf16[192,768]{1,0:T(8,128)(2,1)} %refs_0_.9), custom_call_target="tpu_custom_call" | custom-call | tf_op jit(solution)/shard_map/pallas_call | solution.py:476
  3.1 6.3 %all-to-all-start = ((bf16[4,48,1920]{2,1,0:T(8,128)(2,1)}), bf16[4,48,1920]{2,1,0:T(8,128)(2,1)S(1)}, u32[]{:S(2)}, u32[]{:S(2)}) async-start(bf16[4,48,1920]{2,1,0:T(8,128)(2,1)} %bitcast.4), calls=%async_computation | async-start | bytes 1474560 | tf_op jit(solution)/shard_map/all_to_all | solution.py:405
  10.0 2.5 %collective-permute-start.2 = (bf16[160,768]{1,0:T(8,128)(2,1)S(1)}, bf16[160,768]{1,0:T(8,128)(2,1)S(1)}, u32[]{:S(2)}, u32[]{:S(2)}) collective-permute-start(bf16[160,768]{1,0:T(8,128)(2,1)S(1)} %get-tuple-element.151.refs_0_), channel_id=1, source_target_pairs={{0,24},{4,28},{8,16},{12,20},{16,8},{20,12},{24,0},{28,4},{1,25},{... | collective-permute-start | bytes 737288 | tf_op jit(solution)/shard_map/ppermute | solution.py:390
  15.6 4.4 %collective-permute-done.2.refs_3_ = bf16[160,768]{1,0:T(8,128)(2,1)S(1)} collective-permute-done((bf16[160,768]{1,0:T(8,128)(2,1)S(1)}, bf16[160,768]{1,0:T(8,128)(2,1)S(1)}, u32[]{:S(2)}, u32[]{:S(2)}) %collective-permute-start.2) | collective-permute-done | bytes 245792 | tf_op jit(solution)/shard_map/ppermute | solution.py:390
  19.9 3.8 %collective-permute-done.1.refs_2_ = bf16[160,768]{1,0:T(8,128)(2,1)S(1)} collective-permute-done((bf16[160,768]{1,0:T(8,128)(2,1)S(1)}, bf16[160,768]{1,0:T(8,128)(2,1)S(1)}, u32[]{:S(2)}, u32[]{:S(2)}) %collective-permute-start.1) | collective-permute-done | bytes 245792 | tf_op jit(solution)/shard_map/ppermute | solution.py:390
  24.5 4.0 %all-to-all-done = bf16[4,48,1920]{2,1,0:T(8,128)(2,1)S(1)} async-done(((bf16[4,48,1920]{2,1,0:T(8,128)(2,1)}), bf16[4,48,1920]{2,1,0:T(8,128)(2,1)S(1)}, u32[]{:S(2)}, u32[]{:S(2)}) %all-to-all-start) | async-done | bytes 737312 | tf_op jit(solution)/shard_map/all_to_all | solution.py:405
  33.7 2.9 %collective-permute-start.4 = (bf16[96,640]{1,0:T(8,128)(2,1)S(1)}, bf16[96,640]{1,0:T(8,128)(2,1)S(1)}, u32[]{:S(2)}, u32[]{:S(2)}) collective-permute-start(bf16[96,640]{1,0:T(8,128)(2,1)S(1)} %get-tuple-element.161.refs_0_.refs_3_), channel_id=1, source_target_pairs={{0,1},{1,0},{2,3},{3,2},{4,5},{5,4},{6,7},{7,6},{8,9},{9,8},{10,11... | collective-permute-start | bytes 368648 | tf_op jit(solution)/shard_map/ppermute | solution.py:395
  36.6 2.4 %shard_map.336 = (f32[1152,768]{1,0:T(8,128)S(1)}, f32[8,1152]{1,0:T(8,128)S(1)}, f32[576,128]{1,0:T(8,128)S(1)}, f32[8,128]{1,0:T(8,128)S(1)}) custom-call(s32[3]{0:T(128)S(1)} %pad_add_fusion.where_ref, bf16[640,768]{1,0:T(8,128)(2,1)S(1)} %get-tuple-element.154.refs_0_, bf16[640,768]{1,0:T(8,128)(2,1)} %collective-permute-done.3.refs_1_, ...), custom_call_target="tpu_custom_call" | custom-call | flops 1000000000 | bytes 1000000 | tf_op jit(solution)/shard_map/pallas_call | solution.py:476
  40.3 2.9 %collective-permute-done.5.refs_2_.refs_5_ = bf16[96,640]{1,0:T(8,128)(2,1)S(1)} collective-permute-done((bf16[96,640]{1,0:T(8,128)(2,1)S(1)}, bf16[96,640]{1,0:T(8,128)(2,1)S(1)}, u32[]{:S(2)}, u32[]{:S(2)}) %collective-permute-start.5) | collective-permute-done | bytes 122912 | tf_op jit(solution)/shard_map/ppermute | solution.py:395
  52.7 10.5 %shard_map.340 = (bf16[1152,768]{1,0:T(8,128)(2,1)}, bf16[768,576]{1,0:T(8,128)(2,1)}, bf16[1152,576]{1,0:T(8,128)(2,1)}, bf16[3,576,1152]{2,1,0:T(8,128)(2,1)},...) custom-call(s32[3]{0:T(128)S(1)} %pad_add_fusion.where_ref, ...), custom_call_target="tpu_custom_call" | custom-call | flops 49999998976 | bytes 50000000 | tf_op jit(solution)/shard_map/pallas_call | solution.py:476
  63.7 4.3 %all-to-all-start.1 = ((bf16[4,160,192]{2,1,0:T(8,128)(2,1)}), bf16[4,160,192]{2,1,0:T(8,128)(2,1)}, u32[]{:S(2)}, u32[]{:S(2)}) async-start(bf16[4,160,192]{2,1,0:T(8,128)(2,1)} %bitcast.6), calls=%async_computation.1 | async-start | bytes 655360 | tf_op jit(solution)/shard_map/all_to_all | solution.py:401
  74.6 2.4 %shard_map.343 = (bf16[768,1536]{1,0:T(8,128)(2,1)S(1)}, f32[8,128]{1,0:T(8,128)S(1)}) custom-call(s32[3]{0:T(128)S(1)} %pad_add_fusion.where_ref, bf16[192,3072]{1,0:T(8,128)(2,1)} %refs_0_.10, bf16[144,1920]{1,0:T(8,128)(2,1)} %copy-done.4, bf16[144,1920]{1,0:T(8,128)(2,1)} %copy-done.6, bf16[144,1920]{1,0:T(8,128)(2,1)} %copy-done.5, ...), custom_call_target="tpu_custom_call" | custom-call | flops 49999998976 | bytes 50000000 | tf_op jit(solution)/shard_map/pallas_call | solution.py:476
  77.8 4.1 %collective-permute-done.17.refs_1_.refs_3_ = bf16[288,768]{1,0:T(8,128)(2,1)S(1)} collective-permute-done((bf16[288,768]{1,0:T(8,128)(2,1)S(1)}, bf16[288,768]{1,0:T(8,128)(2,1)S(1)}, u32[]{:S(2)}, u32[]{:S(2)}) %collective-permute-start.17) | collective-permute-done | bytes 442400 | tf_op jit(solution)/shard_map/ppermute | solution.py:390
  102.4 3.1 %shard_map.351 = (bf16[384,768]{1,0:T(8,128)(2,1)S(1)}, bf16[384,768]{1,0:T(8,128)(2,1)}, bf16[384,768]{1,0:T(8,128)(2,1)}, bf16[192,768]{1,0:T(8,128)(2,1)S(1)}...) custom-call(s32[3]{0:T(128)S(1)} %pad_add_fusion.where_ref, bf16[288,1536]{1,0:T(8,128)(2,1)S(1)} %get-tuple-element.187.refs_0_, ...), custom_call_target="tpu_custom_call" | custom-call | tf_op jit(solution)/shard_map/pallas_call | solution.py:476
  107.5 3.9 %shard_map.352 = (bf16[288,1536]{1,0:T(8,128)(2,1)S(1)}, f32[144,768]{1,0:T(8,128)S(1)}, bf16[144,768]{1,0:T(8,128)(2,1)S(1)}, f32[1,1536]{1,0:T(1,128)S(1)}, f32[8,128]{1,0:T(8,128)S(1)}) custom-call(s32[3]{0:T(128)S(1)} %pad_add_fusion.where_ref, bf16[288,768]{1,0:T(8,128)(2,1)S(1)} %all_gather.14.refs_1_.refs_0_, ...), custom_call_target="tpu_custom_call" | custom-call | flops 49999998976 | bytes 50000000 | tf_op jit(solution)/shard_map/pallas_call | solution.py:476
  116.5 3.5 %all-to-all-start.2 = ((bf16[4,144,192]{2,1,0:T(8,128)(2,1)}), bf16[4,144,192]{2,1,0:T(8,128)(2,1)S(1)}, u32[]{:S(2)}, u32[]{:S(2)}) async-start(bf16[4,144,192]{2,1,0:T(8,128)(2,1)} %bitcast.11), calls=%async_computation.2 | async-start | bytes 589824 | tf_op jit(solution)/shard_map/all_to_all | solution.py:401
  126.8 4.5 %shard_map.356 = (bf16[192,1920]{1,0:T(8,128)(2,1)}, bf16[192,1920]{1,0:T(8,128)(2,1)}, bf16[192,1920]{1,0:T(8,128)(2,1)}, bf16[192,1920]{1,0:T(8,128)(2,1)}, f32[8,128]{1,0:T(8,128)S(1)}) custom-call(s32[3]{0:T(128)S(1)} %pad_add_fusion.where_ref, bf16[288,768]{1,0:T(8,128)(2,1)S(1)} %copy-done.1, bf16[288,1536]{1,0:T(8,128)(2,1)S(1)} %copy-done.36, ...), custom_call_target="tpu_custom_call" | custom-call | flops 5000000000 | bytes 5000000 | tf_op jit(solution)/shard_map/pallas_call | solution.py:476
  132.4 2.4 %collective-permute-start.29 = (bf16[192,1920]{1,0:T(8,128)(2,1)}, bf16[192,1920]{1,0:T(8,128)(2,1)}, u32[]{:S(2)}, u32[]{:S(2)}) collective-permute-start(bf16[192,1920]{1,0:T(8,128)(2,1)} %get-tuple-element.243), channel_id=1, source_target_pairs={{0,24},{4,28},{8,16},{12,20},{16,8},{20,12},{24,0},{28,4},{1,25},{... | collective-permute-start | bytes 2211848 | tf_op jit(solution)/shard_map/ppermute | solution.py:390
  134.8 2.3 %shard_map.357 = (bf16[384,768]{1,0:T(8,128)(2,1)}, f32[8,128]{1,0:T(8,128)S(1)}) custom-call(s32[3]{0:T(128)S(1)} %pad_add_fusion.where_ref, bf16[384,768]{1,0:T(8,128)(2,1)S(1)} %copy-done.3, bf16[384,768]{1,0:T(8,128)(2,1)} %collective-permute-done.20.refs_0_.refs_1_, bf16[384,768]{1,0:T(8,128)(2,1)} %collective-permute-done.21.refs_1_.refs_2_, ...), custom_call_target="tpu_custom_call" | custom-call | tf_op jit(solution)/shard_map/pallas_call | solution.py:476
  137.1 3.7 %all-to-all-start.3 = ((bf16[4,96,768]{2,1,0:T(8,128)(2,1)}), bf16[4,96,768]{2,1,0:T(8,128)(2,1)S(1)}, u32[]{:S(2)}, u32[]{:S(2)}) async-start(bf16[4,96,768]{2,1,0:T(8,128)(2,1)} %bitcast.13), calls=%async_computation.3 | async-start | bytes 1179648 | tf_op jit(solution)/shard_map/all_to_all | solution.py:405
  140.8 12.4 %shard_map.358 = (bf16[576,768]{1,0:T(8,128)(2,1)S(1)}, bf16[576,768]{1,0:T(8,128)(2,1)S(1)}, bf16[384,576]{1,0:T(8,128)(2,1)}, bf16[384,576]{1,0:T(8,128)(2,1)}...) custom-call(s32[3]{0:T(128)S(1)} %pad_add_fusion.where_ref, bf16[576,192]{1,0:T(8,128)(2,1)S(1)} %bitcast.27, ...), custom_call_target="tpu_custom_call" | custom-call | flops 49999998976 | bytes 50000000 | tf_op jit(solution)/shard_map/pallas_call | solution.py:476
  154.6 2.4 %collective-permute-done.25.refs_1_ = bf16[384,576]{1,0:T(8,128)(2,1)} collective-permute-done((bf16[384,576]{1,0:T(8,128)(2,1)}, bf16[384,576]{1,0:T(8,128)(2,1)}, u32[]{:S(2)}, u32[]{:S(2)}) %collective-permute-start.25) | collective-permute-done | bytes 442400 | tf_op jit(solution)/shard_map/ppermute | solution.py:380
  157.0 2.9 %shard_map.359 = (bf16[384,640]{1,0:T(8,128)(2,1)}, bf16[96,768]{1,0:T(8,128)(2,1)S(1)}, f32[8,128]{1,0:T(8,128)S(1)}) custom-call(s32[3]{0:T(128)S(1)} %pad_add_fusion.where_ref, bf16[384,576]{1,0:T(8,128)(2,1)} %get-tuple-element.228.refs_0_, bf16[384,576]{1,0:T(8,128)(2,1)} %collective-permute-done.25.refs_1_, f32[8,768]{1,0:T(8,128)S(1)} %get-tuple-element.230.refs_2_, ...), custom_call_target="tpu_custom_call" | custom-call | flops 1000000000 | bytes 1000000 | tf_op jit(solution)/shard_map/pallas_call | solution.py:476
  159.9 4.8 %all-to-all-start.4 = ((bf16[4,96,640]{2,1,0:T(8,128)(2,1)}), bf16[4,96,640]{2,1,0:T(8,128)(2,1)S(1)}, u32[]{:S(2)}, u32[]{:S(2)}) async-start(bf16[4,96,640]{2,1,0:T(8,128)(2,1)} %bitcast.15), calls=%async_computation.4 | async-start | bytes 983040 | tf_op jit(solution)/shard_map/all_to_all | solution.py:405
  166.1 4.0 %shard_map.360 = (bf16[48,1920]{1,0:T(8,128)(2,1)S(1)}, bf16[48,1920]{1,0:T(8,128)(2,1)}, bf16[48,1920]{1,0:T(8,128)(2,1)}, bf16[48,1920]{1,0:T(8,128)(2,1)}, f32[8,128]{1,0:T(8,128)S(1)}) custom-call(s32[3]{0:T(128)S(1)} %pad_add_fusion.where_ref, bf16[192,1920]{1,0:T(8,128)(2,1)} %get-tuple-element.240.refs_0_, ...), custom_call_target="tpu_custom_call" | custom-call | flops 49999998976 | bytes 50000000 | tf_op jit(solution)/shard_map/pallas_call | solution.py:476
  170.8 2.4 %collective-permute-start.32 = (bf16[48,1920]{1,0:T(8,128)(2,1)}, bf16[48,1920]{1,0:T(8,128)(2,1)}, u32[]{:S(2)}, u32[]{:S(2)}) collective-permute-start(bf16[48,1920]{1,0:T(8,128)(2,1)} %get-tuple-element.250), channel_id=1, source_target_pairs={{0,2},{1,3},{2,0},{3,1},{4,6},{5,7},{6,4},{7,5},{8,10},{9,11},{10,... | collective-permute-start | bytes 552968 | tf_op jit(solution)/shard_map/ppermute | solution.py:395
  181.7 3.7 %all-to-all-start.5 = ((bf16[4,192,768]{2,1,0:T(8,128)(2,1)}), bf16[4,192,768]{2,1,0:T(8,128)(2,1)S(1)}, u32[]{:S(2)}, u32[]{:S(2)}) async-start(bf16[4,192,768]{2,1,0:T(8,128)(2,1)} %bitcast.17), calls=%async_computation.5 | async-start | bytes 2359296 | tf_op jit(solution)/shard_map/all_to_all | solution.py:401
  187.4 4.4 %collective-permute-done.32.refs_2_ = bf16[48,1920]{1,0:T(8,128)(2,1)} collective-permute-done((bf16[48,1920]{1,0:T(8,128)(2,1)}, bf16[48,1920]{1,0:T(8,128)(2,1)}, u32[]{:S(2)}, u32[]{:S(2)}) %collective-permute-start.32) | collective-permute-done | bytes 184352 | tf_op jit(solution)/shard_map/ppermute | solution.py:395
  196.6 5.2 %all-to-all-done.5 = bf16[4,192,768]{2,1,0:T(8,128)(2,1)S(1)} async-done(((bf16[4,192,768]{2,1,0:T(8,128)(2,1)}), bf16[4,192,768]{2,1,0:T(8,128)(2,1)S(1)}, u32[]{:S(2)}, u32[]{:S(2)}) %all-to-all-start.5) | async-done | bytes 1179680 | tf_op jit(solution)/shard_map/all_to_all | solution.py:401
  201.8 4.8 %collective-permute-done.39.refs_3_ = bf16[144,768]{1,0:T(8,128)(2,1)} collective-permute-done((bf16[144,768]{1,0:T(8,128)(2,1)S(1)}, bf16[144,768]{1,0:T(8,128)(2,1)}, u32[]{:S(2)}, u32[]{:S(2)}) %collective-permute-start.39) | collective-permute-done | bytes 221216 | tf_op jit(solution)/shard_map/ppermute | solution.py:390
  206.7 3.1 %shard_map.364 = (bf16[144,768]{1,0:T(8,128)(2,1)}, f32[8,128]{1,0:T(8,128)S(1)}) custom-call(s32[3]{0:T(128)S(1)} %pad_add_fusion.where_ref, bf16[144,768]{1,0:T(8,128)(2,1)} %get-tuple-element.254.refs_0_, bf16[144,768]{1,0:T(8,128)(2,1)S(1)} %collective-permute-done.37.refs_1_, bf16[144,768]{1,0:T(8,128)(2,1)S(1)} %collective-permute-done.38.refs_2_, ...), custom_call_target="tpu_custom_call" | custom-call | flops 49999998976 | bytes 50000000 | tf_op jit(solution)/shard_map/pallas_call | solution.py:476
  215.9 2.9 %shard_map.368 = (f32[192,3072]{1,0:T(8,128)}, f32[192,768]{1,0:T(8,128)}, f32[8,128]{1,0:T(8,128)}) custom-call(s32[3]{0:T(128)S(1)} %pad_add_fusion.where_ref, bf16[48,1920]{1,0:T(8,128)(2,1)S(1)} %get-tuple-element.253.refs_0_, bf16[48,1920]{1,0:T(8,128)(2,1)S(1)} %collective-permute-done.34.refs_1_, ...), custom_call_target="tpu_custom_call" | custom-call | tf_op jit(solution)/shard_map/pallas_call | solution.py:476
  (191 shorter events, 88.4 us)
Async XLA Ops:
  3.1 25.4 %all-to-all-start = ((bf16[4,48,1920]{2,1,0:T(8,128)(2,1)}), bf16[4,48,1920]{2,1,0:T(8,128)(2,1)S(1)}, u32[]{:S(2)}, u32[]{:S(2)}) async-start(bf16[4,48,1920]{2,1,0:T(8,128)(2,1)} %bitcast.4), calls=%async_computation | async-start | bytes 1474560 | tf_op jit(solution)/shard_map/all_to_all | solution.py:405
  12.5 11.1 %collective-permute-start.1 = (bf16[160,768]{1,0:T(8,128)(2,1)S(1)}, bf16[160,768]{1,0:T(8,128)(2,1)S(1)}, u32[]{:S(2)}, u32[]{:S(2)}) collective-permute-start(bf16[160,768]{1,0:T(8,128)(2,1)S(1)} %get-tuple-element.151.refs_0_), channel_id=1, source_target_pairs={{0,16},{4,20},{8,24},{12,28},{16,0},{20,4},{24,8},{28,12},{1,17},{... | collective-permute-start | bytes 737288 | tf_op jit(solution)/shard_map/ppermute | solution.py:390
  29.1 14.7 %collective-permute-start.9 = (bf16[144,1920]{1,0:T(8,128)(2,1)S(1)}, bf16[144,1920]{1,0:T(8,128)(2,1)S(1)}, u32[]{:S(2)}, u32[]{:S(2)}) collective-permute-start(bf16[144,1920]{1,0:T(8,128)(2,1)S(1)} %get-tuple-element.164.refs_1_), channel_id=1, source_target_pairs={{0,16},{4,20},{8,24},{12,28},{16,0},{20,4},{24,8},{28,12},{1,17},{... | collective-permute-start | bytes 1658888 | tf_op jit(solution)/shard_map/ppermute | solution.py:390
  30.7 13.2 %collective-permute-start.8 = (bf16[144,1920]{1,0:T(8,128)(2,1)S(1)}, bf16[144,1920]{1,0:T(8,128)(2,1)S(1)}, u32[]{:S(2)}, u32[]{:S(2)}) collective-permute-start(bf16[144,1920]{1,0:T(8,128)(2,1)S(1)} %get-tuple-element.164.refs_1_), channel_id=1, source_target_pairs={{0,8},{4,12},{8,0},{12,4},{16,24},{20,28},{24,16},{28,20},{1,9},{5... | collective-permute-start | bytes 1658888 | tf_op jit(solution)/shard_map/ppermute | solution.py:390
  46.3 21.7 %collective-permute-start.14 = (bf16[96,768]{1,0:T(8,128)(2,1)S(1)}, bf16[96,768]{1,0:T(8,128)(2,1)S(1)}, u32[]{:S(2)}, u32[]{:S(2)}) collective-permute-start(bf16[96,768]{1,0:T(8,128)(2,1)S(1)} %get-tuple-element.171), channel_id=1, source_target_pairs={{0,3},{1,2},{2,1},{3,0},{4,7},{5,6},{6,5},{7,4},{8,11},{9,10},{10,... | collective-permute-start | bytes 442376 | tf_op jit(solution)/shard_map/ppermute | solution.py:395
  48.6 19.5 %collective-permute-start.13 = (bf16[96,768]{1,0:T(8,128)(2,1)S(1)}, bf16[96,768]{1,0:T(8,128)(2,1)S(1)}, u32[]{:S(2)}, u32[]{:S(2)}) collective-permute-start(bf16[96,768]{1,0:T(8,128)(2,1)S(1)} %get-tuple-element.171), channel_id=1, source_target_pairs={{0,2},{1,3},{2,0},{3,1},{4,6},{5,7},{6,4},{7,5},{8,10},{9,11},{10,... | collective-permute-start | bytes 442376 | tf_op jit(solution)/shard_map/ppermute | solution.py:395
  48.6 19.5 %collective-permute-start.12 = (bf16[96,768]{1,0:T(8,128)(2,1)S(1)}, bf16[96,768]{1,0:T(8,128)(2,1)S(1)}, u32[]{:S(2)}, u32[]{:S(2)}) collective-permute-start(bf16[96,768]{1,0:T(8,128)(2,1)S(1)} %get-tuple-element.171), channel_id=1, source_target_pairs={{0,1},{1,0},{2,3},{3,2},{4,5},{5,4},{6,7},{7,6},{8,9},{9,8},{10,11... | collective-permute-start | bytes 442376 | tf_op jit(solution)/shard_map/ppermute | solution.py:395
  50.8 21.2 %collective-permute-start.11 = (bf16[64,1920]{1,0:T(8,128)(2,1)S(1)}, bf16[64,1920]{1,0:T(8,128)(2,1)S(1)}, u32[]{:S(2)}, u32[]{:S(2)}) collective-permute-start(bf16[64,1920]{1,0:T(8,128)(2,1)S(1)} %get-tuple-element.170), channel_id=1, source_target_pairs={{0,16},{4,20},{8,24},{12,28},{16,0},{20,4},{24,8},{28,12},{1,17},{... | collective-permute-start | bytes 737288 | tf_op jit(solution)/shard_map/ppermute | solution.py:390
  51.3 20.7 %collective-permute-start.10 = (bf16[80,1920]{1,0:T(8,128)(2,1)S(1)}, bf16[80,1920]{1,0:T(8,128)(2,1)S(1)}, u32[]{:S(2)}, u32[]{:S(2)}) collective-permute-start(bf16[80,1920]{1,0:T(8,128)(2,1)S(1)} %get-tuple-element.169), channel_id=1, source_target_pairs={{0,8},{4,12},{8,0},{12,4},{16,24},{20,28},{24,16},{28,20},{1,9},{5... | collective-permute-start | bytes 921608 | tf_op jit(solution)/shard_map/ppermute | solution.py:390
  63.7 21.6 %all-to-all-start.1 = ((bf16[4,160,192]{2,1,0:T(8,128)(2,1)}), bf16[4,160,192]{2,1,0:T(8,128)(2,1)}, u32[]{:S(2)}, u32[]{:S(2)}) async-start(bf16[4,160,192]{2,1,0:T(8,128)(2,1)} %bitcast.6), calls=%async_computation.1 | async-start | bytes 655360 | tf_op jit(solution)/shard_map/all_to_all | solution.py:401
  68.6 13.2 %collective-permute-start.17 = (bf16[288,768]{1,0:T(8,128)(2,1)S(1)}, bf16[288,768]{1,0:T(8,128)(2,1)S(1)}, u32[]{:S(2)}, u32[]{:S(2)}) collective-permute-start(bf16[288,768]{1,0:T(8,128)(2,1)S(1)} %get-tuple-element.179.refs_1_), channel_id=1, source_target_pairs={{0,16},{4,20},{8,24},{12,28},{16,0},{20,4},{24,8},{28,12},{1,17},{... | collective-permute-start | bytes 1327112 | tf_op jit(solution)/shard_map/ppermute | solution.py:390
  70.5 11.5 %collective-permute-start.16 = (bf16[288,768]{1,0:T(8,128)(2,1)S(1)}, bf16[288,768]{1,0:T(8,128)(2,1)S(1)}, u32[]{:S(2)}, u32[]{:S(2)}) collective-permute-start(bf16[288,768]{1,0:T(8,128)(2,1)S(1)} %get-tuple-element.179.refs_1_), channel_id=1, source_target_pairs={{0,8},{4,12},{8,0},{12,4},{16,24},{20,28},{24,16},{28,20},{1,9},{5... | collective-permute-start | bytes 1327112 | tf_op jit(solution)/shard_map/ppermute | solution.py:390
  105.5 16.4 %collective-permute-start.20 = (bf16[384,768]{1,0:T(8,128)(2,1)}, bf16[384,768]{1,0:T(8,128)(2,1)}, u32[]{:S(2)}, u32[]{:S(2)}) collective-permute-start(bf16[384,768]{1,0:T(8,128)(2,1)} %get-tuple-element.213), channel_id=1, source_target_pairs={{0,8},{4,12},{8,0},{12,4},{16,24},{20,28},{24,16},{28,20},{1,9},{5... | collective-permute-start | bytes 1769480 | tf_op jit(solution)/shard_map/ppermute | solution.py:390
  106.8 15.4 %collective-permute-start.21 = (bf16[384,768]{1,0:T(8,128)(2,1)}, bf16[384,768]{1,0:T(8,128)(2,1)}, u32[]{:S(2)}, u32[]{:S(2)}) collective-permute-start(bf16[384,768]{1,0:T(8,128)(2,1)} %get-tuple-element.214), channel_id=1, source_target_pairs={{0,16},{4,20},{8,24},{12,28},{16,0},{20,4},{24,8},{28,12},{1,17},{... | collective-permute-start | bytes 1769480 | tf_op jit(solution)/shard_map/ppermute | solution.py:390
  116.5 20.6 %all-to-all-start.2 = ((bf16[4,144,192]{2,1,0:T(8,128)(2,1)}), bf16[4,144,192]{2,1,0:T(8,128)(2,1)S(1)}, u32[]{:S(2)}, u32[]{:S(2)}) async-start(bf16[4,144,192]{2,1,0:T(8,128)(2,1)} %bitcast.11), calls=%async_computation.2 | async-start | bytes 589824 | tf_op jit(solution)/shard_map/all_to_all | solution.py:401
  123.7 11.1 %collective-permute-start.22 = (bf16[192,768]{1,0:T(8,128)(2,1)S(1)}, bf16[192,768]{1,0:T(8,128)(2,1)S(1)}, u32[]{:S(2)}, u32[]{:S(2)}) collective-permute-start(bf16[192,768]{1,0:T(8,128)(2,1)S(1)} %get-tuple-element.220), channel_id=1, source_target_pairs={{0,8},{4,12},{8,0},{12,4},{16,24},{20,28},{24,16},{28,20},{1,9},{5... | collective-permute-start | bytes 884744 | tf_op jit(solution)/shard_map/ppermute | solution.py:390
  131.2 33.5 %collective-permute-start.27 = (bf16[192,1920]{1,0:T(8,128)(2,1)}, bf16[192,1920]{1,0:T(8,128)(2,1)S(1)}, u32[]{:S(2)}, u32[]{:S(2)}) collective-permute-start(bf16[192,1920]{1,0:T(8,128)(2,1)} %get-tuple-element.241), channel_id=1, source_target_pairs={{0,8},{4,12},{8,0},{12,4},{16,24},{20,28},{24,16},{28,20},{1,9},{5... | collective-permute-start | bytes 2211848 | tf_op jit(solution)/shard_map/ppermute | solution.py:390
  131.9 34.2 %collective-permute-start.28 = (bf16[192,1920]{1,0:T(8,128)(2,1)}, bf16[192,1920]{1,0:T(8,128)(2,1)}, u32[]{:S(2)}, u32[]{:S(2)}) collective-permute-start(bf16[192,1920]{1,0:T(8,128)(2,1)} %get-tuple-element.242), channel_id=1, source_target_pairs={{0,16},{4,20},{8,24},{12,28},{16,0},{20,4},{24,8},{28,12},{1,17},{... | collective-permute-start | bytes 2211848 | tf_op jit(solution)/shard_map/ppermute | solution.py:390
  132.4 33.7 %collective-permute-start.29 = (bf16[192,1920]{1,0:T(8,128)(2,1)}, bf16[192,1920]{1,0:T(8,128)(2,1)}, u32[]{:S(2)}, u32[]{:S(2)}) collective-permute-start(bf16[192,1920]{1,0:T(8,128)(2,1)} %get-tuple-element.243), channel_id=1, source_target_pairs={{0,24},{4,28},{8,16},{12,20},{16,8},{20,12},{24,0},{28,4},{1,25},{... | collective-permute-start | bytes 2211848 | tf_op jit(solution)/shard_map/ppermute | solution.py:390
  137.1 19.9 %all-to-all-start.3 = ((bf16[4,96,768]{2,1,0:T(8,128)(2,1)}), bf16[4,96,768]{2,1,0:T(8,128)(2,1)S(1)}, u32[]{:S(2)}, u32[]{:S(2)}) async-start(bf16[4,96,768]{2,1,0:T(8,128)(2,1)} %bitcast.13), calls=%async_computation.3 | async-start | bytes 1179648 | tf_op jit(solution)/shard_map/all_to_all | solution.py:405
  154.1 20.4 %collective-permute-start.26 = (bf16[576,768]{1,0:T(8,128)(2,1)S(1)}, bf16[576,768]{1,0:T(8,128)(2,1)S(1)}, u32[]{:S(2)}, u32[]{:S(2)}) collective-permute-start(bf16[576,768]{1,0:T(8,128)(2,1)S(1)} %get-tuple-element.239), channel_id=1, source_target_pairs={{0,4},{4,0},{8,12},{12,8},{16,20},{20,16},{24,28},{28,24},{1,5},{5... | collective-permute-start | bytes 2654216 | tf_op jit(solution)/shard_map/ppermute | solution.py:380
  159.9 20.0 %all-to-all-start.4 = ((bf16[4,96,640]{2,1,0:T(8,128)(2,1)}), bf16[4,96,640]{2,1,0:T(8,128)(2,1)S(1)}, u32[]{:S(2)}, u32[]{:S(2)}) async-start(bf16[4,96,640]{2,1,0:T(8,128)(2,1)} %bitcast.15), calls=%async_computation.4 | async-start | bytes 983040 | tf_op jit(solution)/shard_map/all_to_all | solution.py:405
  170.1 15.3 %collective-permute-start.31 = (bf16[48,1920]{1,0:T(8,128)(2,1)}, bf16[48,1920]{1,0:T(8,128)(2,1)}, u32[]{:S(2)}, u32[]{:S(2)}) collective-permute-start(bf16[48,1920]{1,0:T(8,128)(2,1)} %get-tuple-element.249), channel_id=1, source_target_pairs={{0,1},{1,0},{2,3},{3,2},{4,5},{5,4},{6,7},{7,6},{8,9},{9,8},{10,11... | collective-permute-start | bytes 552968 | tf_op jit(solution)/shard_map/ppermute | solution.py:395
  170.8 21.0 %collective-permute-start.32 = (bf16[48,1920]{1,0:T(8,128)(2,1)}, bf16[48,1920]{1,0:T(8,128)(2,1)}, u32[]{:S(2)}, u32[]{:S(2)}) collective-permute-start(bf16[48,1920]{1,0:T(8,128)(2,1)} %get-tuple-element.250), channel_id=1, source_target_pairs={{0,2},{1,3},{2,0},{3,1},{4,6},{5,7},{6,4},{7,5},{8,10},{9,11},{10,... | collective-permute-start | bytes 552968 | tf_op jit(solution)/shard_map/ppermute | solution.py:395
  173.2 18.6 %collective-permute-start.33 = (bf16[48,1920]{1,0:T(8,128)(2,1)}, bf16[48,1920]{1,0:T(8,128)(2,1)}, u32[]{:S(2)}, u32[]{:S(2)}) collective-permute-start(bf16[48,1920]{1,0:T(8,128)(2,1)} %get-tuple-element.251), channel_id=1, source_target_pairs={{0,3},{1,2},{2,1},{3,0},{4,7},{5,6},{6,5},{7,4},{8,11},{9,10},{10,... | collective-permute-start | bytes 552968 | tf_op jit(solution)/shard_map/ppermute | solution.py:395
  175.9 19.3 %collective-permute-start.37 = (bf16[144,768]{1,0:T(8,128)(2,1)S(1)}, bf16[144,768]{1,0:T(8,128)(2,1)S(1)}, u32[]{:S(2)}, u32[]{:S(2)}) collective-permute-start(bf16[144,768]{1,0:T(8,128)(2,1)S(1)} %get-tuple-element.255), channel_id=1, source_target_pairs={{0,24},{4,28},{8,16},{12,20},{16,8},{20,12},{24,0},{28,4},{1,25},{... | collective-permute-start | bytes 663560 | tf_op jit(solution)/shard_map/ppermute | solution.py:390
  177.4 19.2 %collective-permute-start.38 = (bf16[144,768]{1,0:T(8,128)(2,1)S(1)}, bf16[144,768]{1,0:T(8,128)(2,1)S(1)}, u32[]{:S(2)}, u32[]{:S(2)}) collective-permute-start(bf16[144,768]{1,0:T(8,128)(2,1)S(1)} %get-tuple-element.256), channel_id=1, source_target_pairs={{0,16},{4,20},{8,24},{12,28},{16,0},{20,4},{24,8},{28,12},{1,17},{... | collective-permute-start | bytes 663560 | tf_op jit(solution)/shard_map/ppermute | solution.py:390
  181.7 20.1 %all-to-all-start.5 = ((bf16[4,192,768]{2,1,0:T(8,128)(2,1)}), bf16[4,192,768]{2,1,0:T(8,128)(2,1)S(1)}, u32[]{:S(2)}, u32[]{:S(2)}) async-start(bf16[4,192,768]{2,1,0:T(8,128)(2,1)} %bitcast.17), calls=%async_computation.5 | async-start | bytes 2359296 | tf_op jit(solution)/shard_map/all_to_all | solution.py:401
  185.4 21.3 %collective-permute-start.39 = (bf16[144,768]{1,0:T(8,128)(2,1)S(1)}, bf16[144,768]{1,0:T(8,128)(2,1)}, u32[]{:S(2)}, u32[]{:S(2)}) collective-permute-start(bf16[144,768]{1,0:T(8,128)(2,1)S(1)} %get-tuple-element.257), channel_id=1, source_target_pairs={{0,8},{4,12},{8,0},{12,4},{16,24},{20,28},{24,16},{28,20},{1,9},{5... | collective-permute-start | bytes 663560 | tf_op jit(solution)/shard_map/ppermute | solution.py:390
  193.1 16.9 %collective-permute-start.36 = (bf16[48,1920]{1,0:T(8,128)(2,1)S(1)}, bf16[48,1920]{1,0:T(8,128)(2,1)S(1)}, u32[]{:S(2)}, u32[]{:S(2)}) collective-permute-start(bf16[48,1920]{1,0:T(8,128)(2,1)S(1)} %get-tuple-element.253.refs_0_), channel_id=1, source_target_pairs={{0,24},{4,28},{8,16},{12,20},{16,8},{20,12},{24,0},{28,4},{1,25},{... | collective-permute-start | bytes 552968 | tf_op jit(solution)/shard_map/ppermute | solution.py:390
  194.3 15.7 %collective-permute-start.35 = (bf16[48,1920]{1,0:T(8,128)(2,1)S(1)}, bf16[48,1920]{1,0:T(8,128)(2,1)S(1)}, u32[]{:S(2)}, u32[]{:S(2)}) collective-permute-start(bf16[48,1920]{1,0:T(8,128)(2,1)S(1)} %get-tuple-element.253.refs_0_), channel_id=1, source_target_pairs={{0,16},{4,20},{8,24},{12,28},{16,0},{20,4},{24,8},{28,12},{1,17},{... | collective-permute-start | bytes 552968 | tf_op jit(solution)/shard_map/ppermute | solution.py:390
  195.2 15.9 %collective-permute-start.34 = (bf16[48,1920]{1,0:T(8,128)(2,1)S(1)}, bf16[48,1920]{1,0:T(8,128)(2,1)S(1)}, u32[]{:S(2)}, u32[]{:S(2)}) collective-permute-start(bf16[48,1920]{1,0:T(8,128)(2,1)S(1)} %get-tuple-element.253.refs_0_), channel_id=1, source_target_pairs={{0,8},{4,12},{8,0},{12,4},{16,24},{20,28},{24,16},{28,20},{1,9},{5... | collective-permute-start | bytes 552968 | tf_op jit(solution)/shard_map/ppermute | solution.py:390
  (58 other events, 336.2 us)
